TPU v7x, 512 devices: a whole 4x4x16 slice. The times are simulated.
512 devices in a mesh: vocab: 64 (over x, z), rows: 8 (over y, core).
Axes of the slice: x: 4, y: 4, z: 16, core: 2. Of those that a mesh axis runs over, the one named last changes fastest.
Arguments:
- hidden: bfloat16 [4096, 4096], P('rows', 'vocab'), may hold values from -48 to 48
- head_weight: bfloat16 [4096, 65536], P('rows', 'vocab'), may hold values from -1 to 1
- in_proj: bfloat16 [4096, 64], replicated, may hold values from -0.09375 to 0.09375
- out_proj: bfloat16 [65536, 64], P('vocab'), may hold values from -6 to 6
- targets: int32 [4096], P('rows'), may hold values from 0 to 65535
- lengths: int32 [32], replicated, may hold values from 1 to 128, as said below
- grad_store: bfloat16 [131072, 4096], P(('vocab', 'rows')), may hold values from -0.09375 to 0.09375
Outputs:
- scores: float32 [32, 131072], P(None, ('vocab', 'rows'))
Inputs may be any that keep to these rules, and one draw needn't show every extreme that they name: `lengths`: at least one sequence has exactly 128 valid rows.
All inputs are finite; a program needn't handle non-finite values.
Results may differ from a plain program's by a relative error of at most 0.0029.
Values may be sent and summed in bfloat16 or wider, within the bound.
No kernel may reach another device: no remote copies, remote signals or barrier semaphores. Data moves between devices by JAX's collectives and lax.ppermute only.
A program may use at most 64 MiB of HBM per device.

v0:
```python
import jax
import jax.numpy as jnp
from jax import lax
from jax.sharding import PartitionSpec as P

TILE = 128


damping_ratio = 0.1
tiny_value = 1e-06


def whiten(seq_grads, cov_out, cov_in):
    proj_width = cov_out.shape[0]
    seq_count = seq_grads.shape[0]
    identity = jnp.eye(proj_width, dtype=jnp.float32)
    damp_out = damping_ratio * jnp.trace(cov_out) / proj_width + tiny_value
    damp_in = damping_ratio * jnp.trace(cov_in) / proj_width + tiny_value
    lower_out = jnp.linalg.cholesky(cov_out + damp_out * identity)
    lower_in = jnp.linalg.cholesky(cov_in + damp_in * identity)
    stacked = jnp.transpose(seq_grads, (1, 0, 2)).reshape(proj_width, seq_count * proj_width)
    left_half = lax.linalg.triangular_solve(lower_out, stacked, left_side=True, lower=True)
    left_full = lax.linalg.triangular_solve(
        lower_out, left_half, left_side=True, lower=True, transpose_a=True
    )
    rows_form = jnp.transpose(
        left_full.reshape(proj_width, seq_count, proj_width), (1, 0, 2)
    ).reshape(seq_count * proj_width, proj_width)
    right_half = lax.linalg.triangular_solve(
        lower_in, rows_form, left_side=False, lower=True, transpose_a=True
    )
    right_full = lax.linalg.triangular_solve(lower_in, right_half, left_side=False, lower=True)
    return right_full.reshape(seq_count, proj_width * proj_width)


def per_device(hidden, head_weight, in_proj, out_proj, targets, lengths, grad_store):
    token_count = hidden.shape[0]
    vocab_cols = head_weight.shape[1]
    proj_width = in_proj.shape[1]
    tile_count = token_count // TILE
    features = lax.all_gather(hidden, "vocab", axis=1, tiled=True)
    out_table = out_proj.astype(jnp.float32)
    first_column = lax.axis_index("vocab") * vocab_cols
    column_ids = lax.broadcasted_iota(jnp.int32, (token_count, vocab_cols), 1) + first_column
    onehot = (column_ids == targets[:, None]).astype(jnp.float32)
    logits = jnp.dot(
        features,
        lax.all_gather(head_weight, "rows", axis=0, tiled=True),
        preferred_element_type=jnp.float32,
    )
    row_max = lax.pmax(jnp.max(logits, axis=1), "vocab")
    exponent = jnp.exp(logits - row_max[:, None])
    row_sum = lax.psum(jnp.sum(exponent, axis=1), "vocab")
    gradient = exponent / row_sum[:, None] - onehot
    out_grad = lax.psum(jnp.dot(gradient, out_table, precision=lax.Precision.HIGHEST), "vocab")
    input_proj = jnp.dot(features, in_proj, preferred_element_type=jnp.float32)
    own_lengths = lax.dynamic_slice_in_dim(lengths, lax.axis_index("rows") * tile_count, tile_count)
    position = lax.broadcasted_iota(jnp.int32, (tile_count, TILE), 1)
    is_valid = (position < own_lengths[:, None]).astype(jnp.float32)[:, :, None]
    out_tiles = out_grad.reshape(tile_count, TILE, proj_width) * is_valid
    in_tiles = input_proj.reshape(tile_count, TILE, proj_width) * is_valid
    flat_out = out_tiles.reshape(token_count, proj_width)
    flat_in = in_tiles.reshape(token_count, proj_width)
    local_out = jnp.dot(flat_out.T, flat_out, precision=lax.Precision.HIGHEST)
    local_in = jnp.dot(flat_in.T, flat_in, precision=lax.Precision.HIGHEST)
    cov_out, cov_in = lax.psum((local_out, local_in), "rows")
    row_total = jnp.sum(lengths).astype(jnp.float32)
    seq_grads = jnp.einsum("stk,stj->skj", out_tiles, in_tiles, precision=lax.Precision.HIGHEST)
    seq_grads = seq_grads / jnp.sqrt(own_lengths.astype(jnp.float32))[:, None, None]
    whitened = whiten(seq_grads, cov_out / row_total, cov_in / row_total).astype(jnp.bfloat16)
    return jnp.dot(
        lax.all_gather(whitened, "rows", axis=0, tiled=True),
        grad_store.T,
        preferred_element_type=jnp.float32,
    )


def solution(mesh):
    return jax.shard_map(
        per_device,
        mesh=mesh,
        in_specs=(
            P("rows", "vocab"),
            P("rows", "vocab"),
            P(),
            P("vocab", None),
            P("rows"),
            P(),
            P(("vocab", "rows"), None),
        ),
        out_specs=P(None, ("vocab", "rows")),
        check_vma=False,
    )
```

profile of v0, /device:TPU:1, one launch (start us, length us, event | category | flops | bytes accessed | tf_op | source)
XLA Modules:
  0.0 845.4 jit_solution(4309254859739480681)
XLA Ops:
  6.5 0.0 copy-start
  6.5 0.7 all-gather.4.cloned.1.call-update
  7.3 0.0 all-gather.6.cloned.1.call-start
  7.3 0.7 all-gather.6.cloned.1.call-update
  8.0 0.0 all-reduce.3.cloned.1.call-start
  8.1 1.3 reduce_sum.35
  10.0 0.7 convert_sqrt_fusion
  10.8 0.1 fusion.40
  10.8 141.4 %all-gather.4.cloned.1.call-done = bf16[512,4096]{0,1:T(8,128)(2,1)} async-done(((bf16[512,64]{0,1:T(8,128)(2,1)}), bf16[512,4096]{0,1:T(8,128)(2,1)}) %all-gather.4.cloned.1.call-update) | async-done | bytes 4194320 | tf_op jit(solution)/shard_map/all_gather | solution.py:41
  152.3 3.2 fusion.43
  155.4 61.0 %all-gather.6.cloned.1.call-done = bf16[4096,1024]{1,0:T(8,128)(2,1)} async-done(((bf16[512,1024]{1,0:T(8,128)(2,1)}), bf16[4096,1024]{1,0:T(8,128)(2,1)}) %all-gather.6.cloned.1.call-update) | async-done | bytes 8388624 | tf_op jit(solution)/shard_map/all_gather | solution.py:48
  216.4 10.5 %fusion.41 = (f32[512]{0:T(512)S(1)}, f32[512,1024]{1,0:T(8,128)}) fusion(bf16[512,4096]{0,1:T(8,128)(2,1)} %all-gather.4.cloned.1.call-done, bf16[4096,1024]{1,0:T(8,128)(2,1)} %all-gather.6.cloned.1.call-done), kind=kOutput, calls=%fused_computation.61 | convolution fusion | flops 4295491072 | bytes 14682112 | tf_op jit(solution)/shard_map/dot_general | solution.py:46
  227.0 116.9 %pmax.7 = f32[512]{0:T(512)S(1)} all-reduce(f32[512]{0:T(512)S(1)} %get-tuple-element.12), channel_id=1, replica_groups=mesh['vocab'=64,'rows'=8] {'vocab'}, use_global_device_ids=true, to_apply=%region_1.0 | all-reduce | flops 512 | bytes 4096 | tf_op jit(solution)/shard_map/pmax | solution.py:51
  343.8 2.0 fusion.5
  345.9 110.8 %psum.28 = f32[512]{0:T(512)S(1)} all-reduce(f32[512]{0:T(512)S(1)} %fusion.5), channel_id=1, replica_groups=mesh['vocab'=64,'rows'=8] {'vocab'}, use_global_device_ids=true, to_apply=%region_3.0 | all-reduce | flops 512 | bytes 4096 | tf_op jit(solution)/shard_map/psum | solution.py:53
  456.7 0.0 copy-done.2
  456.7 4.0 fusion
  460.7 0.0 all-reduce.3.cloned.1.call-update
  460.7 0.3 fusion.13
  461.0 297.5 %all-reduce.3.cloned.1.call-done = f32[512,64]{0,1:T(8,128)} async-done(((f32[512,64]{0,1:T(8,128)}), f32[512,64]{0,1:T(8,128)}) %all-reduce.3.cloned.1.call-update) | async-done | bytes 131088 | tf_op jit(solution)/shard_map/psum | solution.py:55
  758.5 1.2 fusion.15
  759.8 32.3 %all-reduce = (f32[64,64]{1,0:T(8,128)S(1)}, f32[64,64]{1,0:T(8,128)S(1)}) all-reduce(f32[64,64]{1,0:T(8,128)S(1)} %fusion.15, f32[64,64]{1,0:T(8,128)S(1)} %fusion.13), channel_id=1, replica_groups=mesh['vocab'=64,'rows'=8] {'rows'}, use_global_device_ids=true, to_apply=%region_5.0 | all-reduce | flops 8192 | bytes 65536 | tf_op jit(solution)/shard_map/psum | solution.py:66
  792.1 0.6 fusion.35
  793.3 0.1 copy.29
  793.4 0.1 copy.30
  793.5 5.9 cholesky.55
  799.4 0.6 compare_reduce_fusion
  800.0 0.6 fusion.21
  800.6 4.9 custom-call.13
  806.2 0.1 copy.22
  806.3 0.1 copy.23
  806.3 5.9 cholesky.44
  812.2 0.6 compare_reduce_fusion.1
  812.9 0.7 fusion.20
  813.5 4.9 custom-call.12
  818.4 1.3 fusion.6
  819.7 0.1 copy.26
  819.8 0.1 reshape.76
  819.9 0.1 copy.33
  820.0 0.3 fusion.26
  820.3 0.5 fusion.28
  820.8 0.3 fusion.23
  821.1 0.2 convolution_convert_fusion
  821.3 0.1 copy.31
  821.4 0.1 reshape.79
  821.5 15.9 %all-gather = bf16[8,4,4096]{2,1,0:T(4,128)(2,1)S(1)} all-gather(bf16[1,4,4096]{2,1,0:T(4,128)(2,1)S(1)} %reshape.79), channel_id=1, replica_groups=mesh['vocab'=64,'rows'=8] {'rows'}, dimensions={0}, use_global_device_ids=true | all-gather | bytes 294912 | tf_op jit(solution)/shard_map/all_gather | solution.py:72
  837.4 0.1 reshape.80
  837.5 1.4 fusion.42
  (12 shorter events, 0.1 us)
Async XLA Ops:
  6.5 830.9 %copy-start = (bf16[256,4096]{1,0:T(8,128)(2,1)S(1)}, bf16[256,4096]{1,0:T(8,128)(2,1)}, u32[]{:S(2)}) copy-start(bf16[256,4096]{1,0:T(8,128)(2,1)} %param.14) | copy-start | bytes 6291460
  6.5 145.7 %all-gather.4.cloned.1.call-start = ((), (), s32[]{:S(2)}) async-start(), calls=%async_computation | async-start | bytes 4259840 | tf_op jit(solution)/shard_map/all_gather | solution.py:41
  7.3 209.2 %all-gather.6.cloned.1.call-start = ((), (), s32[]{:S(2)}) async-start(), calls=%async_computation.1 | async-start | bytes 9437184 | tf_op jit(solution)/shard_map/all_gather | solution.py:48
  8.0 750.5 %all-reduce.3.cloned.1.call-start = ((), (), s32[]{:S(2)}) async-start(), calls=%async_computation.2 | async-start | bytes 262144 | tf_op jit(solution)/shard_map/psum | solution.py:55
  227.0 229.7 %copy-start.1 = (bf16[1024,64]{0,1:T(8,128)(2,1)S(1)}, bf16[1024,64]{0,1:T(8,128)(2,1)}, u32[]{:S(2)}) copy-start(bf16[1024,64]{0,1:T(8,128)(2,1)} %param.11) | copy-start | bytes 393220
  227.0 229.7 %copy-start.2 = (s32[512]{0:T(512)S(1)}, s32[512]{0:T(512)}, u32[]{:S(2)}) copy-start(s32[512]{0:T(512)} %param.12) | copy-start | bytes 6148
Sparse Core Ops, SparseCore 0:
  10.3 141.9 all-gather.3
  154.4 61.9 all-gather.5
  460.8 297.6 all-reduce.2
where the time goes:
time: 846 us; the launch traced here: 845 us
  waiting for transfers between devices  501 us (59%)
  blocking collectives  276 us (33%)
  other arithmetic  28.9 us (3%)
  matrix products  23.1 us (3%)
  between operations  15.2 us (2%)
    psum x1, waiting for transfers between devices, per_device(): lax.psum(jnp.dot(gradient, out_table, precision=lax.Precision.HIGHEST), '...  298 us
    all_gather x1, waiting for transfers between devices, per_device(): features = lax.all_gather(hidden, 'vocab', axis=1, tiled=True)  141 us
    pmax x1, blocking collectives, per_device(): row_max = lax.pmax(jnp.max(logits, axis=1), 'vocab')  117 us
    psum x1, blocking collectives, per_device(): row_sum = lax.psum(jnp.sum(exponent, axis=1), 'vocab')  111 us
    all_gather x1, waiting for transfers between devices, per_device(): lax.all_gather(head_weight, 'rows', axis=0, tiled=True)  61 us
    psum x1, blocking collectives, per_device(): cov_out, cov_in = lax.psum((local_out, local_in), 'rows')  32.3 us
  transfers between devices with their start and end apart: 3, of which 3 were waited for; matrix products, arithmetic and copies ran while one was open for 1% of the time, Pallas kernels for 0%

commit v1 on v0

v1 whole, which is shorter than its diff:
```python
import functools
import jax
import jax.numpy as jnp
from jax import lax
from jax.experimental import pallas as pl
from jax.experimental.pallas import tpu as pltpu
from jax.sharding import Mesh, PartitionSpec as P

TILE = 128
NX, NZ, NY, NC = 4, 16, 4, 2

damping_ratio = 0.1
tiny_value = 1e-06
HI = lax.Precision.HIGHEST
F32 = jnp.float32
BF16 = jnp.bfloat16


def shift(value, axis, step, size):
    return lax.ppermute(value, axis, [(i, (i + step) % size) for i in range(size)])


def spread(value, axis, size):
    copies = jnp.broadcast_to(value[None], (size,) + value.shape)
    return lax.all_to_all(copies, axis, 0, 0, tiled=True)


def exchange(value, axis):
    return lax.all_to_all(value, axis, 0, 0, tiled=True)


def logits_kernel(offsets, place_ref, *refs):
    count = len(offsets)
    chunks = refs[:count]
    head, in_proj, out_proj, targets, packed, proj = refs[count : count + 6]
    feat_buf, head_buf, proj_buf, logit_buf, sems = refs[count + 6 :]
    x, z = place_ref[0], place_ref[1]
    width = chunks[0].shape[1]
    group = width // NX
    stride = head.shape[0] // NX
    copies = []
    for j, offset in enumerate(offsets):
        copy = pltpu.make_async_copy(chunks[j], feat_buf.at[:, pl.ds(j * width, width)], sems.at[j])
        copy.start()
        copies.append(copy)
        other = (z + offset + NZ) % NZ
        for i in range(NX):
            first = pl.multiple_of(i * stride + other * group, group)
            copy = pltpu.make_async_copy(
                head.at[pl.ds(first, group), :],
                head_buf.at[pl.ds(j * width + i * group, group), :],
                sems.at[count + j * NX + i],
            )
            copy.start()
            copies.append(copy)
            proj_buf[pl.ds(j * width + i * group, group), :] = in_proj[pl.ds(first, group), :]
    for copy in copies:
        copy.wait()
    cols = head.shape[1]
    block = 256

    def column_block(n, carry):
        first = pl.multiple_of(n * block, block)
        logit_buf[:, pl.ds(first, block)] = jnp.dot(
            feat_buf[...], head_buf[:, pl.ds(first, block)], preferred_element_type=F32
        )
        return carry

    lax.fori_loop(0, cols // block, column_block, 0)
    own = pl.multiple_of(x * TILE, TILE)
    proj[...] = jnp.dot(feat_buf[pl.ds(own, TILE), :], proj_buf[...], preferred_element_type=F32)
    table = out_proj[...]
    vocab_first = (x * NZ + z) * cols

    def row_block(i, carry):
        first = pl.multiple_of(i * TILE, TILE)
        logits = logit_buf[pl.ds(first, TILE), :]
        peak = jnp.max(logits, axis=1, keepdims=True)
        weight = jnp.exp(logits - peak)
        total = jnp.sum(weight, axis=1, keepdims=True)
        part1 = weight.astype(BF16)
        rest = weight - part1.astype(F32)
        part2 = rest.astype(BF16)
        part3 = (rest - part2.astype(F32)).astype(BF16)
        mixed = jnp.dot(part1, table, preferred_element_type=F32)
        mixed += jnp.dot(part2, table, preferred_element_type=F32)
        mixed += jnp.dot(part3, table, preferred_element_type=F32)
        column = lax.broadcasted_iota(jnp.int32, logits.shape, 1) + vocab_first
        hit = jnp.where(column == targets[pl.ds(first, TILE), :], 1.0, 0.0).astype(BF16)
        picked = jnp.dot(hit, table, preferred_element_type=F32)
        packed[i, 0:TILE, :] = jnp.concatenate([mixed, picked], axis=1)
        half = mixed.shape
        packed[i, TILE : 2 * TILE, :] = jnp.concatenate(
            [jnp.broadcast_to(peak, half), jnp.broadcast_to(total, half)], axis=1
        )
        return carry

    lax.fori_loop(0, NX, row_block, 0)


def merge(parts, size):
    width = 64
    peaks = [stat[:, 0:1] for _, stat in parts]
    peak = functools.reduce(jnp.maximum, peaks)
    scales = [jnp.exp(p - peak) for p in peaks]
    total = sum(s * stat[:, width : width + 1] for s, (_, stat) in zip(scales, parts))
    mixed = sum(s * data[:, :width] for s, (data, _) in zip(scales, parts))
    picked = sum(data[:, width:] for data, _ in parts)
    return mixed, picked, peak, total


def merge_x_kernel(packed, out):
    parts = [(packed[i, 0:TILE, :], packed[i, TILE : 2 * TILE, :]) for i in range(NX)]
    mixed, picked, peak, total = merge(parts, NX)
    data = jnp.concatenate([mixed, picked], axis=1)
    stat = jnp.concatenate([jnp.broadcast_to(peak, mixed.shape), jnp.broadcast_to(total, mixed.shape)], axis=1)
    rows = TILE // NZ
    out[:, 0:rows, :] = data.reshape(NZ, rows, TILE)
    out[:, rows : 2 * rows, :] = stat.reshape(NZ, rows, TILE)


def merge_z_kernel(packed, out):
    rows = TILE // NZ
    parts = [(packed[i, 0:rows, :], packed[i, rows : 2 * rows, :]) for i in range(NZ)]
    mixed, picked, peak, total = merge(parts, NZ)
    grad = mixed / total - picked
    out[...] = jnp.concatenate([grad, jnp.zeros_like(grad)], axis=1)


def gram_kernel(place_ref, lengths, grads, proj, out):
    seq = place_ref[2]
    length = lengths[seq]
    both = jnp.concatenate([grads[...].reshape(TILE, TILE)[:, :64], proj[...]], axis=1)
    row = lax.broadcasted_iota(jnp.int32, both.shape, 0)
    both = jnp.where(row < length, both, 0.0)
    gram = lax.dot_general(both, both, (((0,), (0,)), ((), ())), precision=HI, preferred_element_type=F32)
    root = jnp.sqrt(jnp.full((64, 64), length.astype(F32)))
    out[0:64, 0:64] = gram[0:64, 0:64]
    out[0:64, 64:128] = gram[0:64, 64:128] / root
    out[64:96, 0:64] = gram[64:96, 64:128]
    out[64:96, 64:128] = gram[96:128, 64:128]


def inverse_kernel(lengths, grams, out):
    total = functools.reduce(jnp.add, [lengths[s] for s in range(lengths.shape[0])]).astype(F32)
    summed = functools.reduce(jnp.add, [grams[d] for d in range(grams.shape[0])])
    cov_out = summed[0:64, 0:64]
    cov_in = jnp.concatenate([summed[64:96, 0:64], summed[64:96, 64:128]], axis=0)
    work = jnp.concatenate([cov_out, cov_in], axis=1) / total
    row = lax.broadcasted_iota(jnp.int32, work.shape, 0)
    lane = lax.broadcasted_iota(jnp.int32, work.shape, 1)
    left = lane < 64
    inner = jnp.where(left, lane, lane - 64)
    diag = jnp.where(row == inner, work, 0.0)
    trace_out = jnp.sum(jnp.where(left, diag, 0.0))
    trace_in = jnp.sum(jnp.where(left, 0.0, diag))
    damp = jnp.where(left, damping_ratio * trace_out / 64 + tiny_value, damping_ratio * trace_in / 64 + tiny_value)
    work = work + jnp.where(row == inner, damp, 0.0)

    def step(k, work):
        at_row = row == k
        at_lane = inner == k
        pivot_row = jnp.sum(jnp.where(at_row, work, 0.0), axis=0, keepdims=True)
        picked = jnp.where(at_lane, work, 0.0)
        col_out = jnp.sum(jnp.where(left, picked, 0.0), axis=1, keepdims=True)
        col_in = jnp.sum(jnp.where(left, 0.0, picked), axis=1, keepdims=True)
        column = jnp.where(left, col_out, col_in)
        pivot = jnp.sum(jnp.where(at_row, column, 0.0), axis=0, keepdims=True)
        inv = 1.0 / pivot
        scaled = pivot_row * inv
        body = jnp.where(at_lane, 0.0, work) - column * jnp.where(at_lane, inv, scaled)
        top = jnp.where(at_lane, inv, scaled)
        return jnp.where(at_row, top, body)

    out[...] = lax.fori_loop(0, 64, step, work)


def full(shape, dtype=F32):
    return jax.ShapeDtypeStruct(shape, dtype)


VMEM = pl.BlockSpec(memory_space=pltpu.VMEM)
SMEM = pl.BlockSpec(memory_space=pltpu.SMEM)
ANY = pl.BlockSpec(memory_space=pl.ANY)


def per_device(hidden, head_weight, in_proj, out_proj, targets, lengths, grad_store):
    token_count, width = hidden.shape
    x, z = lax.axis_index("x"), lax.axis_index("z")
    rows = lax.axis_index("y") * NC + lax.axis_index("c")
    place = jnp.stack([x, z, rows * NX + x]).astype(jnp.int32)
    head = lax.all_gather(head_weight, ("y", "c"), axis=0, tiled=True)
    mine = spread(hidden.T, "x", NX).reshape(NX * width, token_count).T
    chunks, offsets = [mine], [0]
    up = down = mine
    for k in range(1, NZ // 2):
        up, down = shift(up, "z", 1, NZ), shift(down, "z", -1, NZ)
        chunks += [up, down]
        offsets += [-k, k]
    chunks.append(shift(up, "z", 1, NZ))
    offsets.append(-(NZ // 2))
    count = len(chunks)
    features = head.shape[0]
    packed, proj = pl.pallas_call(
        functools.partial(logits_kernel, offsets),
        out_shape=(full((NX, 2 * TILE, TILE)), full((TILE, 64))),
        in_specs=[SMEM] + [ANY] * count + [ANY, VMEM, VMEM, VMEM],
        out_specs=(VMEM, VMEM),
        scratch_shapes=[
            pltpu.VMEM((token_count, features), BF16),
            pltpu.VMEM((features, head.shape[1]), BF16),
            pltpu.VMEM((features, 64), BF16),
            pltpu.VMEM((token_count, head.shape[1]), F32),
            pltpu.SemaphoreType.DMA((count * (NX + 1),)),
        ],
        name="logits",
    )(place, *chunks, head, in_proj, out_proj, targets[:, None])
    merged = pl.pallas_call(
        merge_x_kernel,
        out_shape=full((NZ, 2 * TILE // NZ, TILE)),
        in_specs=[VMEM],
        out_specs=VMEM,
        name="merge_x",
    )(exchange(packed, "x"))
    grad = pl.pallas_call(
        merge_z_kernel,
        out_shape=full((TILE // NZ, TILE)),
        in_specs=[VMEM],
        out_specs=VMEM,
        name="merge_z",
    )(exchange(merged, "z"))
    gram = pl.pallas_call(
        gram_kernel,
        out_shape=full((96, TILE)),
        in_specs=[SMEM, SMEM, VMEM, VMEM],
        out_specs=VMEM,
        name="gram",
    )(place, lengths, spread(grad, "z", NZ), proj)
    grams = spread(gram, ("x", "y", "c"), NX * NY * NC)
    inverses = pl.pallas_call(
        inverse_kernel,
        out_shape=full((64, TILE)),
        in_specs=[SMEM, VMEM],
        out_specs=VMEM,
        name="inverse",
    )(lengths, grams)
    seq_grads = grams.reshape(NX, NY * NC, 96, TILE)[:, :, :64, 64:]
    seq_grads = jnp.transpose(seq_grads, (1, 0, 2, 3)).reshape(NX * NY * NC, 64, 64)
    half = jnp.einsum("skj,jl->skl", seq_grads, inverses[:, 64:], precision=HI)
    whitened = jnp.einsum("ik,skl->sil", inverses[:, :64], half, precision=HI)
    whitened = whitened.reshape(NX * NY * NC, 64 * 64).astype(BF16)
    return jnp.dot(whitened, grad_store.T, preferred_element_type=F32)


def solution(mesh):
    grid = Mesh(mesh.devices.reshape(NX, NZ, NY, NC), ("x", "z", "y", "c"))
    return jax.shard_map(
        per_device,
        mesh=grid,
        in_specs=(
            P(("y", "c"), ("x", "z")),
            P(("y", "c"), ("x", "z")),
            P(),
            P(("x", "z"), None),
            P(("y", "c")),
            P(),
            P(("x", "z", "y", "c"), None),
        ),
        out_specs=P(None, ("x", "z", "y", "c")),
        check_vma=False,
    )
```

time: 846 us -> 238 us (0.28)
  waiting for transfers between devices: 501 us -> 20.7 us
  blocking collectives: 276 us -> 102 us
  starting transfers between devices: 0.08 us -> 54 us
  Pallas kernels: 0 us -> 30.6 us
  other arithmetic: 28.9 us -> 0.61 us
  matrix products: 23.1 us -> 6.32 us
    psum x1 -> x0, waiting for transfers between devices: 298 us -> none  [per_device(): lax.psum(jnp.dot(gradient, out_table, precision=lax.Precision.HIGHEST), '...]
    all_gather x2 -> x1, waiting for transfers between devices: 202 us -> 0.01 us  [per_device(): head = lax.all_gather(head_weight, ('y', 'c'), axis=0, tiled=True)]
    psum x2 -> x0, blocking collectives: 143 us -> none  [the longest x1 111 us: per_device(): row_sum = lax.psum(jnp.sum(exponent, axis=1), 'vocab')]
    pmax x1 -> x0, blocking collectives: 117 us -> none  [per_device(): row_max = lax.pmax(jnp.max(logits, axis=1), 'vocab')]
    all_to_all x0 -> x5, blocking collectives: none -> 102 us  [the longest x3 70.4 us: spread(): return lax.all_to_all(copies, axis, 0, 0, tiled=True)]
    ppermute x0 -> x15, starting transfers between devices: none -> 54 us  [shift(): lax.ppermute(value, axis, [(i, (i + step) % size) for i in range(size)])]
    pallas_call x0 -> x5, Pallas kernels: none -> 30.6 us  [the longest x1 15.6 us: per_device(): pl.pallas_call(functools.partial(logits_kernel, offsets), out_shape=(full...]
    another operation x10 -> x1, other arithmetic: 24.1 us -> 0.61 us  [per_device(): place = jnp.stack([x, z, rows * NX + x]).astype(jnp.int32)]
  transfers between devices with their start and end apart: 3 -> 16, of which waited for: 3 -> 8; matrix products, arithmetic and copies ran while one was open for 1% -> 2% of each run, Pallas kernels for 0% -> 0%
where the time goes in v1:
time: 238 us; the launch traced here: 236 us
  blocking collectives  102 us (43%)
  starting transfers between devices  54 us (23%)
  Pallas kernels  30.6 us (13%)
  waiting for transfers between devices  20.7 us (9%)
  between operations  13.8 us (6%)
  local copies, waits for them, and re-layouts  8.17 us (3%)
  matrix products  6.32 us (3%)
    all_to_all x3, blocking collectives, spread(): return lax.all_to_all(copies, axis, 0, 0, tiled=True)  70.4 us
    ppermute x15, starting transfers between devices, shift(): lax.ppermute(value, axis, [(i, (i + step) % size) for i in range(size)])  54 us
    all_to_all x2, blocking collectives, exchange(): return lax.all_to_all(value, axis, 0, 0, tiled=True)  31.8 us
    ppermute x15, waiting for transfers between devices, shift(): lax.ppermute(value, axis, [(i, (i + step) % size) for i in range(size)])  20 us
    pallas_call x1, Pallas kernels, per_device(): pl.pallas_call(functools.partial(logits_kernel, offsets), out_shape=(full...  15.6 us
    pallas_call x1, Pallas kernels, per_device(): pl.pallas_call(inverse_kernel, out_shape=full((64, TILE)), in_specs=[SMEM...  9.48 us
  transfers between devices with their start and end apart: 16, of which 8 were waited for; matrix products, arithmetic and copies ran while one was open for 2% of the time, Pallas kernels for 0%

profile of v1, /device:TPU:1, one launch (start us, length us, event | category | flops | bytes accessed | tf_op | source)
XLA Modules:
  0.0 236.5 jit_solution(13347136826104513905)
XLA Ops:
  6.6 0.7 all-gather.2.cloned.1.call-update
  7.3 0.9 broadcast_in_dim.8
  8.2 10.2 %all_to_all.25 = bf16[4,64,512]{2,1,0:T(8,128)(2,1)S(1)} all-to-all(bf16[4,64,512]{2,1,0:T(8,128)(2,1)S(1)} %broadcast_in_dim.8), channel_id=1, replica_groups=mesh['x'=4,'z'=16,'y'=4,'c'=2] {'x'}, dimensions={0} | all-to-all | bytes 524288 | tf_op jit(solution)/shard_map/all_to_all | solution.py:25
  18.5 3.6 %collective-permute-start = (bf16[512,256]{1,0:T(8,128)(2,1)S(1)}, bf16[512,256]{1,0:T(8,128)(2,1)S(1)}, u32[]{:S(2)}, u32[]{:S(2)}) collective-permute-start(bf16[512,256]{1,0:T(8,128)(2,1)S(1)} %bitcast.25), channel_id=1, source_target_pairs={{0,8},{8,16},{16,24},{24,32},{32,40},{40,48},{48,56},{56,64},{64,7... | collective-permute-start | bytes 786440 | tf_op jit(solution)/shard_map/ppermute | solution.py:20
  22.1 9.5 %collective-permute-start.1 = (bf16[512,256]{1,0:T(8,128)(2,1)S(1)}, bf16[512,256]{1,0:T(8,128)(2,1)S(1)}, u32[]{:S(2)}, u32[]{:S(2)}) collective-permute-start(bf16[512,256]{1,0:T(8,128)(2,1)S(1)} %bitcast.26), channel_id=1, source_target_pairs={{0,120},{8,0},{16,8},{24,16},{32,24},{40,32},{48,40},{56,48},{64,5... | collective-permute-start | bytes 786440 | tf_op jit(solution)/shard_map/ppermute | solution.py:20
  31.6 2.7 %collective-permute-done.refs_1_ = bf16[512,256]{1,0:T(8,128)(2,1)S(1)} collective-permute-done((bf16[512,256]{1,0:T(8,128)(2,1)S(1)}, bf16[512,256]{1,0:T(8,128)(2,1)S(1)}, u32[]{:S(2)}, u32[]{:S(2)}) %collective-permute-start) | collective-permute-done | bytes 262176 | tf_op jit(solution)/shard_map/ppermute | solution.py:20
  34.2 1.9 collective-permute-start.2
  36.2 4.6 %collective-permute-start.3 = (bf16[512,256]{1,0:T(8,128)(2,1)S(1)}, bf16[512,256]{1,0:T(8,128)(2,1)S(1)}, u32[]{:S(2)}, u32[]{:S(2)}) collective-permute-start(bf16[512,256]{1,0:T(8,128)(2,1)S(1)} %collective-permute-done.1.refs_2_), channel_id=1, source_target_pairs={{0,120},{8,0},{16,8},{24,16},{32,24},{40,32},{48,40},{56,48},{64,5... | collective-permute-start | bytes 786440 | tf_op jit(solution)/shard_map/ppermute | solution.py:20
  40.7 2.2 collective-permute-done.2.refs_3_
  42.9 1.9 collective-permute-start.4
  44.9 4.6 %collective-permute-start.5 = (bf16[512,256]{1,0:T(8,128)(2,1)S(1)}, bf16[512,256]{1,0:T(8,128)(2,1)S(1)}, u32[]{:S(2)}, u32[]{:S(2)}) collective-permute-start(bf16[512,256]{1,0:T(8,128)(2,1)S(1)} %collective-permute-done.3.refs_4_), channel_id=1, source_target_pairs={{0,120},{8,0},{16,8},{24,16},{32,24},{40,32},{48,40},{56,48},{64,5... | collective-permute-start | bytes 786440 | tf_op jit(solution)/shard_map/ppermute | solution.py:20
  49.5 2.2 collective-permute-done.4.refs_5_
  51.7 1.9 collective-permute-start.6
  53.6 4.6 %collective-permute-start.7 = (bf16[512,256]{1,0:T(8,128)(2,1)S(1)}, bf16[512,256]{1,0:T(8,128)(2,1)S(1)}, u32[]{:S(2)}, u32[]{:S(2)}) collective-permute-start(bf16[512,256]{1,0:T(8,128)(2,1)S(1)} %collective-permute-done.5.refs_6_), channel_id=1, source_target_pairs={{0,120},{8,0},{16,8},{24,16},{32,24},{40,32},{48,40},{56,48},{64,5... | collective-permute-start | bytes 786440 | tf_op jit(solution)/shard_map/ppermute | solution.py:20
  58.2 2.2 collective-permute-done.6.refs_7_
  60.4 1.9 collective-permute-start.8
  62.3 4.6 %collective-permute-start.9 = (bf16[512,256]{1,0:T(8,128)(2,1)S(1)}, bf16[512,256]{1,0:T(8,128)(2,1)S(1)}, u32[]{:S(2)}, u32[]{:S(2)}) collective-permute-start(bf16[512,256]{1,0:T(8,128)(2,1)S(1)} %collective-permute-done.7.refs_8_), channel_id=1, source_target_pairs={{0,120},{8,0},{16,8},{24,16},{32,24},{40,32},{48,40},{56,48},{64,5... | collective-permute-start | bytes 786440 | tf_op jit(solution)/shard_map/ppermute | solution.py:20
  66.9 2.2 collective-permute-done.8.refs_9_
  69.1 1.9 collective-permute-start.10
  71.1 4.6 %collective-permute-start.11 = (bf16[512,256]{1,0:T(8,128)(2,1)S(1)}, bf16[512,256]{1,0:T(8,128)(2,1)}, u32[]{:S(2)}, u32[]{:S(2)}) collective-permute-start(bf16[512,256]{1,0:T(8,128)(2,1)S(1)} %collective-permute-done.9.refs_10_), channel_id=1, source_target_pairs={{0,120},{8,0},{16,8},{24,16},{32,24},{40,32},{48,40},{56,48},{64,5... | collective-permute-start | bytes 786440 | tf_op jit(solution)/shard_map/ppermute | solution.py:20
  75.6 1.8 collective-permute-done.10.refs_11_
  77.4 1.9 collective-permute-start.12
  79.4 4.7 %collective-permute-start.13 = (bf16[512,256]{1,0:T(8,128)(2,1)}, bf16[512,256]{1,0:T(8,128)(2,1)}, u32[]{:S(2)}, u32[]{:S(2)}) collective-permute-start(bf16[512,256]{1,0:T(8,128)(2,1)} %collective-permute-done.11.refs_12_), channel_id=1, source_target_pairs={{0,120},{8,0},{16,8},{24,16},{32,24},{40,32},{48,40},{56,48},{64,5... | collective-permute-start | bytes 786440 | tf_op jit(solution)/shard_map/ppermute | solution.py:20
  84.1 2.4 %collective-permute-done.12.refs_13_ = bf16[512,256]{1,0:T(8,128)(2,1)} collective-permute-done((bf16[512,256]{1,0:T(8,128)(2,1)S(1)}, bf16[512,256]{1,0:T(8,128)(2,1)}, u32[]{:S(2)}, u32[]{:S(2)}) %collective-permute-start.12) | collective-permute-done | bytes 262176 | tf_op jit(solution)/shard_map/ppermute | solution.py:20
  86.4 1.9 collective-permute-start.14
  88.4 0.9 copy.13.refs_18_
  89.3 0.9 copy.14.refs_19_
  90.1 1.4 copy.12.refs_17_
  91.5 0.6 pad_add_fusion.place_ref
  92.1 4.4 %collective-permute-done.14.refs_15_ = bf16[512,256]{1,0:T(8,128)(2,1)} collective-permute-done((bf16[512,256]{1,0:T(8,128)(2,1)}, bf16[512,256]{1,0:T(8,128)(2,1)}, u32[]{:S(2)}, u32[]{:S(2)}) %collective-permute-start.14) | collective-permute-done | bytes 262176 | tf_op jit(solution)/shard_map/ppermute | solution.py:20
  96.5 15.6 %logits.1 = (f32[4,256,128]{2,1,0:T(8,128)}, f32[128,64]{1,0:T(8,128)}) custom-call(s32[3]{0:T(128)} %pad_add_fusion.place_ref, bf16[512,256]{1,0:T(8,128)(2,1)} %bitcast.27, bf16[512,256]{1,0:T(8,128)(2,1)} %copy-done.5, bf16[512,256]{1,0:T(8,128)(2,1)} %copy-done.6, bf16[512,256]{1,0:T(8,128)(2,1)} %copy-done.7, bf16[512,256]{1,0:T(8,128)(2,1)} %copy-done.8, ...), custom_call_target="tpu_custom_call" | custom-call | tf_op jit(solution)/shard_map/logits/pallas_call | solution.py:204
  112.2 11.1 %all_to_all.26.packed = f32[4,256,128]{2,1,0:T(8,128)} all-to-all(f32[4,256,128]{2,1,0:T(8,128)} %get-tuple-element.7), channel_id=1, replica_groups=mesh['x'=4,'z'=16,'y'=4,'c'=2] {'x'}, dimensions={0} | all-to-all | bytes 1048576 | tf_op jit(solution)/shard_map/all_to_all | solution.py:29
  123.3 1.9 merge_x.1
  125.2 20.7 %all_to_all.27.packed = f32[16,16,128]{2,1,0:T(8,128)} all-to-all(f32[16,16,128]{2,1,0:T(8,128)} %merge_x.1), channel_id=1, replica_groups=mesh['x'=4,'z'=16,'y'=4,'c'=2] {'z'}, dimensions={0} | all-to-all | bytes 262144 | tf_op jit(solution)/shard_map/all_to_all | solution.py:29
  145.9 1.7 merge_z.1
  147.6 0.7 broadcast_in_dim.10
  148.3 15.2 %all_to_all.28.grads = f32[16,8,128]{2,1,0:T(8,128)} all-to-all(f32[16,8,128]{2,1,0:T(8,128)S(1)} %broadcast_in_dim.10), channel_id=1, replica_groups=mesh['x'=4,'z'=16,'y'=4,'c'=2] {'z'}, dimensions={0} | all-to-all | bytes 131072 | tf_op jit(solution)/shard_map/all_to_all | solution.py:25
  163.5 1.9 gram.1
  165.4 1.0 broadcast_in_dim.11
  166.4 45.0 %all_to_all.29.grams = f32[32,96,128]{2,1,0:T(8,128)S(1)} all-to-all(f32[32,96,128]{2,1,0:T(8,128)S(1)} %broadcast_in_dim.11), channel_id=1, replica_groups=mesh['x'=4,'z'=16,'y'=4,'c'=2] {'x','y','c'}, dimensions={0} | all-to-all | bytes 3145728 | tf_op jit(solution)/shard_map/all_to_all | solution.py:25
  211.4 1.2 copy-done.1
  212.6 0.3 slice.12
  213.0 9.5 %inverse.1 = f32[64,128]{1,0:T(8,128)} custom-call(s32[32]{0:T(128)} %lengths.3, f32[32,96,128]{2,1,0:T(8,128)} %copy-done.1), custom_call_target="tpu_custom_call" | custom-call | tf_op jit(solution)/shard_map/inverse/pallas_call | solution.py:240
  222.5 4.0 %fusion.1 = f32[32,64,64]{1,2,0:T(8,128)S(1)} fusion(f32[32,64,64]{2,1,0:T(8,128)S(1)} %bitcast.24, f32[64,128]{1,0:T(8,128)} %inverse.1), kind=kOutput, calls=%fused_computation.4 | convolution fusion | flops 100663296 | bytes 1081344 | tf_op jit(solution)/shard_map/skj,jl->skl/dot_general | solution.py:249
  226.5 1.0 fusion
  227.5 0.3 copy.16
  227.8 0.5 convert_element_type.11
  228.3 1.4 fusion.2
  (46 shorter events, 0.4 us)
Async XLA Ops:
  6.5 221.7 %copy-start = (bf16[256,4096]{1,0:T(8,128)(2,1)S(1)}, bf16[256,4096]{1,0:T(8,128)(2,1)}, u32[]{:S(2)}) copy-start(bf16[256,4096]{1,0:T(8,128)(2,1)} %param.13) | copy-start | bytes 6291460
  6.5 81.8 %copy-start.16 = (bf16[1024,64]{0,1:T(8,128)(2,1)S(1)}, bf16[1024,64]{0,1:T(8,128)(2,1)}, u32[]{:S(2)}) copy-start(bf16[1024,64]{0,1:T(8,128)(2,1)} %param.10) | copy-start | bytes 393220
  6.5 82.7 %copy-start.17 = (s32[512]{0:T(512)S(1)}, s32[512]{0:T(512)}, u32[]{:S(2)}) copy-start(s32[512]{0:T(512)} %param.11) | copy-start | bytes 6148
  6.5 83.6 %copy-start.3 = (bf16[4096,64]{0,1:T(8,128)(2,1)S(1)}, bf16[4096,64]{0,1:T(8,128)(2,1)}, u32[]{:S(2)}) copy-start(bf16[4096,64]{0,1:T(8,128)(2,1)} %param.9) | copy-start | bytes 1572868
  6.5 90.0 %all-gather.2.cloned.1.call-start = ((), (), s32[]{:S(2)}) async-start(), calls=%async_computation.5 | async-start | bytes 9437184 | tf_op jit(solution)/shard_map/all_gather | solution.py:192
  18.5 78.1 %copy-start.2 = (bf16[256,512]{0,1:T(8,128)(2,1)}, bf16[256,512]{0,1:T(8,128)(2,1)S(1)}, u32[]{:S(2)}) copy-start(bf16[256,512]{0,1:T(8,128)(2,1)S(1)} %copy.11) | copy-start | bytes 786436
  18.5 15.7 %collective-permute-start = (bf16[512,256]{1,0:T(8,128)(2,1)S(1)}, bf16[512,256]{1,0:T(8,128)(2,1)S(1)}, u32[]{:S(2)}, u32[]{:S(2)}) collective-permute-start(bf16[512,256]{1,0:T(8,128)(2,1)S(1)} %bitcast.25), channel_id=1, source_target_pairs={{0,8},{8,16},{16,24},{24,32},{32,40},{40,48},{48,56},{56,64},{64,7... | collective-permute-start | bytes 786440 | tf_op jit(solution)/shard_map/ppermute | solution.py:20
  22.1 14.1 %collective-permute-start.1 = (bf16[512,256]{1,0:T(8,128)(2,1)S(1)}, bf16[512,256]{1,0:T(8,128)(2,1)S(1)}, u32[]{:S(2)}, u32[]{:S(2)}) collective-permute-start(bf16[512,256]{1,0:T(8,128)(2,1)S(1)} %bitcast.26), channel_id=1, source_target_pairs={{0,120},{8,0},{16,8},{24,16},{32,24},{40,32},{48,40},{56,48},{64,5... | collective-permute-start | bytes 786440 | tf_op jit(solution)/shard_map/ppermute | solution.py:20
  34.2 62.3 %copy-start.5 = (bf16[512,256]{1,0:T(8,128)(2,1)}, bf16[512,256]{1,0:T(8,128)(2,1)S(1)}, u32[]{:S(2)}) copy-start(bf16[512,256]{1,0:T(8,128)(2,1)S(1)} %collective-permute-done.refs_1_) | copy-start | bytes 786436
  34.2 8.7 %collective-permute-start.2 = (bf16[512,256]{1,0:T(8,128)(2,1)S(1)}, bf16[512,256]{1,0:T(8,128)(2,1)S(1)}, u32[]{:S(2)}, u32[]{:S(2)}) collective-permute-start(bf16[512,256]{1,0:T(8,128)(2,1)S(1)} %collective-permute-done.refs_1_), channel_id=1, source_target_pairs={{0,8},{8,16},{16,24},{24,32},{32,40},{40,48},{48,56},{56,64},{64,7... | collective-permute-start | bytes 786440 | tf_op jit(solution)/shard_map/ppermute | solution.py:20
  36.2 60.4 %copy-start.6 = (bf16[512,256]{1,0:T(8,128)(2,1)}, bf16[512,256]{1,0:T(8,128)(2,1)S(1)}, u32[]{:S(2)}) copy-start(bf16[512,256]{1,0:T(8,128)(2,1)S(1)} %collective-permute-done.1.refs_2_) | copy-start | bytes 786436
  36.2 8.7 %collective-permute-start.3 = (bf16[512,256]{1,0:T(8,128)(2,1)S(1)}, bf16[512,256]{1,0:T(8,128)(2,1)S(1)}, u32[]{:S(2)}, u32[]{:S(2)}) collective-permute-start(bf16[512,256]{1,0:T(8,128)(2,1)S(1)} %collective-permute-done.1.refs_2_), channel_id=1, source_target_pairs={{0,120},{8,0},{16,8},{24,16},{32,24},{40,32},{48,40},{56,48},{64,5... | collective-permute-start | bytes 786440 | tf_op jit(solution)/shard_map/ppermute | solution.py:20
  42.9 1.9 copy-start.7
  42.9 8.7 %collective-permute-start.4 = (bf16[512,256]{1,0:T(8,128)(2,1)S(1)}, bf16[512,256]{1,0:T(8,128)(2,1)S(1)}, u32[]{:S(2)}, u32[]{:S(2)}) collective-permute-start(bf16[512,256]{1,0:T(8,128)(2,1)S(1)} %collective-permute-done.2.refs_3_), channel_id=1, source_target_pairs={{0,8},{8,16},{16,24},{24,32},{32,40},{40,48},{48,56},{56,64},{64,7... | collective-permute-start | bytes 786440 | tf_op jit(solution)/shard_map/ppermute | solution.py:20
  44.9 6.8 %copy-start.8 = (bf16[512,256]{1,0:T(8,128)(2,1)}, bf16[512,256]{1,0:T(8,128)(2,1)S(1)}, u32[]{:S(2)}) copy-start(bf16[512,256]{1,0:T(8,128)(2,1)S(1)} %collective-permute-done.3.refs_4_) | copy-start | bytes 786436
  44.9 8.7 %collective-permute-start.5 = (bf16[512,256]{1,0:T(8,128)(2,1)S(1)}, bf16[512,256]{1,0:T(8,128)(2,1)S(1)}, u32[]{:S(2)}, u32[]{:S(2)}) collective-permute-start(bf16[512,256]{1,0:T(8,128)(2,1)S(1)} %collective-permute-done.3.refs_4_), channel_id=1, source_target_pairs={{0,120},{8,0},{16,8},{24,16},{32,24},{40,32},{48,40},{56,48},{64,5... | collective-permute-start | bytes 786440 | tf_op jit(solution)/shard_map/ppermute | solution.py:20
  51.7 1.9 copy-start.9
  51.7 8.7 %collective-permute-start.6 = (bf16[512,256]{1,0:T(8,128)(2,1)S(1)}, bf16[512,256]{1,0:T(8,128)(2,1)S(1)}, u32[]{:S(2)}, u32[]{:S(2)}) collective-permute-start(bf16[512,256]{1,0:T(8,128)(2,1)S(1)} %collective-permute-done.4.refs_5_), channel_id=1, source_target_pairs={{0,8},{8,16},{16,24},{24,32},{32,40},{40,48},{48,56},{56,64},{64,7... | collective-permute-start | bytes 786440 | tf_op jit(solution)/shard_map/ppermute | solution.py:20
  53.6 6.8 %copy-start.10 = (bf16[512,256]{1,0:T(8,128)(2,1)}, bf16[512,256]{1,0:T(8,128)(2,1)S(1)}, u32[]{:S(2)}) copy-start(bf16[512,256]{1,0:T(8,128)(2,1)S(1)} %collective-permute-done.5.refs_6_) | copy-start | bytes 786436
  53.6 8.7 %collective-permute-start.7 = (bf16[512,256]{1,0:T(8,128)(2,1)S(1)}, bf16[512,256]{1,0:T(8,128)(2,1)S(1)}, u32[]{:S(2)}, u32[]{:S(2)}) collective-permute-start(bf16[512,256]{1,0:T(8,128)(2,1)S(1)} %collective-permute-done.5.refs_6_), channel_id=1, source_target_pairs={{0,120},{8,0},{16,8},{24,16},{32,24},{40,32},{48,40},{56,48},{64,5... | collective-permute-start | bytes 786440 | tf_op jit(solution)/shard_map/ppermute | solution.py:20
  60.4 1.9 copy-start.11
  60.4 8.7 %collective-permute-start.8 = (bf16[512,256]{1,0:T(8,128)(2,1)S(1)}, bf16[512,256]{1,0:T(8,128)(2,1)S(1)}, u32[]{:S(2)}, u32[]{:S(2)}) collective-permute-start(bf16[512,256]{1,0:T(8,128)(2,1)S(1)} %collective-permute-done.6.refs_7_), channel_id=1, source_target_pairs={{0,8},{8,16},{16,24},{24,32},{32,40},{40,48},{48,56},{56,64},{64,7... | collective-permute-start | bytes 786440 | tf_op jit(solution)/shard_map/ppermute | solution.py:20
  62.3 6.8 %copy-start.12 = (bf16[512,256]{1,0:T(8,128)(2,1)}, bf16[512,256]{1,0:T(8,128)(2,1)S(1)}, u32[]{:S(2)}) copy-start(bf16[512,256]{1,0:T(8,128)(2,1)S(1)} %collective-permute-done.7.refs_8_) | copy-start | bytes 786436
  62.3 8.7 %collective-permute-start.9 = (bf16[512,256]{1,0:T(8,128)(2,1)S(1)}, bf16[512,256]{1,0:T(8,128)(2,1)S(1)}, u32[]{:S(2)}, u32[]{:S(2)}) collective-permute-start(bf16[512,256]{1,0:T(8,128)(2,1)S(1)} %collective-permute-done.7.refs_8_), channel_id=1, source_target_pairs={{0,120},{8,0},{16,8},{24,16},{32,24},{40,32},{48,40},{56,48},{64,5... | collective-permute-start | bytes 786440 | tf_op jit(solution)/shard_map/ppermute | solution.py:20
  69.1 1.9 copy-start.13
  69.1 8.3 %collective-permute-start.10 = (bf16[512,256]{1,0:T(8,128)(2,1)S(1)}, bf16[512,256]{1,0:T(8,128)(2,1)S(1)}, u32[]{:S(2)}, u32[]{:S(2)}) collective-permute-start(bf16[512,256]{1,0:T(8,128)(2,1)S(1)} %collective-permute-done.8.refs_9_), channel_id=1, source_target_pairs={{0,8},{8,16},{16,24},{24,32},{32,40},{40,48},{48,56},{56,64},{64,7... | collective-permute-start | bytes 786440 | tf_op jit(solution)/shard_map/ppermute | solution.py:20
  71.0 6.4 %copy-start.14 = (bf16[512,256]{1,0:T(8,128)(2,1)}, bf16[512,256]{1,0:T(8,128)(2,1)S(1)}, u32[]{:S(2)}) copy-start(bf16[512,256]{1,0:T(8,128)(2,1)S(1)} %collective-permute-done.9.refs_10_) | copy-start | bytes 786436
  71.1 8.3 %collective-permute-start.11 = (bf16[512,256]{1,0:T(8,128)(2,1)S(1)}, bf16[512,256]{1,0:T(8,128)(2,1)}, u32[]{:S(2)}, u32[]{:S(2)}) collective-permute-start(bf16[512,256]{1,0:T(8,128)(2,1)S(1)} %collective-permute-done.9.refs_10_), channel_id=1, source_target_pairs={{0,120},{8,0},{16,8},{24,16},{32,24},{40,32},{48,40},{56,48},{64,5... | collective-permute-start | bytes 786440 | tf_op jit(solution)/shard_map/ppermute | solution.py:20
  77.4 1.9 copy-start.15
  77.4 9.0 %collective-permute-start.12 = (bf16[512,256]{1,0:T(8,128)(2,1)S(1)}, bf16[512,256]{1,0:T(8,128)(2,1)}, u32[]{:S(2)}, u32[]{:S(2)}) collective-permute-start(bf16[512,256]{1,0:T(8,128)(2,1)S(1)} %collective-permute-done.10.refs_11_), channel_id=1, source_target_pairs={{0,8},{8,16},{16,24},{24,32},{32,40},{40,48},{48,56},{56,64},{64,7... | collective-permute-start | bytes 786440 | tf_op jit(solution)/shard_map/ppermute | solution.py:20
  79.4 12.7 %collective-permute-start.13 = (bf16[512,256]{1,0:T(8,128)(2,1)}, bf16[512,256]{1,0:T(8,128)(2,1)}, u32[]{:S(2)}, u32[]{:S(2)}) collective-permute-start(bf16[512,256]{1,0:T(8,128)(2,1)} %collective-permute-done.11.refs_12_), channel_id=1, source_target_pairs={{0,120},{8,0},{16,8},{24,16},{32,24},{40,32},{48,40},{56,48},{64,5... | collective-permute-start | bytes 786440 | tf_op jit(solution)/shard_map/ppermute | solution.py:20
  86.4 10.1 %collective-permute-start.14 = (bf16[512,256]{1,0:T(8,128)(2,1)}, bf16[512,256]{1,0:T(8,128)(2,1)}, u32[]{:S(2)}, u32[]{:S(2)}) collective-permute-start(bf16[512,256]{1,0:T(8,128)(2,1)} %collective-permute-done.12.refs_13_), channel_id=1, source_target_pairs={{0,8},{8,16},{16,24},{24,32},{32,40},{40,48},{48,56},{56,64},{64,7... | collective-permute-start | bytes 786440 | tf_op jit(solution)/shard_map/ppermute | solution.py:20
  211.4 1.2 copy-start.1
  222.5 4.0 %copy-start.4 = (f32[64,128]{1,0:T(8,128)S(1)}, f32[64,128]{1,0:T(8,128)}, u32[]{:S(2)}) copy-start(f32[64,128]{1,0:T(8,128)} %inverse.1) | copy-start | bytes 98308
Sparse Core Ops, SparseCore 0:
  9.5 63.0 all-gather.1

commit v2 on v0

v2 whole, which is shorter than its diff:
```python
import functools
import jax
import jax.numpy as jnp
from jax import lax
from jax.experimental import pallas as pl
from jax.experimental.pallas import tpu as pltpu
from jax.sharding import Mesh, PartitionSpec as P

TILE = 128
NX, NZ, NY, NC = 4, 16, 4, 2
ZH, ZL = 4, 4
HALF = 32
ROWS = TILE // ZL
STEPS = (0, -1, 1, -2)
BLOCK = 256

damping_ratio = 0.1
tiny_value = 1e-06
HI = lax.Precision.HIGHEST
F32 = jnp.float32
BF16 = jnp.bfloat16


def shift(value, axis, step, size):
    return lax.ppermute(value, axis, [(i, (i + step) % size) for i in range(size)])


def spread(value, axis, size):
    copies = jnp.broadcast_to(value[None], (size,) + value.shape)
    return lax.all_to_all(copies, axis, 0, 0, tiled=True)


def fetch(kinds, chunks, head, in_proj, x, z, feat_buf, head_buf, proj_buf, sems):
    copies = []
    for j, (kind, step) in enumerate(kinds):
        width = chunks[j].shape[1]
        copy = pltpu.make_async_copy(chunks[j], feat_buf.at[:, pl.ds(j * width, width)], sems.at[j, 0])
        copy.start()
        copies.append(copy)
        for a in range(4):
            for i in range(ZH):
                if kind == "x":
                    xs, zs, low = (x + step + NX) % NX, (z + STEPS[a] + NZ) % ZL, 0
                else:
                    xs, zs, low = a, (z + step + NZ) % ZL, HALF
                first = pl.multiple_of(xs * (NZ * 2 * HALF) + (i * ZL + zs) * (2 * HALF) + low, HALF)
                place = j * width + (a * ZH + i) * HALF
                copy = pltpu.make_async_copy(
                    head.at[pl.ds(first, HALF), :], head_buf.at[pl.ds(place, HALF), :], sems.at[j, 1 + a * ZH + i]
                )
                copy.start()
                copies.append(copy)
                proj_buf[pl.ds(place, HALF), :] = in_proj[pl.ds(first, HALF), :]
    for copy in copies:
        copy.wait()


def first_kernel(kinds, place_ref, *refs):
    count = len(kinds)
    chunks = refs[:count]
    head, in_proj, acc, proj = refs[count : count + 4]
    feat_buf, head_buf, proj_buf, sems = refs[count + 4 :]
    x, z = place_ref[0], place_ref[1]
    fetch(kinds, chunks, head, in_proj, x, z, feat_buf, head_buf, proj_buf, sems)

    def column_block(n, carry):
        cols = pl.ds(pl.multiple_of(n * BLOCK, BLOCK), BLOCK)
        acc[:, cols] = jnp.dot(feat_buf[...], head_buf[:, cols], preferred_element_type=F32)
        return carry

    lax.fori_loop(0, acc.shape[1] // BLOCK, column_block, 0)
    own = pl.ds(pl.multiple_of(x * TILE, TILE), TILE)
    proj[...] = jnp.dot(feat_buf[own, :], proj_buf[...], preferred_element_type=F32)


def stat_tile(peak, total, rows):
    lane = lax.broadcasted_iota(jnp.int32, (rows, TILE), 1)
    stat = jnp.where(lane == 0, peak, jnp.where(lane == 1, total, 0.0))
    if rows < TILE:
        stat = jnp.concatenate([stat, jnp.zeros((TILE - rows, TILE), F32)], axis=0)
    return stat.T[0:8, :]


def logits_kernel(kinds, place_ref, *refs):
    count = len(kinds)
    chunks = refs[:count]
    head, in_proj, acc, proj_in, out_proj, targets, packed, proj = refs[count : count + 8]
    feat_buf, head_buf, proj_buf, logit_buf, sems = refs[count + 8 :]
    x, z = place_ref[0], place_ref[1]
    fetch(kinds, chunks, head, in_proj, x, z, feat_buf, head_buf, proj_buf, sems)
    total_cols = head.shape[1]

    def column_block(n, carry):
        cols = pl.ds(pl.multiple_of(n * BLOCK, BLOCK), BLOCK)
        logit_buf[:, cols] = acc[:, cols] + jnp.dot(feat_buf[...], head_buf[:, cols], preferred_element_type=F32)
        return carry

    lax.fori_loop(0, total_cols // BLOCK, column_block, 0)
    own = pl.ds(pl.multiple_of(x * TILE, TILE), TILE)
    proj[...] = proj_in[...] + jnp.dot(feat_buf[own, :], proj_buf[...], preferred_element_type=F32)
    table = out_proj[...]
    vocab_first = (x * NZ + z) * total_cols

    def row_block(i, carry):
        rows = pl.ds(pl.multiple_of(i * TILE, TILE), TILE)
        logits = logit_buf[rows, :]
        peak = jnp.max(logits, axis=1, keepdims=True)
        weight = jnp.exp(logits - peak)
        total = jnp.sum(weight, axis=1, keepdims=True)
        part1 = weight.astype(BF16)
        rest = weight - part1.astype(F32)
        part2 = rest.astype(BF16)
        part3 = (rest - part2.astype(F32)).astype(BF16)
        mixed = jnp.dot(part1, table, preferred_element_type=F32)
        mixed += jnp.dot(part2, table, preferred_element_type=F32)
        mixed += jnp.dot(part3, table, preferred_element_type=F32)
        column = lax.broadcasted_iota(jnp.int32, logits.shape, 1) + vocab_first
        hit = jnp.where(column == targets[rows, :], 1.0, 0.0).astype(BF16)
        picked = jnp.dot(hit, table, preferred_element_type=F32)
        data = jnp.concatenate([mixed, picked], axis=1)
        stat = stat_tile(peak, total, TILE)
        for b in range(ZL):
            packed[i * ZL + b, 0:ROWS, :] = data[b * ROWS : (b + 1) * ROWS, :]
            packed[i * ZL + b, ROWS : ROWS + 8, :] = stat
        return carry

    lax.fori_loop(0, NX, row_block, 0)


def merge(parts):
    peak = functools.reduce(jnp.maximum, [p for _, p, _ in parts])
    scales = [jnp.exp(p - peak) for _, p, _ in parts]
    total = sum(s * t for s, (_, _, t) in zip(scales, parts))
    mixed = sum(s * data[:, :64] for s, (data, _, _) in zip(scales, parts))
    picked = sum(data[:, 64:] for data, _, _ in parts)
    return mixed, picked, peak, total


def merge_kernel(place_ref, packed, out, turned):
    low = place_ref[1] % ZL
    count = packed.shape[0]
    turned[...] = packed[:, ROWS : ROWS + 8, :].reshape(count * 8, TILE).T
    stat = turned[pl.ds(pl.multiple_of(low * ROWS, ROWS), ROWS), :]
    parts = [(packed[i, 0:ROWS, :], stat[:, 8 * i : 8 * i + 1], stat[:, 8 * i + 1 : 8 * i + 2]) for i in range(count)]
    mixed, picked, peak, total = merge(parts)
    out[0:ROWS, :] = jnp.concatenate([mixed, picked], axis=1)
    out[ROWS : ROWS + 8, :] = stat_tile(peak, total, ROWS)


def gram_kernel(place_ref, lengths, packed, proj, out):
    stat = packed[:, ROWS : ROWS + 8, :].reshape(NZ * 8, TILE).T[0:ROWS, :]
    blocks = []
    for b in range(ZL):
        parts = []
        for i in range(ZH):
            at = i * ZL + b
            parts.append((packed[at, 0:ROWS, :], stat[:, 8 * at : 8 * at + 1], stat[:, 8 * at + 1 : 8 * at + 2]))
        mixed, picked, _, total = merge(parts)
        blocks.append(mixed / total - picked)
    length = lengths[place_ref[2]]
    both = jnp.concatenate([jnp.concatenate(blocks, axis=0), proj[...]], axis=1)
    row = lax.broadcasted_iota(jnp.int32, both.shape, 0)
    both = jnp.where(row < length, both, 0.0)
    gram = lax.dot_general(both, both, (((0,), (0,)), ((), ())), precision=HI, preferred_element_type=F32)
    row = lax.broadcasted_iota(jnp.int32, (64, 64), 0)
    col = lax.broadcasted_iota(jnp.int32, (64, 64), 1)
    cov_in = gram[64:128, 64:128]
    root = jnp.sqrt(jnp.full((64, 64), length.astype(F32)))
    out[0:64, :] = jnp.concatenate(
        [jnp.where(row <= col, gram[0:64, 0:64], cov_in), gram[0:64, 64:128] / root], axis=1
    )
    diag = jnp.sum(jnp.where(row == col, cov_in, 0.0), axis=0, keepdims=True)
    out[64:72, :] = jnp.broadcast_to(jnp.concatenate([diag, diag], axis=1), (8, TILE))


def whiten_kernel(lengths, grams, out):
    total = functools.reduce(jnp.add, [lengths[s] for s in range(lengths.shape[0])]).astype(F32)
    summed = functools.reduce(jnp.add, [grams[d] for d in range(grams.shape[0])]) / total
    row = lax.broadcasted_iota(jnp.int32, (64, TILE), 0)
    lane = lax.broadcasted_iota(jnp.int32, (64, TILE), 1)
    left = lane < 64
    inner = jnp.where(left, lane, lane - 64)
    block = jnp.where(left, summed[0:64, :], 0.0)
    turned = jnp.concatenate([block, jnp.zeros_like(block)], axis=0).T[0:64, :]
    upper, lower = row < inner, row > inner
    cov_out = jnp.where(lower, turned, block)[:, 0:64]
    cov_in = jnp.where(upper, turned, block)[:, 0:64]
    work = jnp.concatenate([cov_out, cov_in], axis=1)
    on_diag = row == inner
    work = jnp.where(on_diag & (lane >= 64), summed[64:65, :], work)
    diag = jnp.where(on_diag, work, 0.0)
    trace_out = jnp.sum(jnp.where(left, diag, 0.0))
    trace_in = jnp.sum(jnp.where(left, 0.0, diag))
    damp = jnp.where(left, damping_ratio * trace_out / 64 + tiny_value, damping_ratio * trace_in / 64 + tiny_value)
    work = work + jnp.where(on_diag, damp, 0.0)
    for k in range(64):
        at_lane = inner == k
        pivot_row = work[k : k + 1, :]
        column = jnp.where(left, work[:, k : k + 1], work[:, 64 + k : 65 + k])
        inv = 1.0 / column[k : k + 1, :]
        scaled = jnp.where(at_lane[0:1, :], inv, pivot_row * inv)
        body = jnp.where(at_lane, 0.0, work) - column * scaled
        work = jnp.where(row == k, scaled, body)
    inv_out, inv_in = work[:, 0:64], work[:, 64:128]
    zero = jnp.zeros((64, 64), F32)
    twice = jnp.concatenate(
        [jnp.concatenate([inv_in, zero], axis=1), jnp.concatenate([zero, inv_in], axis=1)], axis=0
    )
    pairs = []
    for s in range(0, grams.shape[0], 2):
        at = [(q % NX) * (NY * NC) + q // NX for q in (s, s + 1)]
        pairs.append(jnp.concatenate([grams[at[0], 0:64, 64:128], grams[at[1], 0:64, 64:128]], axis=1))
    half = jnp.dot(jnp.concatenate(pairs, axis=0), twice, precision=HI, preferred_element_type=F32)
    half = jnp.concatenate([half[64 * p : 64 * p + 64, :] for p in range(len(pairs))], axis=1)
    out[...] = jnp.dot(inv_out, half, precision=HI, preferred_element_type=F32).astype(BF16)


def full(shape, dtype=F32):
    return jax.ShapeDtypeStruct(shape, dtype)


VMEM = pl.BlockSpec(memory_space=pltpu.VMEM)
SMEM = pl.BlockSpec(memory_space=pltpu.SMEM)
ANY = pl.BlockSpec(memory_space=pl.ANY)
ZAXIS = ("zh", "zl")


def per_device(hidden, head_weight, in_proj, out_proj, targets, lengths, grad_store):
    token_count, width = hidden.shape
    x = lax.axis_index("x")
    z = lax.axis_index("zh") * ZL + lax.axis_index("zl")
    rows = lax.axis_index("y") * NC + lax.axis_index("c")
    place = jnp.stack([x, z, rows * NX + x]).astype(jnp.int32)
    head = lax.all_gather(head_weight, ("y", "c"), axis=0, tiled=True)
    strided = spread(hidden.T, "zh", ZH)
    a_own = strided[:, :HALF, :].reshape(ZH * HALF, token_count).T
    a_parts = [a_own] + [shift(a_own, ZAXIS, -s, NZ) for s in STEPS[1:]]
    b_own = spread(strided[:, HALF:, :].reshape(ZH * HALF, token_count), "x", NX)
    b_own = b_own.reshape(NX * ZH * HALF, token_count).T
    a_own = jnp.concatenate(a_parts, axis=1)
    b_back, b_next = shift(b_own, ZAXIS, 1, NZ), shift(b_own, ZAXIS, -1, NZ)
    a_back, a_next = shift(a_own, "x", 1, NX), shift(a_own, "x", -1, NX)
    b_far, a_far = shift(b_back, ZAXIS, 1, NZ), shift(a_back, "x", 1, NX)
    cols = head.shape[1]
    size = a_own.shape[1]

    def buffers(count):
        return [
            pltpu.VMEM((token_count, count * size), BF16),
            pltpu.VMEM((count * size, cols), BF16),
            pltpu.VMEM((count * size, 64), BF16),
        ]

    early = (("x", 0), ("z", 0), ("x", -1), ("x", 1), ("z", -1), ("z", 1))
    acc, proj = pl.pallas_call(
        functools.partial(first_kernel, early),
        out_shape=(full((token_count, cols)), full((TILE, 64))),
        in_specs=[SMEM] + [ANY] * len(early) + [ANY, VMEM],
        out_specs=(VMEM, VMEM),
        scratch_shapes=buffers(len(early)) + [pltpu.SemaphoreType.DMA((len(early), 17))],
        name="logits_first",
    )(place, a_own, b_own, a_back, a_next, b_back, b_next, head, in_proj)
    late = (("x", -2), ("z", -2))
    packed, proj = pl.pallas_call(
        functools.partial(logits_kernel, late),
        out_shape=(full((NX * ZL, ROWS + 8, TILE)), full((TILE, 64))),
        in_specs=[SMEM] + [ANY] * len(late) + [ANY] + [VMEM] * 5,
        out_specs=(VMEM, VMEM),
        scratch_shapes=buffers(len(late))
        + [pltpu.VMEM((token_count, cols), F32), pltpu.SemaphoreType.DMA((len(late), 17))],
        name="logits_last",
    )(place, a_far, b_far, head, in_proj, acc, proj, out_proj, targets[:, None])
    merged = pl.pallas_call(
        merge_kernel,
        out_shape=full((ROWS + 8, TILE)),
        in_specs=[SMEM, VMEM],
        out_specs=VMEM,
        scratch_shapes=[pltpu.VMEM((TILE, TILE), F32)],
        name="merge",
    )(place, lax.all_to_all(packed, ("x", "zl"), 0, 0, tiled=True))
    gram = pl.pallas_call(
        gram_kernel,
        out_shape=full((72, TILE)),
        in_specs=[SMEM, SMEM, VMEM, VMEM],
        out_specs=VMEM,
        name="gram",
    )(place, lengths, spread(merged, ZAXIS, NZ), proj)
    seqs = NX * NY * NC
    grams = spread(gram, ("x", "y", "c"), seqs)
    whitened = pl.pallas_call(
        whiten_kernel,
        out_shape=full((64, seqs * 64), BF16),
        in_specs=[SMEM, VMEM],
        out_specs=VMEM,
        name="whiten",
    )(lengths, grams)
    whitened = jnp.transpose(whitened.reshape(64, seqs, 64), (1, 0, 2)).reshape(seqs, 64 * 64)
    return jnp.dot(whitened, grad_store.T, preferred_element_type=F32)


def solution(mesh):
    grid = Mesh(mesh.devices.reshape(NX, ZH, ZL, NY, NC), ("x", "zh", "zl", "y", "c"))
    return jax.shard_map(
        per_device,
        mesh=grid,
        in_specs=(
            P(("y", "c"), ("x", "zh", "zl")),
            P(("y", "c"), ("x", "zh", "zl")),
            P(),
            P(("x", "zh", "zl"), None),
            P(("y", "c")),
            P(),
            P(("x", "zh", "zl", "y", "c"), None),
        ),
        out_specs=P(None, ("x", "zh", "zl", "y", "c")),
        check_vma=False,
    )
```

time: 846 us -> 204 us (0.24)
  waiting for transfers between devices: 501 us -> 4.85 us
  blocking collectives: 276 us -> 95.6 us
  starting transfers between devices: 0.08 us -> 40.3 us
  Pallas kernels: 0 us -> 35.3 us
  other arithmetic: 28.9 us -> 0.74 us
  matrix products: 23.1 us -> 1.35 us
  local copies, waits for them, and re-layouts: 0.92 us -> 10.9 us
    psum x1 -> x0, waiting for transfers between devices: 298 us -> none  [per_device(): lax.psum(jnp.dot(gradient, out_table, precision=lax.Precision.HIGHEST), '...]
    all_gather x2 -> x1, waiting for transfers between devices: 202 us -> 0.01 us  [per_device(): head = lax.all_gather(head_weight, ('y', 'c'), axis=0, tiled=True)]
    psum x2 -> x0, blocking collectives: 143 us -> none  [the longest x1 111 us: per_device(): row_sum = lax.psum(jnp.sum(exponent, axis=1), 'vocab')]
    pmax x1 -> x0, blocking collectives: 117 us -> none  [per_device(): row_max = lax.pmax(jnp.max(logits, axis=1), 'vocab')]
    all_to_all x0 -> x4, blocking collectives: none -> 95.6 us  [the longest x3 82.6 us: spread(): return lax.all_to_all(copies, axis, 0, 0, tiled=True)]
    ppermute x0 -> x9, starting transfers between devices: none -> 36.1 us  [shift(): lax.ppermute(value, axis, [(i, (i + step) % size) for i in range(size)])]
    pallas_call x0 -> x5, Pallas kernels: none -> 35.3 us  [the longest x1 11.3 us: per_device(): pl.pallas_call(functools.partial(first_kernel, early), out_shape=(full((t...]
    another operation x10 -> x1, other arithmetic: 24.1 us -> 0.66 us  [per_device(): place = jnp.stack([x, z, rows * NX + x]).astype(jnp.int32)]
  transfers between devices with their start and end apart: 3 -> 11, of which waited for: 3 -> 2; matrix products, arithmetic and copies ran while one was open for 1% -> 4% of each run, Pallas kernels for 0% -> 6%
where the time goes in v2:
time: 204 us; the launch traced here: 203 us
  blocking collectives  95.6 us (47%)
  starting transfers between devices  40.3 us (20%)
  Pallas kernels  35.3 us (17%)
  between operations  13.6 us (7%)
  local copies, waits for them, and re-layouts  10.9 us (5%)
  waiting for transfers between devices  4.85 us (2%)
    all_to_all x3, blocking collectives, spread(): return lax.all_to_all(copies, axis, 0, 0, tiled=True)  82.6 us
    ppermute x9, starting transfers between devices, shift(): lax.ppermute(value, axis, [(i, (i + step) % size) for i in range(size)])  36.1 us
    all_to_all x1, blocking collectives, per_device(): lax.all_to_all(packed, ('x', 'zl'), 0, 0, tiled=True)  13 us
    pallas_call x1, Pallas kernels, per_device(): pl.pallas_call(functools.partial(first_kernel, early), out_shape=(full((t...  11.3 us
    pallas_call x1, Pallas kernels, per_device(): pl.pallas_call(whiten_kernel, out_shape=full((64, seqs * 64), BF16), in_s...  9.86 us
    pallas_call x1, Pallas kernels, per_device(): pl.pallas_call(functools.partial(logits_kernel, late), out_shape=(full((N...  9.47 us
    all_to_all x1, starting transfers between devices, spread(): return lax.all_to_all(copies, axis, 0, 0, tiled=True)  4.15 us
    ppermute x9, waiting for transfers between devices, shift(): lax.ppermute(value, axis, [(i, (i + step) % size) for i in range(size)])  4.13 us
  transfers between devices with their start and end apart: 11, of which 2 were waited for; matrix products, arithmetic and copies ran while one was open for 4% of the time, Pallas kernels for 6%

profile of v2, /device:TPU:1, one launch (start us, length us, event | category | flops | bytes accessed | tf_op | source)
XLA Modules:
  0.0 202.7 jit_solution(8935202482683558366)
XLA Ops:
  6.5 0.7 all-gather.2.cloned.1.call-update
  7.3 0.9 broadcast_in_dim.12
  8.1 29.6 %all_to_all.25 = bf16[4,64,512]{2,1,0:T(8,128)(2,1)S(1)} all-to-all(bf16[4,64,512]{2,1,0:T(8,128)(2,1)S(1)} %broadcast_in_dim.12), channel_id=1, replica_groups=mesh['x'=4,'zh'=4,'zl'=4,'y'=4,'c'=2] {'zh'}, dimensions={0} | all-to-all | bytes 524288 | tf_op jit(solution)/shard_map/all_to_all | solution.py:30
  37.8 0.1 copy.20
  37.9 0.9 broadcast_in_dim.14
  38.8 4.2 %all-to-all-start.1 = ((bf16[4,128,512]{1,2,0:T(8,128)(2,1)}), bf16[4,128,512]{1,2,0:T(8,128)(2,1)}, u32[]{:S(2)}, u32[]{:S(2)}) async-start(bf16[4,128,512]{1,2,0:T(8,128)(2,1)} %broadcast_in_dim.14), calls=%async_computation.1 | async-start | bytes 1048576 | tf_op jit(solution)/shard_map/all_to_all | solution.py:30
  43.0 0.0 copy-start.3
  43.0 0.1 copy.19
  43.1 0.0 copy-start.4
  43.1 9.2 %collective-permute-start = (bf16[512,128]{1,0:T(8,128)(2,1)S(1)}, bf16[512,128]{1,0:T(8,128)(2,1)S(1)}, u32[]{:S(2)}, u32[]{:S(2)}) collective-permute-start(bf16[512,128]{1,0:T(8,128)(2,1)S(1)} %bitcast.23), channel_id=1, source_target_pairs={{0,8},{8,16},{16,24},{24,32},{32,40},{40,48},{48,56},{56,64},{64,7... | collective-permute-start | bytes 393224 | tf_op jit(solution)/shard_map/ppermute | solution.py:25
  52.3 1.9 collective-permute-start.1
  54.3 3.9 %collective-permute-start.2 = (bf16[512,128]{1,0:T(8,128)(2,1)S(1)}, bf16[512,128]{1,0:T(8,128)(2,1)S(1)}, u32[]{:S(2)}, u32[]{:S(2)}) collective-permute-start(bf16[512,128]{1,0:T(8,128)(2,1)S(1)} %bitcast.25), channel_id=1, source_target_pairs={{0,16},{8,24},{16,32},{24,40},{32,48},{40,56},{48,64},{56,72},{64,... | collective-permute-start | bytes 393224 | tf_op jit(solution)/shard_map/ppermute | solution.py:25
  58.2 0.0 collective-permute-done
  58.2 0.2 collective-permute-done.1
  58.5 3.9 %collective-permute-done.2 = bf16[512,128]{1,0:T(8,128)(2,1)S(1)} collective-permute-done((bf16[512,128]{1,0:T(8,128)(2,1)S(1)}, bf16[512,128]{1,0:T(8,128)(2,1)S(1)}, u32[]{:S(2)}, u32[]{:S(2)}) %collective-permute-start.2) | collective-permute-done | bytes 131104 | tf_op jit(solution)/shard_map/ppermute | solution.py:25
  62.3 0.1 pad_maximum_fusion.refs_0_
  62.4 3.3 %collective-permute-start.3 = (bf16[512,512]{1,0:T(8,128)(2,1)S(1)}, bf16[512,512]{1,0:T(8,128)(2,1)}, u32[]{:S(2)}, u32[]{:S(2)}) collective-permute-start(bf16[512,512]{1,0:T(8,128)(2,1)S(1)} %pad_maximum_fusion.refs_0_), channel_id=1, source_target_pairs={{0,128},{128,256},{256,384},{384,0},{1,129},{129,257},{257,385},{3... | collective-permute-start | bytes 1572872 | tf_op jit(solution)/shard_map/ppermute | solution.py:25
  65.7 0.0 all-to-all-done.1
  65.8 1.1 bitcast_bitcast_fusion.refs_1_
  66.9 4.7 %collective-permute-start.5 = (bf16[512,512]{1,0:T(8,128)(2,1)S(1)}, bf16[512,512]{1,0:T(8,128)(2,1)}, u32[]{:S(2)}, u32[]{:S(2)}) collective-permute-start(bf16[512,512]{1,0:T(8,128)(2,1)S(1)} %bitcast_bitcast_fusion.refs_1_), channel_id=1, source_target_pairs={{0,8},{8,16},{16,24},{24,32},{32,40},{40,48},{48,56},{56,64},{64,7... | collective-permute-start | bytes 1572872 | tf_op jit(solution)/shard_map/ppermute | solution.py:25
  71.5 4.3 %collective-permute-start.7 = (bf16[512,512]{1,0:T(8,128)(2,1)S(1)}, bf16[512,512]{1,0:T(8,128)(2,1)}, u32[]{:S(2)}, u32[]{:S(2)}) collective-permute-start(bf16[512,512]{1,0:T(8,128)(2,1)S(1)} %pad_maximum_fusion.refs_0_), channel_id=1, source_target_pairs={{0,384},{128,0},{256,128},{384,256},{1,385},{129,1},{257,129},{385... | collective-permute-start | bytes 1572872 | tf_op jit(solution)/shard_map/ppermute | solution.py:25
  75.8 1.9 collective-permute-start.8
  77.7 0.0 collective-permute-done.3.refs_2_
  77.7 1.9 collective-permute-start.4
  79.7 0.0 collective-permute-done.5.refs_4_
  79.7 5.0 %collective-permute-start.6 = (bf16[512,512]{1,0:T(8,128)(2,1)}, bf16[512,512]{1,0:T(8,128)(2,1)}, u32[]{:S(2)}, u32[]{:S(2)}) collective-permute-start(bf16[512,512]{1,0:T(8,128)(2,1)} %collective-permute-done.5.refs_4_), channel_id=1, source_target_pairs={{0,8},{8,16},{16,24},{24,32},{32,40},{40,48},{48,56},{56,64},{64,7... | collective-permute-start | bytes 1572872 | tf_op jit(solution)/shard_map/ppermute | solution.py:25
  84.7 2.4 %copy.23.refs_7_.refs_3_ = bf16[4096,64]{1,0:T(8,128)(2,1)} copy(bf16[4096,64]{0,1:T(8,128)(2,1)} %param.9) | data formatting | bytes 1048576 | tf_op args[2]
  87.1 0.8 copy.24.refs_6_
  87.9 0.9 copy.25.refs_7_
  88.7 0.7 pad_add_fusion.place_ref
  89.4 0.0 collective-permute-done.7.refs_3_
  89.4 0.0 collective-permute-done.8.refs_5_
  89.4 11.3 %logits_first.1 = (f32[512,1024]{1,0:T(8,128)}, f32[128,64]{1,0:T(8,128)}) custom-call(s32[3]{0:T(128)} %pad_add_fusion.place_ref, bf16[512,512]{1,0:T(8,128)(2,1)} %copy-done.1, bf16[512,512]{1,0:T(8,128)(2,1)} %copy-done.2, bf16[512,512]{1,0:T(8,128)(2,1)} %collective-permute-done.3.refs_2_, bf16[512,512]{1,0:T(8,128)(2,1)} %collective-permute-done.7.refs_3_, ...), custom_call_target="tpu_custom_call" | custom-call | tf_op jit(solution)/shard_map/logits_first/pallas_call | solution.py:255
  100.7 0.0 collective-permute-done.4.refs_0_
  100.7 0.0 collective-permute-done.6.refs_1_
  100.7 9.5 %logits_last.1 = (f32[16,40,128]{2,1,0:T(8,128)}, f32[128,64]{1,0:T(8,128)}) custom-call(s32[3]{0:T(128)} %pad_add_fusion.place_ref, bf16[512,512]{1,0:T(8,128)(2,1)} %collective-permute-done.4.refs_0_, bf16[512,512]{1,0:T(8,128)(2,1)} %collective-permute-done.6.refs_1_, bf16[4096,1024]{1,0:T(8,128)(2,1)} %all-gather.2.cloned.1.call-done.refs_6_.refs_2_, ...), custom_call_target="tpu_custom_call" | custom-call | tf_op jit(solution)/shard_map/logits_last/pallas_call | solution.py:264
  110.2 13.0 %all_to_all.26.packed = f32[16,40,128]{2,1,0:T(8,128)} all-to-all(f32[16,40,128]{2,1,0:T(8,128)} %get-tuple-element.11), channel_id=1, replica_groups=mesh['x'=4,'zh'=4,'zl'=4,'y'=4,'c'=2] {'x','zl'}, dimensions={0} | all-to-all | bytes 655360 | tf_op jit(solution)/shard_map/all_to_all | solution.py:280
  123.2 2.2 %merge.1 = f32[40,128]{1,0:T(8,128)} custom-call(s32[3]{0:T(128)} %pad_add_fusion.place_ref, f32[16,40,128]{2,1,0:T(8,128)} %all_to_all.26.packed), custom_call_target="tpu_custom_call" | custom-call | tf_op jit(solution)/shard_map/merge/pallas_call | solution.py:273
  125.5 0.7 broadcast_in_dim.32
  126.2 17.9 %all_to_all.27.packed = f32[16,40,128]{2,1,0:T(8,128)} all-to-all(f32[16,40,128]{2,1,0:T(8,128)S(1)} %broadcast_in_dim.32), channel_id=1, replica_groups=mesh['x'=4,'zh'=4,'zl'=4,'y'=4,'c'=2] {'zh','zl'}, dimensions={0} | all-to-all | bytes 655360 | tf_op jit(solution)/shard_map/all_to_all | solution.py:30
  144.1 2.5 %gram.1 = f32[72,128]{1,0:T(8,128)} custom-call(s32[3]{0:T(128)} %pad_add_fusion.place_ref, s32[32]{0:T(128)} %lengths.3, f32[16,40,128]{2,1,0:T(8,128)} %all_to_all.27.packed, f32[128,64]{1,0:T(8,128)} %get-tuple-element.12.proj), custom_call_target="tpu_custom_call" | custom-call | tf_op jit(solution)/shard_map/gram/pallas_call | solution.py:281
  146.6 0.8 broadcast_in_dim.33
  147.4 35.1 %all_to_all.28.grams = f32[32,72,128]{2,1,0:T(8,128)} all-to-all(f32[32,72,128]{2,1,0:T(8,128)S(1)} %broadcast_in_dim.33), channel_id=1, replica_groups=mesh['x'=4,'zh'=4,'zl'=4,'y'=4,'c'=2] {'x','y','c'}, dimensions={0} | all-to-all | bytes 2359296 | tf_op jit(solution)/shard_map/all_to_all | solution.py:30
  182.5 9.9 %whiten.1 = bf16[64,2048]{1,0:T(8,128)(2,1)} custom-call(s32[32]{0:T(128)} %lengths.3, f32[32,72,128]{2,1,0:T(8,128)} %all_to_all.28.grams), custom_call_target="tpu_custom_call" | custom-call | tf_op jit(solution)/shard_map/whiten/pallas_call | solution.py:290
  192.4 1.5 reshape.18
  193.8 0.2 copy.30
  194.0 0.5 reshape.19
  194.5 1.4 fusion.1
  (11 shorter events, 0.0 us)
Async XLA Ops:
  6.5 188.0 %copy-start = (bf16[256,4096]{1,0:T(8,128)(2,1)S(1)}, bf16[256,4096]{1,0:T(8,128)(2,1)}, u32[]{:S(2)}) copy-start(bf16[256,4096]{1,0:T(8,128)(2,1)} %param.13) | copy-start | bytes 6291460
  6.5 82.9 %all-gather.2.cloned.1.call-start = ((), (), s32[]{:S(2)}) async-start(), calls=%async_computation.5 | async-start | bytes 9437184 | tf_op jit(solution)/shard_map/all_gather | solution.py:234
  38.8 26.9 %all-to-all-start.1 = ((bf16[4,128,512]{1,2,0:T(8,128)(2,1)}), bf16[4,128,512]{1,2,0:T(8,128)(2,1)}, u32[]{:S(2)}, u32[]{:S(2)}) async-start(bf16[4,128,512]{1,2,0:T(8,128)(2,1)} %broadcast_in_dim.14), calls=%async_computation.1 | async-start | bytes 1048576 | tf_op jit(solution)/shard_map/all_to_all | solution.py:30
  43.0 44.1 %copy-start.3 = (bf16[1024,64]{0,1:T(8,128)(2,1)S(1)}, bf16[1024,64]{0,1:T(8,128)(2,1)}, u32[]{:S(2)}) copy-start(bf16[1024,64]{0,1:T(8,128)(2,1)} %param.10) | copy-start | bytes 393220
  43.1 44.8 %copy-start.4 = (s32[512]{0:T(512)S(1)}, s32[512]{0:T(512)}, u32[]{:S(2)}) copy-start(s32[512]{0:T(512)} %param.11) | copy-start | bytes 6148
  43.1 15.1 %collective-permute-start = (bf16[512,128]{1,0:T(8,128)(2,1)S(1)}, bf16[512,128]{1,0:T(8,128)(2,1)S(1)}, u32[]{:S(2)}, u32[]{:S(2)}) collective-permute-start(bf16[512,128]{1,0:T(8,128)(2,1)S(1)} %bitcast.23), channel_id=1, source_target_pairs={{0,8},{8,16},{16,24},{24,32},{32,40},{40,48},{48,56},{56,64},{64,7... | collective-permute-start | bytes 393224 | tf_op jit(solution)/shard_map/ppermute | solution.py:25
  52.3 6.1 %collective-permute-start.1 = (bf16[512,128]{1,0:T(8,128)(2,1)S(1)}, bf16[512,128]{1,0:T(8,128)(2,1)S(1)}, u32[]{:S(2)}, u32[]{:S(2)}) collective-permute-start(bf16[512,128]{1,0:T(8,128)(2,1)S(1)} %bitcast.24), channel_id=1, source_target_pairs={{0,120},{8,0},{16,8},{24,16},{32,24},{40,32},{48,40},{56,48},{64,5... | collective-permute-start | bytes 393224 | tf_op jit(solution)/shard_map/ppermute | solution.py:25
  54.3 8.1 %collective-permute-start.2 = (bf16[512,128]{1,0:T(8,128)(2,1)S(1)}, bf16[512,128]{1,0:T(8,128)(2,1)S(1)}, u32[]{:S(2)}, u32[]{:S(2)}) collective-permute-start(bf16[512,128]{1,0:T(8,128)(2,1)S(1)} %bitcast.25), channel_id=1, source_target_pairs={{0,16},{8,24},{16,32},{24,40},{32,48},{40,56},{48,64},{56,72},{64,... | collective-permute-start | bytes 393224 | tf_op jit(solution)/shard_map/ppermute | solution.py:25
  62.4 27.0 %copy-start.1 = (bf16[512,512]{1,0:T(8,128)(2,1)}, bf16[512,512]{1,0:T(8,128)(2,1)S(1)}, u32[]{:S(2)}) copy-start(bf16[512,512]{1,0:T(8,128)(2,1)S(1)} %pad_maximum_fusion.refs_0_) | copy-start | bytes 1572868
  62.4 15.3 %collective-permute-start.3 = (bf16[512,512]{1,0:T(8,128)(2,1)S(1)}, bf16[512,512]{1,0:T(8,128)(2,1)}, u32[]{:S(2)}, u32[]{:S(2)}) collective-permute-start(bf16[512,512]{1,0:T(8,128)(2,1)S(1)} %pad_maximum_fusion.refs_0_), channel_id=1, source_target_pairs={{0,128},{128,256},{256,384},{384,0},{1,129},{129,257},{257,385},{3... | collective-permute-start | bytes 1572872 | tf_op jit(solution)/shard_map/ppermute | solution.py:25
  66.9 22.6 %copy-start.2 = (bf16[512,512]{1,0:T(8,128)(2,1)}, bf16[512,512]{1,0:T(8,128)(2,1)S(1)}, u32[]{:S(2)}) copy-start(bf16[512,512]{1,0:T(8,128)(2,1)S(1)} %bitcast_bitcast_fusion.refs_1_) | copy-start | bytes 1572868
  66.9 12.8 %collective-permute-start.5 = (bf16[512,512]{1,0:T(8,128)(2,1)S(1)}, bf16[512,512]{1,0:T(8,128)(2,1)}, u32[]{:S(2)}, u32[]{:S(2)}) collective-permute-start(bf16[512,512]{1,0:T(8,128)(2,1)S(1)} %bitcast_bitcast_fusion.refs_1_), channel_id=1, source_target_pairs={{0,8},{8,16},{16,24},{24,32},{32,40},{40,48},{48,56},{56,64},{64,7... | collective-permute-start | bytes 1572872 | tf_op jit(solution)/shard_map/ppermute | solution.py:25
  71.5 17.9 %collective-permute-start.7 = (bf16[512,512]{1,0:T(8,128)(2,1)S(1)}, bf16[512,512]{1,0:T(8,128)(2,1)}, u32[]{:S(2)}, u32[]{:S(2)}) collective-permute-start(bf16[512,512]{1,0:T(8,128)(2,1)S(1)} %pad_maximum_fusion.refs_0_), channel_id=1, source_target_pairs={{0,384},{128,0},{256,128},{384,256},{1,385},{129,1},{257,129},{385... | collective-permute-start | bytes 1572872 | tf_op jit(solution)/shard_map/ppermute | solution.py:25
  75.8 13.6 %collective-permute-start.8 = (bf16[512,512]{1,0:T(8,128)(2,1)S(1)}, bf16[512,512]{1,0:T(8,128)(2,1)}, u32[]{:S(2)}, u32[]{:S(2)}) collective-permute-start(bf16[512,512]{1,0:T(8,128)(2,1)S(1)} %bitcast_bitcast_fusion.refs_1_), channel_id=1, source_target_pairs={{0,120},{8,0},{16,8},{24,16},{32,24},{40,32},{48,40},{56,48},{64,5... | collective-permute-start | bytes 1572872 | tf_op jit(solution)/shard_map/ppermute | solution.py:25
  77.7 23.0 %collective-permute-start.4 = (bf16[512,512]{1,0:T(8,128)(2,1)}, bf16[512,512]{1,0:T(8,128)(2,1)}, u32[]{:S(2)}, u32[]{:S(2)}) collective-permute-start(bf16[512,512]{1,0:T(8,128)(2,1)} %collective-permute-done.3.refs_2_), channel_id=1, source_target_pairs={{0,128},{128,256},{256,384},{384,0},{1,129},{129,257},{257,385},{3... | collective-permute-start | bytes 1572872 | tf_op jit(solution)/shard_map/ppermute | solution.py:25
  79.7 21.0 %collective-permute-start.6 = (bf16[512,512]{1,0:T(8,128)(2,1)}, bf16[512,512]{1,0:T(8,128)(2,1)}, u32[]{:S(2)}, u32[]{:S(2)}) collective-permute-start(bf16[512,512]{1,0:T(8,128)(2,1)} %collective-permute-done.5.refs_4_), channel_id=1, source_target_pairs={{0,8},{8,16},{16,24},{24,32},{32,40},{40,48},{48,56},{56,64},{64,7... | collective-permute-start | bytes 1572872 | tf_op jit(solution)/shard_map/ppermute | solution.py:25
Sparse Core Ops, SparseCore 0:
  9.5 63.0 all-gather.1

commit v3 on v2

v3 whole, which is shorter than its diff:
```python
import functools
import jax
import jax.numpy as jnp
from jax import lax
from jax.experimental import pallas as pl
from jax.experimental.pallas import tpu as pltpu
from jax.sharding import Mesh, PartitionSpec as P

TILE = 128
NX, NZ, NY, NC = 4, 16, 4, 2
ZH, ZL = 4, 4
HALF = 32
ROWS = TILE // ZL
STEPS = (0, -1, 1, -2)
BLOCK = 1024
UNROLL = 4
EARLY, LATE = (0, 4, 1, 2, 5, 6), (3, 7)

damping_ratio = 0.1
tiny_value = 1e-06
HI = lax.Precision.HIGHEST
F32 = jnp.float32
BF16 = jnp.bfloat16


def shift(value, axis, step, size):
    return lax.ppermute(value, axis, [(i, (i + step) % size) for i in range(size)])


def spread(value, axis, size):
    copies = jnp.broadcast_to(value[None], (size,) + value.shape)
    return lax.all_to_all(copies, axis, 0, 0, tiled=True)


def exchange(value, axis):
    return lax.all_to_all(value, axis, 0, 0, tiled=True)


def prepare_kernel(place_ref, in_proj, out_proj, targets, picked, in_copy, out_copy):
    x, z = place_ref[0], place_ref[1]
    table = out_proj[...]
    cols = table.shape[0]
    column = lax.broadcasted_iota(jnp.int32, (targets.shape[0], cols), 1) + (x * NZ + z) * cols
    hit = jnp.where(column == targets[...], 1.0, 0.0).astype(BF16)
    picked[...] = jnp.dot(hit, table, preferred_element_type=F32)
    in_copy[...] = in_proj[...]
    out_copy[...] = table


def stat_tile(peak, total, rows):
    lane = lax.broadcasted_iota(jnp.int32, (rows, TILE), 1)
    stat = jnp.where(lane == 0, peak, jnp.where(lane == 1, total, 0.0))
    if rows < TILE:
        stat = jnp.concatenate([stat, jnp.zeros((TILE - rows, TILE), F32)], axis=0)
    return stat.T[0:8, :]


def fetch(js, chunks, head, in_proj, x, z, feat_buf, head_buf, proj_buf, sems):
    waits, late_waits = [], []
    for at, j in enumerate(js):
        step = STEPS[j % len(STEPS)]
        copies = [pltpu.make_async_copy(chunks[at], feat_buf.at[at], sems.at[at, 0])]
        others = []
        if j < len(STEPS):
            xs = (x + step + NX) % NX
            for a in range(ZL):
                zs = (z + STEPS[a] + NZ) % ZL
                copies.append(pltpu.make_async_copy(head.at[xs, :, zs, 0], head_buf.at[at, a], sems.at[at, 1 + a]))
                others.append(pltpu.make_async_copy(in_proj.at[xs, :, zs, 0], proj_buf.at[at, a], sems.at[at, 5 + a]))
        else:
            zs = (z + step + NZ) % ZL
            copies.append(pltpu.make_async_copy(head.at[:, :, zs, 1], head_buf.at[at], sems.at[at, 1]))
            others.append(pltpu.make_async_copy(in_proj.at[:, :, zs, 1], proj_buf.at[at], sems.at[at, 5]))
        for copy in copies:
            copy.start()
        waits.append(copies)
        late_waits += others
    for copy in late_waits:
        copy.start()
    return waits, late_waits


def add_products(waits, feat_buf, head_buf, out, ready=None, then=None):
    count, width = feat_buf.shape[0], feat_buf.shape[2]
    for g in range(0, count, 2):
        for copy in waits[g] + waits[g + 1]:
            copy.wait()
        if g == 0 and ready is not None:
            ready.wait()

        def column_block(n, carry, g=g):
            at = pl.ds(pl.multiple_of(n * BLOCK, BLOCK), BLOCK)
            part = None if g == 0 and ready is None else out[:, at]
            for j in (g, g + 1):
                more = jnp.dot(feat_buf[j], head_buf[j, :, :, :, at].reshape(width, BLOCK), preferred_element_type=F32)
                part = more if part is None else part + more
            out[:, at] = part
            if then is not None and g + 2 == count:
                then(n, at).start()
            return carry

        lax.fori_loop(0, out.shape[1] // BLOCK, column_block, 0)


def project(feat_buf, proj_buf, x, waits):
    own = pl.ds(pl.multiple_of(x * TILE, TILE), TILE)
    for copy in waits:
        copy.wait()
    return sum(
        jnp.dot(feat_buf[j, own, :], proj_buf[j].reshape(feat_buf.shape[2], 64), preferred_element_type=F32)
        for j in range(feat_buf.shape[0])
    )


def first_kernel(place_ref, *refs):
    chunks = refs[: len(EARLY)]
    head, in_proj, acc, proj, feat_buf, head_buf, proj_buf, sems, acc_buf, out_sems = refs[len(EARLY) :]
    x, z = place_ref[0], place_ref[1]
    waits, others = fetch(EARLY, chunks, head, in_proj, x, z, feat_buf, head_buf, proj_buf, sems)

    def store(n, at):
        return pltpu.make_async_copy(acc_buf.at[:, at], acc.at[:, at], out_sems.at[n])

    add_products(waits, feat_buf, head_buf, acc_buf, then=store)
    proj[...] = project(feat_buf, proj_buf, x, others)
    for n in range(acc_buf.shape[1] // BLOCK):
        store(n, pl.ds(n * BLOCK, BLOCK)).wait()


def logits_kernel(place_ref, *refs):
    chunks = refs[: len(LATE)]
    head, in_proj, acc, proj_in, out_proj, picked, packed, proj = refs[len(LATE) : len(LATE) + 8]
    feat_buf, head_buf, proj_buf, sems, logit_buf, in_sem = refs[len(LATE) + 8 :]
    x, z = place_ref[0], place_ref[1]
    waits, others = fetch(LATE, chunks, head, in_proj, x, z, feat_buf, head_buf, proj_buf, sems)
    ready = pltpu.make_async_copy(acc, logit_buf, in_sem)
    ready.start()
    add_products(waits, feat_buf, head_buf, logit_buf, ready=ready)
    proj[...] = proj_in[...] + project(feat_buf, proj_buf, x, others)
    table = out_proj[...]

    def row_block(i, carry):
        rows = pl.ds(pl.multiple_of(i * TILE, TILE), TILE)
        logits = logit_buf[rows, :]
        peak = jnp.max(logits, axis=1, keepdims=True)
        weight = jnp.exp(logits - peak)
        total = jnp.sum(weight, axis=1, keepdims=True)
        part1 = weight.astype(BF16)
        rest = weight - part1.astype(F32)
        part2 = rest.astype(BF16)
        part3 = (rest - part2.astype(F32)).astype(BF16)
        mixed = jnp.dot(part1, table, preferred_element_type=F32)
        mixed += jnp.dot(part2, table, preferred_element_type=F32)
        mixed += jnp.dot(part3, table, preferred_element_type=F32)
        data = jnp.concatenate([mixed, picked[rows, :]], axis=1)
        stat = stat_tile(peak, total, TILE)
        for b in range(ZL):
            packed[i * ZL + b, 0:ROWS, :] = data[b * ROWS : (b + 1) * ROWS, :]
            packed[i * ZL + b, ROWS : ROWS + 8, :] = stat
        return carry

    lax.fori_loop(0, NX, row_block, 0, unroll=UNROLL)


def merge(parts):
    peak = functools.reduce(jnp.maximum, [p for _, p, _ in parts])
    scales = [jnp.exp(p - peak) for _, p, _ in parts]
    total = sum(s * t for s, (_, _, t) in zip(scales, parts))
    mixed = sum(s * data[:, :64] for s, (data, _, _) in zip(scales, parts))
    picked = sum(data[:, 64:] for data, _, _ in parts)
    return mixed, picked, peak, total


def merge_kernel(place_ref, packed, out, turned):
    low = place_ref[1] % ZL
    count = packed.shape[0]
    turned[...] = packed[:, ROWS : ROWS + 8, :].reshape(count * 8, TILE).T
    stat = turned[pl.ds(pl.multiple_of(low * ROWS, ROWS), ROWS), :]
    parts = [(packed[i, 0:ROWS, :], stat[:, 8 * i : 8 * i + 1], stat[:, 8 * i + 1 : 8 * i + 2]) for i in range(count)]
    mixed, picked, peak, total = merge(parts)
    data, stat = jnp.concatenate([mixed, picked], axis=1), stat_tile(peak, total, ROWS)
    for i in range(NZ):
        out[i, 0:ROWS, :] = data
        out[i, ROWS : ROWS + 8, :] = stat


def gram_kernel(place_ref, lengths, packed, proj, out):
    stat = packed[:, ROWS : ROWS + 8, :].reshape(NZ * 8, TILE).T[0:ROWS, :]
    blocks = []
    for b in range(ZL):
        parts = []
        for i in range(ZH):
            at = i * ZL + b
            parts.append((packed[at, 0:ROWS, :], stat[:, 8 * at : 8 * at + 1], stat[:, 8 * at + 1 : 8 * at + 2]))
        mixed, picked, _, total = merge(parts)
        blocks.append(mixed / total - picked)
    length = lengths[place_ref[2]]
    both = jnp.concatenate([jnp.concatenate(blocks, axis=0), proj[...]], axis=1)
    row = lax.broadcasted_iota(jnp.int32, both.shape, 0)
    both = jnp.where(row < length, both, 0.0)
    gram = lax.dot_general(both, both, (((0,), (0,)), ((), ())), precision=HI, preferred_element_type=F32)
    row = lax.broadcasted_iota(jnp.int32, (64, 64), 0)
    col = lax.broadcasted_iota(jnp.int32, (64, 64), 1)
    cov_in = gram[64:128, 64:128]
    root = jnp.sqrt(jnp.full((64, 64), length.astype(F32)))
    data = jnp.concatenate([jnp.where(row <= col, gram[0:64, 0:64], cov_in), gram[0:64, 64:128] / root], axis=1)
    diag = jnp.sum(jnp.where(row == col, cov_in, 0.0), axis=0, keepdims=True)
    diag = jnp.broadcast_to(jnp.concatenate([diag, diag], axis=1), (8, TILE))
    for i in range(out.shape[0]):
        out[i, 0:64, :] = data
        out[i, 64:72, :] = diag


def whiten_kernel(lengths, grams, out):
    total = functools.reduce(jnp.add, [lengths[s] for s in range(lengths.shape[0])]).astype(F32)
    summed = functools.reduce(jnp.add, [grams[d] for d in range(grams.shape[0])]) / total
    row = lax.broadcasted_iota(jnp.int32, (64, TILE), 0)
    lane = lax.broadcasted_iota(jnp.int32, (64, TILE), 1)
    left = lane < 64
    inner = jnp.where(left, lane, lane - 64)
    block = jnp.where(left, summed[0:64, :], 0.0)
    turned = jnp.concatenate([block, jnp.zeros_like(block)], axis=0).T[0:64, :]
    upper, lower = row < inner, row > inner
    cov_out = jnp.where(lower, turned, block)[:, 0:64]
    cov_in = jnp.where(upper, turned, block)[:, 0:64]
    work = jnp.concatenate([cov_out, cov_in], axis=1)
    on_diag = row == inner
    work = jnp.where(on_diag & (lane >= 64), summed[64:65, :], work)
    diag = jnp.where(on_diag, work, 0.0)
    trace_out = jnp.sum(jnp.where(left, diag, 0.0))
    trace_in = jnp.sum(jnp.where(left, 0.0, diag))
    damp = jnp.where(left, damping_ratio * trace_out / 64 + tiny_value, damping_ratio * trace_in / 64 + tiny_value)
    work = work + jnp.where(on_diag, damp, 0.0)
    def column(work, k):
        return jnp.where(left, work[:, k : k + 1], work[:, 64 + k : 65 + k])

    for k in range(0, 64, 2):
        at0, at1 = inner == k, inner == k + 1
        row0, row1 = work[k : k + 1, :], work[k + 1 : k + 2, :]
        col0, col1 = column(work, k), column(work, k + 1)
        p00, p01 = col0[k : k + 1, :], col1[k : k + 1, :]
        p10, p11 = col0[k + 1 : k + 2, :], col1[k + 1 : k + 2, :]
        inv = 1.0 / (p00 * p11 - p01 * p10)
        q00, q01, q10, q11 = p11 * inv, -p01 * inv, -p10 * inv, p00 * inv
        new0, new1 = q00 * row0 + q01 * row1, q10 * row0 + q11 * row1
        new0 = jnp.where(at0[0:1, :], q00, jnp.where(at1[0:1, :], q01, new0))
        new1 = jnp.where(at0[0:1, :], q10, jnp.where(at1[0:1, :], q11, new1))
        body = jnp.where(at0 | at1, 0.0, work) - col0 * new0 - col1 * new1
        work = jnp.where(row == k, new0, jnp.where(row == k + 1, new1, body))
    inv_out, inv_in = work[:, 0:64], work[:, 64:128]
    zero = jnp.zeros((64, 64), F32)
    twice = jnp.concatenate(
        [jnp.concatenate([inv_in, zero], axis=1), jnp.concatenate([zero, inv_in], axis=1)], axis=0
    )
    pairs = []
    for s in range(0, grams.shape[0], 2):
        at = [(q % NX) * (NY * NC) + q // NX for q in (s, s + 1)]
        pairs.append(jnp.concatenate([grams[at[0], 0:64, 64:128], grams[at[1], 0:64, 64:128]], axis=1))
    half = jnp.dot(jnp.concatenate(pairs, axis=0), twice, precision=HI, preferred_element_type=F32)
    half = jnp.concatenate([half[64 * p : 64 * p + 64, :] for p in range(len(pairs))], axis=1)
    full_white = jnp.dot(inv_out, half, precision=HI, preferred_element_type=F32)
    for s in range(grams.shape[0]):
        out[s] = full_white[:, 64 * s : 64 * s + 64].astype(BF16)


def full(shape, dtype=F32):
    return jax.ShapeDtypeStruct(shape, dtype)


VMEM = pl.BlockSpec(memory_space=pltpu.VMEM)
SMEM = pl.BlockSpec(memory_space=pltpu.SMEM)
ANY = pl.BlockSpec(memory_space=pl.ANY)
ZAXIS = ("zh", "zl")


def per_device(hidden, head_weight, in_proj, out_proj, targets, lengths, grad_store):
    token_count, width = hidden.shape
    x = lax.axis_index("x")
    z = lax.axis_index("zh") * ZL + lax.axis_index("zl")
    rows = lax.axis_index("y") * NC + lax.axis_index("c")
    place = jnp.stack([x, z, rows * NX + x]).astype(jnp.int32)
    cols = head_weight.shape[1]
    head = lax.all_gather(head_weight, ("y", "c"), axis=0, tiled=True)
    picked, in_rows, out_rows = pl.pallas_call(
        prepare_kernel,
        out_shape=(full((token_count, 64)), full(in_proj.shape, BF16), full(out_proj.shape, BF16)),
        in_specs=[SMEM, VMEM, VMEM, VMEM],
        out_specs=(VMEM, VMEM, VMEM),
        name="prepare",
    )(place, in_proj, out_proj, targets[:, None])
    strided = spread(hidden.T, "zh", ZH)
    strided, picked, in_rows, out_rows = lax.optimization_barrier((strided, picked, in_rows, out_rows))
    size = NX * ZH * HALF
    a_own = strided[:, :HALF, :].reshape(ZH * HALF, token_count).T
    a_parts = [a_own] + [shift(a_own, ZAXIS, -s, NZ) for s in STEPS[1:]]
    b_own = spread(strided[:, HALF:, :].reshape(ZH * HALF, token_count), "x", NX)
    b_own = b_own.reshape(size, token_count).T
    a_own = jnp.concatenate(a_parts, axis=1)
    b_back, b_next = shift(b_own, ZAXIS, 1, NZ), shift(b_own, ZAXIS, -1, NZ)
    a_back, a_next = shift(a_own, "x", 1, NX), shift(a_own, "x", -1, NX)
    b_far, a_far = shift(b_back, ZAXIS, 1, NZ), shift(a_back, "x", 1, NX)
    chunks = [a_own, a_back, a_next, a_far, b_own, b_back, b_next, b_far]
    head = head.reshape(NX, ZH, ZL, 2, HALF, cols)
    in_rows = in_rows.reshape(NX, ZH, ZL, 2, HALF, 64)

    def buffers(count):
        return [
            pltpu.VMEM((count, token_count, size), BF16),
            pltpu.VMEM((count, NX, ZH, HALF, cols), BF16),
            pltpu.VMEM((count, NX, ZH, HALF, 64), BF16),
            pltpu.SemaphoreType.DMA((count, 1 + 2 * ZL)),
            pltpu.VMEM((token_count, cols), F32),
        ]

    acc, proj = pl.pallas_call(
        first_kernel,
        out_shape=(full((token_count, cols)), full((TILE, 64))),
        in_specs=[SMEM] + [ANY] * (len(EARLY) + 2),
        out_specs=(ANY, VMEM),
        scratch_shapes=buffers(len(EARLY)) + [pltpu.SemaphoreType.DMA((cols // BLOCK,))],
        name="logits_first",
    )(place, *[chunks[j] for j in EARLY], head, in_rows)
    packed, proj = pl.pallas_call(
        logits_kernel,
        out_shape=(full((NX * ZL, ROWS + 8, TILE)), full((TILE, 64))),
        in_specs=[SMEM] + [ANY] * (len(LATE) + 3) + [VMEM] * 3,
        out_specs=(VMEM, VMEM),
        scratch_shapes=buffers(len(LATE)) + [pltpu.SemaphoreType.DMA(())],
        name="logits_last",
    )(place, *[chunks[j] for j in LATE], head, in_rows, acc, proj, out_rows, picked)
    merged = pl.pallas_call(
        merge_kernel,
        out_shape=full((NZ, ROWS + 8, TILE)),
        in_specs=[SMEM, VMEM],
        out_specs=VMEM,
        scratch_shapes=[pltpu.VMEM((TILE, TILE), F32)],
        name="merge",
    )(place, exchange(packed, ("x", "zl")))
    seqs = NX * NY * NC
    gram = pl.pallas_call(
        gram_kernel,
        out_shape=full((seqs, 72, TILE)),
        in_specs=[SMEM, SMEM, VMEM, VMEM],
        out_specs=VMEM,
        name="gram",
    )(place, lengths, exchange(merged, ZAXIS), proj)
    grams = exchange(gram, ("x", "y", "c"))
    whitened = pl.pallas_call(
        whiten_kernel,
        out_shape=full((seqs, 64, 64), BF16),
        in_specs=[SMEM, VMEM],
        out_specs=VMEM,
        name="whiten",
    )(lengths, grams)
    whitened = whitened.reshape(seqs, 64 * 64)
    return jnp.dot(whitened, grad_store.T, preferred_element_type=F32)


def solution(mesh):
    grid = Mesh(mesh.devices.reshape(NX, ZH, ZL, NY, NC), ("x", "zh", "zl", "y", "c"))
    return jax.shard_map(
        per_device,
        mesh=grid,
        in_specs=(
            P(("y", "c"), ("x", "zh", "zl")),
            P(("y", "c"), ("x", "zh", "zl")),
            P(),
            P(("x", "zh", "zl"), None),
            P(("y", "c")),
            P(),
            P(("x", "zh", "zl", "y", "c"), None),
        ),
        out_specs=P(None, ("x", "zh", "zl", "y", "c")),
        check_vma=False,
    )
```

time: 204 us -> 193 us (0.946)
  blocking collectives: 95.6 us -> 68.4 us
  starting transfers between devices: 40.3 us -> 51.6 us
  waiting for transfers between devices: 4.85 us -> 15.2 us
  Pallas kernels: 35.3 us -> 32.4 us
    all_to_all x4 -> x3, blocking collectives: 95.6 us -> 68.4 us  [exchange(): return lax.all_to_all(value, axis, 0, 0, tiled=True)]
    all_to_all x1 -> x2, starting transfers between devices: 4.15 us -> 19.8 us  [spread(): return lax.all_to_all(copies, axis, 0, 0, tiled=True)]
    all_to_all x1 -> x2, waiting for transfers between devices: 0.01 us -> 6.95 us  [spread(): return lax.all_to_all(copies, axis, 0, 0, tiled=True)]
    ppermute x9, starting transfers between devices: 36.1 us -> 31.8 us  [shift(): lax.ppermute(value, axis, [(i, (i + step) % size) for i in range(size)])]
    ppermute x9, waiting for transfers between devices: 4.13 us -> 7.55 us  [shift(): lax.ppermute(value, axis, [(i, (i + step) % size) for i in range(size)])]
    pallas_call x5 -> x6, Pallas kernels: 35.3 us -> 32.4 us  [the longest x1 8.6 us: per_device(): pl.pallas_call(first_kernel, out_shape=(full((token_count, cols)), full((...]
  transfers between devices with their start and end apart: 11 -> 12, of which waited for: 2 -> 5; matrix products, arithmetic and copies ran while one was open for 4% -> 4% of each run, Pallas kernels for 6% -> 6%
where the time goes in v3:
time: 193 us; the launch traced here: 192 us
  blocking collectives  68.4 us (35%)
  starting transfers between devices  51.6 us (27%)
  Pallas kernels  32.4 us (17%)
  waiting for transfers between devices  15.2 us (8%)
  between operations  13.6 us (7%)
  local copies, waits for them, and re-layouts  9.27 us (5%)
    all_to_all x3, blocking collectives, exchange(): return lax.all_to_all(value, axis, 0, 0, tiled=True)  68.4 us
    ppermute x9, starting transfers between devices, shift(): lax.ppermute(value, axis, [(i, (i + step) % size) for i in range(size)])  31.8 us
    all_to_all x2, starting transfers between devices, spread(): return lax.all_to_all(copies, axis, 0, 0, tiled=True)  19.8 us
    pallas_call x1, Pallas kernels, per_device(): pl.pallas_call(first_kernel, out_shape=(full((token_count, cols)), full((...  8.6 us
    pallas_call x1, Pallas kernels, per_device(): pl.pallas_call(whiten_kernel, out_shape=full((seqs, 64, 64), BF16), in_sp...  8.1 us
    ppermute x9, waiting for transfers between devices, shift(): lax.ppermute(value, axis, [(i, (i + step) % size) for i in range(size)])  7.55 us
    pallas_call x1, Pallas kernels, per_device(): pl.pallas_call(logits_kernel, out_shape=(full((NX * ZL, ROWS + 8, TILE)),...  7.27 us
    all_to_all x2, waiting for transfers between devices, spread(): return lax.all_to_all(copies, axis, 0, 0, tiled=True)  6.95 us
  transfers between devices with their start and end apart: 12, of which 5 were waited for; matrix products, arithmetic and copies ran while one was open for 4% of the time, Pallas kernels for 6%

profile of v3, /device:TPU:1, one launch (start us, length us, event | category | flops | bytes accessed | tf_op | source)
XLA Modules:
  0.0 192.4 jit_solution(603939530045232408)
XLA Ops:
  6.5 0.0 copy-start
  6.5 0.0 all-gather.2.cloned.1.call-start
  6.6 0.7 all-gather.2.cloned.1.call-update
  7.3 1.6 broadcast_in_dim.16
  8.9 15.6 %all-to-all-start = ((bf16[4,64,512]{2,1,0:T(8,128)(2,1)}), bf16[4,64,512]{2,1,0:T(8,128)(2,1)S(1)}, u32[]{:S(2)}, u32[]{:S(2)}) async-start(bf16[4,64,512]{2,1,0:T(8,128)(2,1)} %broadcast_in_dim.16), calls=%async_computation | async-start | bytes 524288 | tf_op jit(solution)/shard_map/all_to_all | solution.py:32
  24.5 1.4 copy.16.in_proj
  25.9 0.8 copy.17.out_proj
  26.8 0.9 copy.18.targets
  27.6 0.6 pad_add_fusion.place_ref
  28.2 3.1 %prepare.1 = (f32[512,64]{1,0:T(8,128)}, bf16[4096,64]{1,0:T(8,128)(2,1)}, bf16[1024,64]{1,0:T(8,128)(2,1)}) custom-call(s32[3]{0:T(128)} %pad_add_fusion.place_ref, bf16[4096,64]{1,0:T(8,128)(2,1)} %copy.16.in_proj, bf16[1024,64]{1,0:T(8,128)(2,1)} %copy.17.out_proj, s32[512,1]{1,0:T(8,128)} %copy.18.targets), custom_call_target="tpu_custom_call" | custom-call | tf_op jit(solution)/shard_map/prepare/pallas_call | solution.py:284
  31.4 7.0 %all-to-all-done = bf16[4,64,512]{2,1,0:T(8,128)(2,1)S(1)} async-done(((bf16[4,64,512]{2,1,0:T(8,128)(2,1)}), bf16[4,64,512]{2,1,0:T(8,128)(2,1)S(1)}, u32[]{:S(2)}, u32[]{:S(2)}) %all-to-all-start) | async-done | bytes 262176 | tf_op jit(solution)/shard_map/all_to_all | solution.py:32
  38.3 0.1 copy.20
  38.4 0.9 broadcast_in_dim.19
  39.3 4.1 %all-to-all-start.1 = ((bf16[4,128,512]{1,2,0:T(8,128)(2,1)}), bf16[4,128,512]{1,2,0:T(8,128)(2,1)}, u32[]{:S(2)}, u32[]{:S(2)}) async-start(bf16[4,128,512]{1,2,0:T(8,128)(2,1)} %broadcast_in_dim.19), calls=%async_computation.1 | async-start | bytes 1048576 | tf_op jit(solution)/shard_map/all_to_all | solution.py:32
  43.5 0.1 copy.19
  43.6 8.4 %collective-permute-start = (bf16[512,128]{1,0:T(8,128)(2,1)S(1)}, bf16[512,128]{1,0:T(8,128)(2,1)S(1)}, u32[]{:S(2)}, u32[]{:S(2)}) collective-permute-start(bf16[512,128]{1,0:T(8,128)(2,1)S(1)} %bitcast.25), channel_id=1, source_target_pairs={{0,8},{8,16},{16,24},{24,32},{32,40},{40,48},{48,56},{56,64},{64,7... | collective-permute-start | bytes 393224 | tf_op jit(solution)/shard_map/ppermute | solution.py:27
  52.0 1.9 collective-permute-start.1
  54.0 3.8 %collective-permute-start.2 = (bf16[512,128]{1,0:T(8,128)(2,1)S(1)}, bf16[512,128]{1,0:T(8,128)(2,1)S(1)}, u32[]{:S(2)}, u32[]{:S(2)}) collective-permute-start(bf16[512,128]{1,0:T(8,128)(2,1)S(1)} %bitcast.27), channel_id=1, source_target_pairs={{0,16},{8,24},{16,32},{24,40},{32,48},{40,56},{48,64},{56,72},{64,... | collective-permute-start | bytes 393224 | tf_op jit(solution)/shard_map/ppermute | solution.py:27
  57.7 0.0 collective-permute-done
  57.7 0.4 collective-permute-done.1
  58.1 4.7 %collective-permute-done.2 = bf16[512,128]{1,0:T(8,128)(2,1)S(1)} collective-permute-done((bf16[512,128]{1,0:T(8,128)(2,1)S(1)}, bf16[512,128]{1,0:T(8,128)(2,1)S(1)}, u32[]{:S(2)}, u32[]{:S(2)}) %collective-permute-start.2) | collective-permute-done | bytes 131104 | tf_op jit(solution)/shard_map/ppermute | solution.py:27
  62.8 0.1 pad_maximum_fusion.refs_0_
  62.9 0.0 copy-start.1
  62.9 3.3 %collective-permute-start.3 = (bf16[512,512]{1,0:T(8,128)(2,1)S(1)}, bf16[512,512]{1,0:T(8,128)(2,1)}, u32[]{:S(2)}, u32[]{:S(2)}) collective-permute-start(bf16[512,512]{1,0:T(8,128)(2,1)S(1)} %pad_maximum_fusion.refs_0_), channel_id=1, source_target_pairs={{0,128},{128,256},{256,384},{384,0},{1,129},{129,257},{257,385},{3... | collective-permute-start | bytes 1572872 | tf_op jit(solution)/shard_map/ppermute | solution.py:27
  66.2 0.0 all-to-all-done.1
  66.3 1.1 bitcast_bitcast_fusion.refs_1_
  67.4 3.8 %collective-permute-start.5 = (bf16[512,512]{1,0:T(8,128)(2,1)S(1)}, bf16[512,512]{1,0:T(8,128)(2,1)}, u32[]{:S(2)}, u32[]{:S(2)}) collective-permute-start(bf16[512,512]{1,0:T(8,128)(2,1)S(1)} %bitcast_bitcast_fusion.refs_1_), channel_id=1, source_target_pairs={{0,8},{8,16},{16,24},{24,32},{32,40},{40,48},{48,56},{56,64},{64,7... | collective-permute-start | bytes 1572872 | tf_op jit(solution)/shard_map/ppermute | solution.py:27
  71.2 3.2 %collective-permute-start.7 = (bf16[512,512]{1,0:T(8,128)(2,1)S(1)}, bf16[512,512]{1,0:T(8,128)(2,1)S(1)}, u32[]{:S(2)}, u32[]{:S(2)}) collective-permute-start(bf16[512,512]{1,0:T(8,128)(2,1)S(1)} %pad_maximum_fusion.refs_0_), channel_id=1, source_target_pairs={{0,384},{128,0},{256,128},{384,256},{1,385},{129,1},{257,129},{385... | collective-permute-start | bytes 1572872 | tf_op jit(solution)/shard_map/ppermute | solution.py:27
  74.4 2.7 %collective-permute-start.8 = (bf16[512,512]{1,0:T(8,128)(2,1)S(1)}, bf16[512,512]{1,0:T(8,128)(2,1)}, u32[]{:S(2)}, u32[]{:S(2)}) collective-permute-start(bf16[512,512]{1,0:T(8,128)(2,1)S(1)} %bitcast_bitcast_fusion.refs_1_), channel_id=1, source_target_pairs={{0,120},{8,0},{16,8},{24,16},{32,24},{40,32},{48,40},{56,48},{64,5... | collective-permute-start | bytes 1572872 | tf_op jit(solution)/shard_map/ppermute | solution.py:27
  77.1 0.0 collective-permute-done.3.refs_2_
  77.1 2.1 %collective-permute-start.4 = (bf16[512,512]{1,0:T(8,128)(2,1)}, bf16[512,512]{1,0:T(8,128)(2,1)}, u32[]{:S(2)}, u32[]{:S(2)}) collective-permute-start(bf16[512,512]{1,0:T(8,128)(2,1)} %collective-permute-done.3.refs_2_), channel_id=1, source_target_pairs={{0,128},{128,256},{256,384},{384,0},{1,129},{129,257},{257,385},{3... | collective-permute-start | bytes 1572872 | tf_op jit(solution)/shard_map/ppermute | solution.py:27
  79.2 0.2 collective-permute-done.5.refs_4_
  79.4 2.6 %collective-permute-start.6 = (bf16[512,512]{1,0:T(8,128)(2,1)}, bf16[512,512]{1,0:T(8,128)(2,1)}, u32[]{:S(2)}, u32[]{:S(2)}) collective-permute-start(bf16[512,512]{1,0:T(8,128)(2,1)} %collective-permute-done.5.refs_4_), channel_id=1, source_target_pairs={{0,8},{8,16},{16,24},{24,32},{32,40},{40,48},{48,56},{56,64},{64,7... | collective-permute-start | bytes 1572872 | tf_op jit(solution)/shard_map/ppermute | solution.py:27
  82.0 0.0 collective-permute-done.7.refs_3_
  82.0 0.8 copy-done.4
  82.8 2.2 %collective-permute-done.8.refs_5_ = bf16[512,512]{1,0:T(8,128)(2,1)} collective-permute-done((bf16[512,512]{1,0:T(8,128)(2,1)S(1)}, bf16[512,512]{1,0:T(8,128)(2,1)}, u32[]{:S(2)}, u32[]{:S(2)}) %collective-permute-start.8) | collective-permute-done | bytes 524320 | tf_op jit(solution)/shard_map/ppermute | solution.py:27
  85.1 8.6 %logits_first.1 = (f32[512,1024]{1,0:T(8,128)}, f32[128,64]{1,0:T(8,128)}) custom-call(s32[3]{0:T(128)} %pad_add_fusion.place_ref, bf16[512,512]{1,0:T(8,128)(2,1)} %copy-done.1, bf16[512,512]{1,0:T(8,128)(2,1)} %copy-done.2, bf16[512,512]{1,0:T(8,128)(2,1)} %collective-permute-done.3.refs_2_, bf16[512,512]{1,0:T(8,128)(2,1)} %copy-done.4, ...), custom_call_target="tpu_custom_call" | custom-call | tf_op jit(solution)/shard_map/logits_first/pallas_call | solution.py:315
  93.7 0.0 collective-permute-done.4.refs_0_
  93.7 0.0 collective-permute-done.6.refs_1_
  93.7 7.3 %logits_last.1 = (f32[16,40,128]{2,1,0:T(8,128)}, f32[128,64]{1,0:T(8,128)}) custom-call(s32[3]{0:T(128)} %pad_add_fusion.place_ref, bf16[512,512]{1,0:T(8,128)(2,1)} %collective-permute-done.4.refs_0_, bf16[512,512]{1,0:T(8,128)(2,1)} %collective-permute-done.6.refs_1_, bf16[4,4,4,2,32,1024]{5,4,3,2,1,0:T(8,128)(2,1)} %bitcast.20, ...), custom_call_target="tpu_custom_call" | custom-call | tf_op jit(solution)/shard_map/logits_last/pallas_call | solution.py:323
  101.0 13.9 %all_to_all.25.packed = f32[16,40,128]{2,1,0:T(8,128)} all-to-all(f32[16,40,128]{2,1,0:T(8,128)} %get-tuple-element.25), channel_id=1, replica_groups=mesh['x'=4,'zh'=4,'zl'=4,'y'=4,'c'=2] {'x','zl'}, dimensions={0} | all-to-all | bytes 655360 | tf_op jit(solution)/shard_map/all_to_all | solution.py:36
  114.9 2.3 %merge.1 = f32[16,40,128]{2,1,0:T(8,128)} custom-call(s32[3]{0:T(128)} %pad_add_fusion.place_ref, f32[16,40,128]{2,1,0:T(8,128)} %all_to_all.25.packed), custom_call_target="tpu_custom_call" | custom-call | tf_op jit(solution)/shard_map/merge/pallas_call | solution.py:331
  117.2 19.9 %all_to_all.26.packed = f32[16,40,128]{2,1,0:T(8,128)} all-to-all(f32[16,40,128]{2,1,0:T(8,128)} %merge.1), channel_id=1, replica_groups=mesh['x'=4,'zh'=4,'zl'=4,'y'=4,'c'=2] {'zh','zl'}, dimensions={0} | all-to-all | bytes 655360 | tf_op jit(solution)/shard_map/all_to_all | solution.py:36
  137.1 2.9 %gram.1 = f32[32,72,128]{2,1,0:T(8,128)} custom-call(s32[3]{0:T(128)} %pad_add_fusion.place_ref, s32[32]{0:T(128)} %lengths.3, f32[16,40,128]{2,1,0:T(8,128)} %all_to_all.26.packed, f32[128,64]{1,0:T(8,128)} %get-tuple-element.26.proj), custom_call_target="tpu_custom_call" | custom-call | tf_op jit(solution)/shard_map/gram/pallas_call | solution.py:340
  140.0 34.6 %all_to_all.27.grams = f32[32,72,128]{2,1,0:T(8,128)} all-to-all(f32[32,72,128]{2,1,0:T(8,128)} %gram.1), channel_id=1, replica_groups=mesh['x'=4,'zh'=4,'zl'=4,'y'=4,'c'=2] {'x','y','c'}, dimensions={0} | all-to-all | bytes 2359296 | tf_op jit(solution)/shard_map/all_to_all | solution.py:36
  174.6 8.1 %whiten.1 = bf16[32,64,64]{2,1,0:T(8,128)(2,1)} custom-call(s32[32]{0:T(128)} %lengths.3, f32[32,72,128]{2,1,0:T(8,128)} %all_to_all.27.grams), custom_call_target="tpu_custom_call" | custom-call | tf_op jit(solution)/shard_map/whiten/pallas_call | solution.py:348
  182.7 1.5 reshape.21
  184.2 1.4 fusion.1
  (13 shorter events, 0.0 us)
Async XLA Ops:
  6.5 177.6 %copy-start = (bf16[256,4096]{1,0:T(8,128)(2,1)S(1)}, bf16[256,4096]{1,0:T(8,128)(2,1)}, u32[]{:S(2)}) copy-start(bf16[256,4096]{1,0:T(8,128)(2,1)} %param.13) | copy-start | bytes 6291460
  6.5 18.0 %copy-start.3 = (bf16[4096,64]{0,1:T(8,128)(2,1)S(1)}, bf16[4096,64]{0,1:T(8,128)(2,1)}, u32[]{:S(2)}) copy-start(bf16[4096,64]{0,1:T(8,128)(2,1)} %param.9) | copy-start | bytes 1572868
  6.5 19.4 %copy-start.5 = (bf16[1024,64]{0,1:T(8,128)(2,1)S(1)}, bf16[1024,64]{0,1:T(8,128)(2,1)}, u32[]{:S(2)}) copy-start(bf16[1024,64]{0,1:T(8,128)(2,1)} %param.10) | copy-start | bytes 393220
  6.5 20.2 %copy-start.6 = (s32[512]{0:T(512)S(1)}, s32[512]{0:T(512)}, u32[]{:S(2)}) copy-start(s32[512]{0:T(512)} %param.11) | copy-start | bytes 6148
  6.5 78.5 %all-gather.2.cloned.1.call-start = ((), (), s32[]{:S(2)}) async-start(), calls=%async_computation.5 | async-start | bytes 9437184 | tf_op jit(solution)/shard_map/all_gather | solution.py:283
  8.9 29.4 %all-to-all-start = ((bf16[4,64,512]{2,1,0:T(8,128)(2,1)}), bf16[4,64,512]{2,1,0:T(8,128)(2,1)S(1)}, u32[]{:S(2)}, u32[]{:S(2)}) async-start(bf16[4,64,512]{2,1,0:T(8,128)(2,1)} %broadcast_in_dim.16), calls=%async_computation | async-start | bytes 524288 | tf_op jit(solution)/shard_map/all_to_all | solution.py:32
  39.3 26.9 %all-to-all-start.1 = ((bf16[4,128,512]{1,2,0:T(8,128)(2,1)}), bf16[4,128,512]{1,2,0:T(8,128)(2,1)}, u32[]{:S(2)}, u32[]{:S(2)}) async-start(bf16[4,128,512]{1,2,0:T(8,128)(2,1)} %broadcast_in_dim.19), calls=%async_computation.1 | async-start | bytes 1048576 | tf_op jit(solution)/shard_map/all_to_all | solution.py:32
  43.6 14.2 %collective-permute-start = (bf16[512,128]{1,0:T(8,128)(2,1)S(1)}, bf16[512,128]{1,0:T(8,128)(2,1)S(1)}, u32[]{:S(2)}, u32[]{:S(2)}) collective-permute-start(bf16[512,128]{1,0:T(8,128)(2,1)S(1)} %bitcast.25), channel_id=1, source_target_pairs={{0,8},{8,16},{16,24},{24,32},{32,40},{40,48},{48,56},{56,64},{64,7... | collective-permute-start | bytes 393224 | tf_op jit(solution)/shard_map/ppermute | solution.py:27
  52.0 6.1 %collective-permute-start.1 = (bf16[512,128]{1,0:T(8,128)(2,1)S(1)}, bf16[512,128]{1,0:T(8,128)(2,1)S(1)}, u32[]{:S(2)}, u32[]{:S(2)}) collective-permute-start(bf16[512,128]{1,0:T(8,128)(2,1)S(1)} %bitcast.26), channel_id=1, source_target_pairs={{0,120},{8,0},{16,8},{24,16},{32,24},{40,32},{48,40},{56,48},{64,5... | collective-permute-start | bytes 393224 | tf_op jit(solution)/shard_map/ppermute | solution.py:27
  54.0 8.9 %collective-permute-start.2 = (bf16[512,128]{1,0:T(8,128)(2,1)S(1)}, bf16[512,128]{1,0:T(8,128)(2,1)S(1)}, u32[]{:S(2)}, u32[]{:S(2)}) collective-permute-start(bf16[512,128]{1,0:T(8,128)(2,1)S(1)} %bitcast.27), channel_id=1, source_target_pairs={{0,16},{8,24},{16,32},{24,40},{32,48},{40,56},{48,64},{56,72},{64,... | collective-permute-start | bytes 393224 | tf_op jit(solution)/shard_map/ppermute | solution.py:27
  62.9 22.1 %copy-start.1 = (bf16[512,512]{1,0:T(8,128)(2,1)}, bf16[512,512]{1,0:T(8,128)(2,1)S(1)}, u32[]{:S(2)}) copy-start(bf16[512,512]{1,0:T(8,128)(2,1)S(1)} %pad_maximum_fusion.refs_0_) | copy-start | bytes 1572868
  62.9 14.2 %collective-permute-start.3 = (bf16[512,512]{1,0:T(8,128)(2,1)S(1)}, bf16[512,512]{1,0:T(8,128)(2,1)}, u32[]{:S(2)}, u32[]{:S(2)}) collective-permute-start(bf16[512,512]{1,0:T(8,128)(2,1)S(1)} %pad_maximum_fusion.refs_0_), channel_id=1, source_target_pairs={{0,128},{128,256},{256,384},{384,0},{1,129},{129,257},{257,385},{3... | collective-permute-start | bytes 1572872 | tf_op jit(solution)/shard_map/ppermute | solution.py:27
  67.4 17.7 %copy-start.2 = (bf16[512,512]{1,0:T(8,128)(2,1)}, bf16[512,512]{1,0:T(8,128)(2,1)S(1)}, u32[]{:S(2)}) copy-start(bf16[512,512]{1,0:T(8,128)(2,1)S(1)} %bitcast_bitcast_fusion.refs_1_) | copy-start | bytes 1572868
  67.4 12.0 %collective-permute-start.5 = (bf16[512,512]{1,0:T(8,128)(2,1)S(1)}, bf16[512,512]{1,0:T(8,128)(2,1)}, u32[]{:S(2)}, u32[]{:S(2)}) collective-permute-start(bf16[512,512]{1,0:T(8,128)(2,1)S(1)} %bitcast_bitcast_fusion.refs_1_), channel_id=1, source_target_pairs={{0,8},{8,16},{16,24},{24,32},{32,40},{40,48},{48,56},{56,64},{64,7... | collective-permute-start | bytes 1572872 | tf_op jit(solution)/shard_map/ppermute | solution.py:27
  71.2 10.8 %collective-permute-start.7 = (bf16[512,512]{1,0:T(8,128)(2,1)S(1)}, bf16[512,512]{1,0:T(8,128)(2,1)S(1)}, u32[]{:S(2)}, u32[]{:S(2)}) collective-permute-start(bf16[512,512]{1,0:T(8,128)(2,1)S(1)} %pad_maximum_fusion.refs_0_), channel_id=1, source_target_pairs={{0,384},{128,0},{256,128},{384,256},{1,385},{129,1},{257,129},{385... | collective-permute-start | bytes 1572872 | tf_op jit(solution)/shard_map/ppermute | solution.py:27
  74.4 10.7 %collective-permute-start.8 = (bf16[512,512]{1,0:T(8,128)(2,1)S(1)}, bf16[512,512]{1,0:T(8,128)(2,1)}, u32[]{:S(2)}, u32[]{:S(2)}) collective-permute-start(bf16[512,512]{1,0:T(8,128)(2,1)S(1)} %bitcast_bitcast_fusion.refs_1_), channel_id=1, source_target_pairs={{0,120},{8,0},{16,8},{24,16},{32,24},{40,32},{48,40},{56,48},{64,5... | collective-permute-start | bytes 1572872 | tf_op jit(solution)/shard_map/ppermute | solution.py:27
  77.1 16.6 %collective-permute-start.4 = (bf16[512,512]{1,0:T(8,128)(2,1)}, bf16[512,512]{1,0:T(8,128)(2,1)}, u32[]{:S(2)}, u32[]{:S(2)}) collective-permute-start(bf16[512,512]{1,0:T(8,128)(2,1)} %collective-permute-done.3.refs_2_), channel_id=1, source_target_pairs={{0,128},{128,256},{256,384},{384,0},{1,129},{129,257},{257,385},{3... | collective-permute-start | bytes 1572872 | tf_op jit(solution)/shard_map/ppermute | solution.py:27
  79.4 14.3 %collective-permute-start.6 = (bf16[512,512]{1,0:T(8,128)(2,1)}, bf16[512,512]{1,0:T(8,128)(2,1)}, u32[]{:S(2)}, u32[]{:S(2)}) collective-permute-start(bf16[512,512]{1,0:T(8,128)(2,1)} %collective-permute-done.5.refs_4_), channel_id=1, source_target_pairs={{0,8},{8,16},{16,24},{24,32},{32,40},{40,48},{48,56},{56,64},{64,7... | collective-permute-start | bytes 1572872 | tf_op jit(solution)/shard_map/ppermute | solution.py:27
  82.0 0.8 copy-start.4
Sparse Core Ops, SparseCore 0:
  9.5 63.0 all-gather.1

commit v4 on v3

--- a/solution.py
+++ b/solution.py
@@ -211,9 +211,19 @@
         out[i, 64:72, :] = diag
 
 
-def whiten_kernel(lengths, grams, out):
+def split_dot(a, b):
+    a_top, b_top = a.astype(BF16), b.astype(BF16)
+    a_rest, b_rest = (a - a_top.astype(F32)).astype(BF16), (b - b_top.astype(F32)).astype(BF16)
+    out = jnp.dot(a_top, b_top, preferred_element_type=F32)
+    out += jnp.dot(a_top, b_rest, preferred_element_type=F32)
+    return out + jnp.dot(a_rest, b_top, preferred_element_type=F32)
+
+
+def whiten_kernel(place_ref, lengths, mine, theirs, out):
     total = functools.reduce(jnp.add, [lengths[s] for s in range(lengths.shape[0])]).astype(F32)
-    summed = functools.reduce(jnp.add, [grams[d] for d in range(grams.shape[0])]) / total
+    count = mine.shape[0]
+    summed = functools.reduce(jnp.add, [mine[d] for d in range(count)])
+    summed = (summed + functools.reduce(jnp.add, [theirs[d] for d in range(count)])) / total
     row = lax.broadcasted_iota(jnp.int32, (64, TILE), 0)
     lane = lax.broadcasted_iota(jnp.int32, (64, TILE), 1)
     left = lane < 64
@@ -253,14 +263,18 @@
         [jnp.concatenate([inv_in, zero], axis=1), jnp.concatenate([zero, inv_in], axis=1)], axis=0
     )
     pairs = []
-    for s in range(0, grams.shape[0], 2):
-        at = [(q % NX) * (NY * NC) + q // NX for q in (s, s + 1)]
-        pairs.append(jnp.concatenate([grams[at[0], 0:64, 64:128], grams[at[1], 0:64, 64:128]], axis=1))
-    half = jnp.dot(jnp.concatenate(pairs, axis=0), twice, precision=HI, preferred_element_type=F32)
+    for grams in (mine, theirs):
+        for d in range(0, count, 2):
+            pairs.append(jnp.concatenate([grams[d, 0:64, 64:128], grams[d + 1, 0:64, 64:128]], axis=1))
+    half = split_dot(jnp.concatenate(pairs, axis=0), twice)
     half = jnp.concatenate([half[64 * p : 64 * p + 64, :] for p in range(len(pairs))], axis=1)
-    full_white = jnp.dot(inv_out, half, precision=HI, preferred_element_type=F32)
-    for s in range(grams.shape[0]):
-        out[s] = full_white[:, 64 * s : 64 * s + 64].astype(BF16)
+    white = split_dot(inv_out, half)
+    core = place_ref[3]
+    for at in range(2 * count):
+        d = at % count
+        owner = core if at < count else 1 - core
+        seq = (d % NY * NC + owner) * NX + d // NY
+        out[seq] = white[:, 64 * at : 64 * at + 64].astype(BF16)
 
 
 def full(shape, dtype=F32):
@@ -277,8 +291,9 @@
     token_count, width = hidden.shape
     x = lax.axis_index("x")
     z = lax.axis_index("zh") * ZL + lax.axis_index("zl")
-    rows = lax.axis_index("y") * NC + lax.axis_index("c")
-    place = jnp.stack([x, z, rows * NX + x]).astype(jnp.int32)
+    core = lax.axis_index("c")
+    rows = lax.axis_index("y") * NC + core
+    place = jnp.stack([x, z, rows * NX + x, core]).astype(jnp.int32)
     cols = head_weight.shape[1]
     head = lax.all_gather(head_weight, ("y", "c"), axis=0, tiled=True)
     picked, in_rows, out_rows = pl.pallas_call(
@@ -339,19 +354,20 @@
     seqs = NX * NY * NC
     gram = pl.pallas_call(
         gram_kernel,
-        out_shape=full((seqs, 72, TILE)),
+        out_shape=full((NX * NY, 72, TILE)),
         in_specs=[SMEM, SMEM, VMEM, VMEM],
         out_specs=VMEM,
         name="gram",
     )(place, lengths, exchange(merged, ZAXIS), proj)
-    grams = exchange(gram, ("x", "y", "c"))
+    mine = exchange(gram, ("x", "y"))
+    theirs = lax.ppermute(mine, "c", [(0, 1), (1, 0)])
     whitened = pl.pallas_call(
         whiten_kernel,
         out_shape=full((seqs, 64, 64), BF16),
-        in_specs=[SMEM, VMEM],
+        in_specs=[SMEM, SMEM, VMEM, VMEM],
         out_specs=VMEM,
         name="whiten",
-    )(lengths, grams)
+    )(place, lengths, mine, theirs)
     whitened = whitened.reshape(seqs, 64 * 64)
     return jnp.dot(whitened, grad_store.T, preferred_element_type=F32)
 

time: 193 us -> 188 us (0.974)
  blocking collectives: 68.4 us -> 48.1 us
  starting transfers between devices: 51.6 us -> 65.3 us
    all_to_all x3, blocking collectives: 68.4 us -> 48.1 us  [exchange(): return lax.all_to_all(value, axis, 0, 0, tiled=True)]
    ppermute x0 -> x1, starting transfers between devices: none -> 13.7 us  [per_device(): theirs = lax.ppermute(mine, 'c', [(0, 1), (1, 0)])]
    unnamed x16 -> x20, local copies, waits for them, and re-layouts: 3.08 us -> 3.87 us
  transfers between devices with their start and end apart: 12 -> 13, of which waited for: 5 -> 6; matrix products, arithmetic and copies ran while one was open for 4% -> 4% of each run, Pallas kernels for 6% -> 6%
where the time goes in v4:
time: 188 us; the launch traced here: 187 us
  starting transfers between devices  65.3 us (35%)
  blocking collectives  48.1 us (26%)
  Pallas kernels  31.2 us (17%)
  waiting for transfers between devices  16.6 us (9%)
  between operations  13.6 us (7%)
  local copies, waits for them, and re-layouts  10.1 us (5%)
    all_to_all x3, blocking collectives, exchange(): return lax.all_to_all(value, axis, 0, 0, tiled=True)  48.1 us
    ppermute x9, starting transfers between devices, shift(): lax.ppermute(value, axis, [(i, (i + step) % size) for i in range(size)])  31.8 us
    all_to_all x2, starting transfers between devices, spread(): return lax.all_to_all(copies, axis, 0, 0, tiled=True)  19.8 us
    ppermute x1, starting transfers between devices, per_device(): theirs = lax.ppermute(mine, 'c', [(0, 1), (1, 0)])  13.7 us
    pallas_call x1, Pallas kernels, per_device(): pl.pallas_call(first_kernel, out_shape=(full((token_count, cols)), full((...  8.54 us
    ppermute x9, waiting for transfers between devices, shift(): lax.ppermute(value, axis, [(i, (i + step) % size) for i in range(size)])  7.54 us
    pallas_call x1, Pallas kernels, per_device(): pl.pallas_call(logits_kernel, out_shape=(full((NX * ZL, ROWS + 8, TILE)),...  7.28 us
    pallas_call x1, Pallas kernels, per_device(): pl.pallas_call(whiten_kernel, out_shape=full((seqs, 64, 64), BF16), in_sp...  7.25 us
  transfers between devices with their start and end apart: 13, of which 6 were waited for; matrix products, arithmetic and copies ran while one was open for 4% of the time, Pallas kernels for 6%

profile of v4, /device:TPU:1, one launch (start us, length us, event | category | flops | bytes accessed | tf_op | source)
XLA Modules:
  0.0 187.0 jit_solution(16270709838025094627)
XLA Ops:
  6.5 0.0 all-gather.2.cloned.1.call-start
  6.6 0.7 all-gather.2.cloned.1.call-update
  7.3 1.6 broadcast_in_dim.16
  8.9 15.6 %all-to-all-start = ((bf16[4,64,512]{2,1,0:T(8,128)(2,1)}), bf16[4,64,512]{2,1,0:T(8,128)(2,1)S(1)}, u32[]{:S(2)}, u32[]{:S(2)}) async-start(bf16[4,64,512]{2,1,0:T(8,128)(2,1)} %broadcast_in_dim.16), calls=%async_computation | async-start | bytes 524288 | tf_op jit(solution)/shard_map/all_to_all | solution.py:32
  24.5 1.4 copy.16.in_proj
  25.9 0.8 copy.17.out_proj
  26.7 0.9 copy.18.targets
  27.6 0.6 pad_add_fusion.place_ref
  28.2 3.1 %prepare.1 = (f32[512,64]{1,0:T(8,128)}, bf16[4096,64]{1,0:T(8,128)(2,1)}, bf16[1024,64]{1,0:T(8,128)(2,1)}) custom-call(s32[4]{0:T(128)} %pad_add_fusion.place_ref, bf16[4096,64]{1,0:T(8,128)(2,1)} %copy.16.in_proj, bf16[1024,64]{1,0:T(8,128)(2,1)} %copy.17.out_proj, s32[512,1]{1,0:T(8,128)} %copy.18.targets), custom_call_target="tpu_custom_call" | custom-call | tf_op jit(solution)/shard_map/prepare/pallas_call | solution.py:299
  31.4 6.9 %all-to-all-done = bf16[4,64,512]{2,1,0:T(8,128)(2,1)S(1)} async-done(((bf16[4,64,512]{2,1,0:T(8,128)(2,1)}), bf16[4,64,512]{2,1,0:T(8,128)(2,1)S(1)}, u32[]{:S(2)}, u32[]{:S(2)}) %all-to-all-start) | async-done | bytes 262176 | tf_op jit(solution)/shard_map/all_to_all | solution.py:32
  38.3 0.1 copy.20
  38.4 0.9 broadcast_in_dim.19
  39.3 4.1 %all-to-all-start.1 = ((bf16[4,128,512]{1,2,0:T(8,128)(2,1)}), bf16[4,128,512]{1,2,0:T(8,128)(2,1)}, u32[]{:S(2)}, u32[]{:S(2)}) async-start(bf16[4,128,512]{1,2,0:T(8,128)(2,1)} %broadcast_in_dim.19), calls=%async_computation.1 | async-start | bytes 1048576 | tf_op jit(solution)/shard_map/all_to_all | solution.py:32
  43.5 0.1 copy.19
  43.6 8.4 %collective-permute-start = (bf16[512,128]{1,0:T(8,128)(2,1)S(1)}, bf16[512,128]{1,0:T(8,128)(2,1)S(1)}, u32[]{:S(2)}, u32[]{:S(2)}) collective-permute-start(bf16[512,128]{1,0:T(8,128)(2,1)S(1)} %bitcast.26), channel_id=1, source_target_pairs={{0,8},{8,16},{16,24},{24,32},{32,40},{40,48},{48,56},{56,64},{64,7... | collective-permute-start | bytes 393224 | tf_op jit(solution)/shard_map/ppermute | solution.py:27
  52.0 1.9 %collective-permute-start.1 = (bf16[512,128]{1,0:T(8,128)(2,1)S(1)}, bf16[512,128]{1,0:T(8,128)(2,1)S(1)}, u32[]{:S(2)}, u32[]{:S(2)}) collective-permute-start(bf16[512,128]{1,0:T(8,128)(2,1)S(1)} %bitcast.27), channel_id=1, source_target_pairs={{0,120},{8,0},{16,8},{24,16},{32,24},{40,32},{48,40},{56,48},{64,5... | collective-permute-start | bytes 393224 | tf_op jit(solution)/shard_map/ppermute | solution.py:27
  54.0 3.8 %collective-permute-start.2 = (bf16[512,128]{1,0:T(8,128)(2,1)S(1)}, bf16[512,128]{1,0:T(8,128)(2,1)S(1)}, u32[]{:S(2)}, u32[]{:S(2)}) collective-permute-start(bf16[512,128]{1,0:T(8,128)(2,1)S(1)} %bitcast.28), channel_id=1, source_target_pairs={{0,16},{8,24},{16,32},{24,40},{32,48},{40,56},{48,64},{56,72},{64,... | collective-permute-start | bytes 393224 | tf_op jit(solution)/shard_map/ppermute | solution.py:27
  57.7 0.0 collective-permute-done
  57.7 0.4 collective-permute-done.1
  58.1 4.7 %collective-permute-done.2 = bf16[512,128]{1,0:T(8,128)(2,1)S(1)} collective-permute-done((bf16[512,128]{1,0:T(8,128)(2,1)S(1)}, bf16[512,128]{1,0:T(8,128)(2,1)S(1)}, u32[]{:S(2)}, u32[]{:S(2)}) %collective-permute-start.2) | collective-permute-done | bytes 131104 | tf_op jit(solution)/shard_map/ppermute | solution.py:27
  62.8 0.1 pad_maximum_fusion.refs_0_
  62.9 3.3 %collective-permute-start.3 = (bf16[512,512]{1,0:T(8,128)(2,1)S(1)}, bf16[512,512]{1,0:T(8,128)(2,1)}, u32[]{:S(2)}, u32[]{:S(2)}) collective-permute-start(bf16[512,512]{1,0:T(8,128)(2,1)S(1)} %pad_maximum_fusion.refs_0_), channel_id=1, source_target_pairs={{0,128},{128,256},{256,384},{384,0},{1,129},{129,257},{257,385},{3... | collective-permute-start | bytes 1572872 | tf_op jit(solution)/shard_map/ppermute | solution.py:27
  66.3 0.0 all-to-all-done.1
  66.3 1.1 bitcast_bitcast_fusion.refs_1_
  67.4 3.8 %collective-permute-start.5 = (bf16[512,512]{1,0:T(8,128)(2,1)S(1)}, bf16[512,512]{1,0:T(8,128)(2,1)}, u32[]{:S(2)}, u32[]{:S(2)}) collective-permute-start(bf16[512,512]{1,0:T(8,128)(2,1)S(1)} %bitcast_bitcast_fusion.refs_1_), channel_id=1, source_target_pairs={{0,8},{8,16},{16,24},{24,32},{32,40},{40,48},{48,56},{56,64},{64,7... | collective-permute-start | bytes 1572872 | tf_op jit(solution)/shard_map/ppermute | solution.py:27
  71.2 3.2 %collective-permute-start.7 = (bf16[512,512]{1,0:T(8,128)(2,1)S(1)}, bf16[512,512]{1,0:T(8,128)(2,1)S(1)}, u32[]{:S(2)}, u32[]{:S(2)}) collective-permute-start(bf16[512,512]{1,0:T(8,128)(2,1)S(1)} %pad_maximum_fusion.refs_0_), channel_id=1, source_target_pairs={{0,384},{128,0},{256,128},{384,256},{1,385},{129,1},{257,129},{385... | collective-permute-start | bytes 1572872 | tf_op jit(solution)/shard_map/ppermute | solution.py:27
  74.4 2.7 %collective-permute-start.8 = (bf16[512,512]{1,0:T(8,128)(2,1)S(1)}, bf16[512,512]{1,0:T(8,128)(2,1)}, u32[]{:S(2)}, u32[]{:S(2)}) collective-permute-start(bf16[512,512]{1,0:T(8,128)(2,1)S(1)} %bitcast_bitcast_fusion.refs_1_), channel_id=1, source_target_pairs={{0,120},{8,0},{16,8},{24,16},{32,24},{40,32},{48,40},{56,48},{64,5... | collective-permute-start | bytes 1572872 | tf_op jit(solution)/shard_map/ppermute | solution.py:27
  77.1 0.0 collective-permute-done.3.refs_2_
  77.1 2.1 %collective-permute-start.4 = (bf16[512,512]{1,0:T(8,128)(2,1)}, bf16[512,512]{1,0:T(8,128)(2,1)}, u32[]{:S(2)}, u32[]{:S(2)}) collective-permute-start(bf16[512,512]{1,0:T(8,128)(2,1)} %collective-permute-done.3.refs_2_), channel_id=1, source_target_pairs={{0,128},{128,256},{256,384},{384,0},{1,129},{129,257},{257,385},{3... | collective-permute-start | bytes 1572872 | tf_op jit(solution)/shard_map/ppermute | solution.py:27
  79.2 0.2 collective-permute-done.5.refs_4_
  79.4 2.6 %collective-permute-start.6 = (bf16[512,512]{1,0:T(8,128)(2,1)}, bf16[512,512]{1,0:T(8,128)(2,1)}, u32[]{:S(2)}, u32[]{:S(2)}) collective-permute-start(bf16[512,512]{1,0:T(8,128)(2,1)} %collective-permute-done.5.refs_4_), channel_id=1, source_target_pairs={{0,8},{8,16},{16,24},{24,32},{32,40},{40,48},{48,56},{56,64},{64,7... | collective-permute-start | bytes 1572872 | tf_op jit(solution)/shard_map/ppermute | solution.py:27
  82.0 0.0 collective-permute-done.7.refs_3_
  82.0 0.8 copy-done.6
  82.8 2.2 %collective-permute-done.8.refs_5_ = bf16[512,512]{1,0:T(8,128)(2,1)} collective-permute-done((bf16[512,512]{1,0:T(8,128)(2,1)S(1)}, bf16[512,512]{1,0:T(8,128)(2,1)}, u32[]{:S(2)}, u32[]{:S(2)}) %collective-permute-start.8) | collective-permute-done | bytes 524320 | tf_op jit(solution)/shard_map/ppermute | solution.py:27
  85.0 8.5 %logits_first.1 = (f32[512,1024]{1,0:T(8,128)}, f32[128,64]{1,0:T(8,128)}) custom-call(s32[4]{0:T(128)} %pad_add_fusion.place_ref, bf16[512,512]{1,0:T(8,128)(2,1)} %copy-done.2, bf16[512,512]{1,0:T(8,128)(2,1)} %copy-done.3, bf16[512,512]{1,0:T(8,128)(2,1)} %collective-permute-done.3.refs_2_, bf16[512,512]{1,0:T(8,128)(2,1)} %copy-done.6, ...), custom_call_target="tpu_custom_call" | custom-call | tf_op jit(solution)/shard_map/logits_first/pallas_call | solution.py:330
  93.6 0.0 collective-permute-done.6.refs_1_
  93.6 7.3 %logits_last.1 = (f32[16,40,128]{2,1,0:T(8,128)}, f32[128,64]{1,0:T(8,128)}) custom-call(s32[4]{0:T(128)} %pad_add_fusion.place_ref, bf16[512,512]{1,0:T(8,128)(2,1)} %collective-permute-done.4.refs_0_, bf16[512,512]{1,0:T(8,128)(2,1)} %collective-permute-done.6.refs_1_, bf16[4,4,4,2,32,1024]{5,4,3,2,1,0:T(8,128)(2,1)} %bitcast.21, ...), custom_call_target="tpu_custom_call" | custom-call | tf_op jit(solution)/shard_map/logits_last/pallas_call | solution.py:338
  100.9 13.9 %all_to_all.25.packed = f32[16,40,128]{2,1,0:T(8,128)} all-to-all(f32[16,40,128]{2,1,0:T(8,128)} %get-tuple-element.25), channel_id=1, replica_groups=mesh['x'=4,'zh'=4,'zl'=4,'y'=4,'c'=2] {'x','zl'}, dimensions={0} | all-to-all | bytes 655360 | tf_op jit(solution)/shard_map/all_to_all | solution.py:36
  114.8 2.3 %merge.1 = f32[16,40,128]{2,1,0:T(8,128)} custom-call(s32[4]{0:T(128)} %pad_add_fusion.place_ref, f32[16,40,128]{2,1,0:T(8,128)} %all_to_all.25.packed), custom_call_target="tpu_custom_call" | custom-call | tf_op jit(solution)/shard_map/merge/pallas_call | solution.py:346
  117.2 19.8 %all_to_all.26.packed = f32[16,40,128]{2,1,0:T(8,128)} all-to-all(f32[16,40,128]{2,1,0:T(8,128)} %merge.1), channel_id=1, replica_groups=mesh['x'=4,'zh'=4,'zl'=4,'y'=4,'c'=2] {'zh','zl'}, dimensions={0} | all-to-all | bytes 655360 | tf_op jit(solution)/shard_map/all_to_all | solution.py:36
  137.0 2.7 %gram.1 = f32[16,72,128]{2,1,0:T(8,128)} custom-call(s32[4]{0:T(128)} %pad_add_fusion.place_ref, s32[32]{0:T(128)} %lengths.3, f32[16,40,128]{2,1,0:T(8,128)} %all_to_all.26.packed, f32[128,64]{1,0:T(8,128)} %get-tuple-element.26.proj), custom_call_target="tpu_custom_call" | custom-call | tf_op jit(solution)/shard_map/gram/pallas_call | solution.py:355
  139.7 14.4 %all_to_all.27.mine = f32[16,72,128]{2,1,0:T(8,128)S(1)} all-to-all(f32[16,72,128]{2,1,0:T(8,128)} %gram.1), channel_id=1, replica_groups=mesh['x'=4,'zh'=4,'zl'=4,'y'=4,'c'=2] {'x','y'}, dimensions={0} | all-to-all | bytes 1179648 | tf_op jit(solution)/shard_map/all_to_all | solution.py:36
  154.1 13.7 %collective-permute-start.9 = (f32[16,72,128]{2,1,0:T(8,128)S(1)}, f32[16,72,128]{2,1,0:T(8,128)S(1)}, u32[]{:S(2)}, u32[]{:S(2)}) collective-permute-start(f32[16,72,128]{2,1,0:T(8,128)S(1)} %all_to_all.27.mine), channel_id=1, source_target_pairs={{0,1},{1,0},{2,3},{3,2},{4,5},{5,4},{6,7},{7,6},{8,9},{9,8},{10,11... | collective-permute-start | bytes 1769480 | tf_op jit(solution)/shard_map/ppermute | solution.py:363
  167.8 1.4 collective-permute-done.9.theirs
  169.2 0.8 copy-done.4
  170.1 7.3 %whiten.1 = bf16[32,64,64]{2,1,0:T(8,128)(2,1)} custom-call(s32[4]{0:T(128)} %pad_add_fusion.place_ref, s32[32]{0:T(128)} %lengths.3, f32[16,72,128]{2,1,0:T(8,128)} %copy-done.1, f32[16,72,128]{2,1,0:T(8,128)} %copy-done.4), custom_call_target="tpu_custom_call" | custom-call | tf_op jit(solution)/shard_map/whiten/pallas_call | solution.py:364
  177.3 1.5 reshape.21
  178.8 1.4 fusion.1
  (19 shorter events, 0.1 us)
Async XLA Ops:
  6.5 172.3 %copy-start = (bf16[256,4096]{1,0:T(8,128)(2,1)S(1)}, bf16[256,4096]{1,0:T(8,128)(2,1)}, u32[]{:S(2)}) copy-start(bf16[256,4096]{1,0:T(8,128)(2,1)} %param.13) | copy-start | bytes 6291460
  6.5 18.0 %copy-start.5 = (bf16[4096,64]{0,1:T(8,128)(2,1)S(1)}, bf16[4096,64]{0,1:T(8,128)(2,1)}, u32[]{:S(2)}) copy-start(bf16[4096,64]{0,1:T(8,128)(2,1)} %param.9) | copy-start | bytes 1572868
  6.5 19.4 %copy-start.7 = (bf16[1024,64]{0,1:T(8,128)(2,1)S(1)}, bf16[1024,64]{0,1:T(8,128)(2,1)}, u32[]{:S(2)}) copy-start(bf16[1024,64]{0,1:T(8,128)(2,1)} %param.10) | copy-start | bytes 393220
  6.5 20.2 %copy-start.8 = (s32[512]{0:T(512)S(1)}, s32[512]{0:T(512)}, u32[]{:S(2)}) copy-start(s32[512]{0:T(512)} %param.11) | copy-start | bytes 6148
  6.5 78.5 %all-gather.2.cloned.1.call-start = ((), (), s32[]{:S(2)}) async-start(), calls=%async_computation.5 | async-start | bytes 9437184 | tf_op jit(solution)/shard_map/all_gather | solution.py:298
  8.9 29.4 %all-to-all-start = ((bf16[4,64,512]{2,1,0:T(8,128)(2,1)}), bf16[4,64,512]{2,1,0:T(8,128)(2,1)S(1)}, u32[]{:S(2)}, u32[]{:S(2)}) async-start(bf16[4,64,512]{2,1,0:T(8,128)(2,1)} %broadcast_in_dim.16), calls=%async_computation | async-start | bytes 524288 | tf_op jit(solution)/shard_map/all_to_all | solution.py:32
  39.3 26.9 %all-to-all-start.1 = ((bf16[4,128,512]{1,2,0:T(8,128)(2,1)}), bf16[4,128,512]{1,2,0:T(8,128)(2,1)}, u32[]{:S(2)}, u32[]{:S(2)}) async-start(bf16[4,128,512]{1,2,0:T(8,128)(2,1)} %broadcast_in_dim.19), calls=%async_computation.1 | async-start | bytes 1048576 | tf_op jit(solution)/shard_map/all_to_all | solution.py:32
  43.6 14.2 %collective-permute-start = (bf16[512,128]{1,0:T(8,128)(2,1)S(1)}, bf16[512,128]{1,0:T(8,128)(2,1)S(1)}, u32[]{:S(2)}, u32[]{:S(2)}) collective-permute-start(bf16[512,128]{1,0:T(8,128)(2,1)S(1)} %bitcast.26), channel_id=1, source_target_pairs={{0,8},{8,16},{16,24},{24,32},{32,40},{40,48},{48,56},{56,64},{64,7... | collective-permute-start | bytes 393224 | tf_op jit(solution)/shard_map/ppermute | solution.py:27
  52.0 6.1 %collective-permute-start.1 = (bf16[512,128]{1,0:T(8,128)(2,1)S(1)}, bf16[512,128]{1,0:T(8,128)(2,1)S(1)}, u32[]{:S(2)}, u32[]{:S(2)}) collective-permute-start(bf16[512,128]{1,0:T(8,128)(2,1)S(1)} %bitcast.27), channel_id=1, source_target_pairs={{0,120},{8,0},{16,8},{24,16},{32,24},{40,32},{48,40},{56,48},{64,5... | collective-permute-start | bytes 393224 | tf_op jit(solution)/shard_map/ppermute | solution.py:27
  54.0 8.9 %collective-permute-start.2 = (bf16[512,128]{1,0:T(8,128)(2,1)S(1)}, bf16[512,128]{1,0:T(8,128)(2,1)S(1)}, u32[]{:S(2)}, u32[]{:S(2)}) collective-permute-start(bf16[512,128]{1,0:T(8,128)(2,1)S(1)} %bitcast.28), channel_id=1, source_target_pairs={{0,16},{8,24},{16,32},{24,40},{32,48},{40,56},{48,64},{56,72},{64,... | collective-permute-start | bytes 393224 | tf_op jit(solution)/shard_map/ppermute | solution.py:27
  62.9 22.1 %copy-start.2 = (bf16[512,512]{1,0:T(8,128)(2,1)}, bf16[512,512]{1,0:T(8,128)(2,1)S(1)}, u32[]{:S(2)}) copy-start(bf16[512,512]{1,0:T(8,128)(2,1)S(1)} %pad_maximum_fusion.refs_0_) | copy-start | bytes 1572868
  62.9 14.2 %collective-permute-start.3 = (bf16[512,512]{1,0:T(8,128)(2,1)S(1)}, bf16[512,512]{1,0:T(8,128)(2,1)}, u32[]{:S(2)}, u32[]{:S(2)}) collective-permute-start(bf16[512,512]{1,0:T(8,128)(2,1)S(1)} %pad_maximum_fusion.refs_0_), channel_id=1, source_target_pairs={{0,128},{128,256},{256,384},{384,0},{1,129},{129,257},{257,385},{3... | collective-permute-start | bytes 1572872 | tf_op jit(solution)/shard_map/ppermute | solution.py:27
  67.4 17.7 %copy-start.3 = (bf16[512,512]{1,0:T(8,128)(2,1)}, bf16[512,512]{1,0:T(8,128)(2,1)S(1)}, u32[]{:S(2)}) copy-start(bf16[512,512]{1,0:T(8,128)(2,1)S(1)} %bitcast_bitcast_fusion.refs_1_) | copy-start | bytes 1572868
  67.4 12.0 %collective-permute-start.5 = (bf16[512,512]{1,0:T(8,128)(2,1)S(1)}, bf16[512,512]{1,0:T(8,128)(2,1)}, u32[]{:S(2)}, u32[]{:S(2)}) collective-permute-start(bf16[512,512]{1,0:T(8,128)(2,1)S(1)} %bitcast_bitcast_fusion.refs_1_), channel_id=1, source_target_pairs={{0,8},{8,16},{16,24},{24,32},{32,40},{40,48},{48,56},{56,64},{64,7... | collective-permute-start | bytes 1572872 | tf_op jit(solution)/shard_map/ppermute | solution.py:27
  71.2 10.8 %collective-permute-start.7 = (bf16[512,512]{1,0:T(8,128)(2,1)S(1)}, bf16[512,512]{1,0:T(8,128)(2,1)S(1)}, u32[]{:S(2)}, u32[]{:S(2)}) collective-permute-start(bf16[512,512]{1,0:T(8,128)(2,1)S(1)} %pad_maximum_fusion.refs_0_), channel_id=1, source_target_pairs={{0,384},{128,0},{256,128},{384,256},{1,385},{129,1},{257,129},{385... | collective-permute-start | bytes 1572872 | tf_op jit(solution)/shard_map/ppermute | solution.py:27
  74.4 10.7 %collective-permute-start.8 = (bf16[512,512]{1,0:T(8,128)(2,1)S(1)}, bf16[512,512]{1,0:T(8,128)(2,1)}, u32[]{:S(2)}, u32[]{:S(2)}) collective-permute-start(bf16[512,512]{1,0:T(8,128)(2,1)S(1)} %bitcast_bitcast_fusion.refs_1_), channel_id=1, source_target_pairs={{0,120},{8,0},{16,8},{24,16},{32,24},{40,32},{48,40},{56,48},{64,5... | collective-permute-start | bytes 1572872 | tf_op jit(solution)/shard_map/ppermute | solution.py:27
  77.1 16.5 %collective-permute-start.4 = (bf16[512,512]{1,0:T(8,128)(2,1)}, bf16[512,512]{1,0:T(8,128)(2,1)}, u32[]{:S(2)}, u32[]{:S(2)}) collective-permute-start(bf16[512,512]{1,0:T(8,128)(2,1)} %collective-permute-done.3.refs_2_), channel_id=1, source_target_pairs={{0,128},{128,256},{256,384},{384,0},{1,129},{129,257},{257,385},{3... | collective-permute-start | bytes 1572872 | tf_op jit(solution)/shard_map/ppermute | solution.py:27
  79.4 14.2 %collective-permute-start.6 = (bf16[512,512]{1,0:T(8,128)(2,1)}, bf16[512,512]{1,0:T(8,128)(2,1)}, u32[]{:S(2)}, u32[]{:S(2)}) collective-permute-start(bf16[512,512]{1,0:T(8,128)(2,1)} %collective-permute-done.5.refs_4_), channel_id=1, source_target_pairs={{0,8},{8,16},{16,24},{24,32},{32,40},{40,48},{48,56},{56,64},{64,7... | collective-permute-start | bytes 1572872 | tf_op jit(solution)/shard_map/ppermute | solution.py:27
  82.0 0.8 copy-start.6
  154.1 15.2 %copy-start.1 = (f32[16,72,128]{2,1,0:T(8,128)}, f32[16,72,128]{2,1,0:T(8,128)S(1)}, u32[]{:S(2)}) copy-start(f32[16,72,128]{2,1,0:T(8,128)S(1)} %all_to_all.27.mine) | copy-start | bytes 1769476
  154.1 15.2 %collective-permute-start.9 = (f32[16,72,128]{2,1,0:T(8,128)S(1)}, f32[16,72,128]{2,1,0:T(8,128)S(1)}, u32[]{:S(2)}, u32[]{:S(2)}) collective-permute-start(f32[16,72,128]{2,1,0:T(8,128)S(1)} %all_to_all.27.mine), channel_id=1, source_target_pairs={{0,1},{1,0},{2,3},{3,2},{4,5},{5,4},{6,7},{7,6},{8,9},{9,8},{10,11... | collective-permute-start | bytes 1769480 | tf_op jit(solution)/shard_map/ppermute | solution.py:363
  169.2 0.8 copy-start.4
Sparse Core Ops, SparseCore 0:
  9.5 63.0 all-gather.1

commit v5 on v4

--- a/solution.py
+++ b/solution.py
@@ -61,16 +61,13 @@
         step = STEPS[j % len(STEPS)]
         copies = [pltpu.make_async_copy(chunks[at], feat_buf.at[at], sems.at[at, 0])]
         others = []
-        if j < len(STEPS):
-            xs = (x + step + NX) % NX
-            for a in range(ZL):
-                zs = (z + STEPS[a] + NZ) % ZL
-                copies.append(pltpu.make_async_copy(head.at[xs, :, zs, 0], head_buf.at[at, a], sems.at[at, 1 + a]))
-                others.append(pltpu.make_async_copy(in_proj.at[xs, :, zs, 0], proj_buf.at[at, a], sems.at[at, 5 + a]))
-        else:
-            zs = (z + step + NZ) % ZL
-            copies.append(pltpu.make_async_copy(head.at[:, :, zs, 1], head_buf.at[at], sems.at[at, 1]))
-            others.append(pltpu.make_async_copy(in_proj.at[:, :, zs, 1], proj_buf.at[at], sems.at[at, 5]))
+        for a in range(4):
+            if j < len(STEPS):
+                xs, zs, half = (x + step + NX) % NX, a, 0
+            else:
+                xs, zs, half = (x + STEPS[a] + NX) % NX, (z + step + NZ) % ZL, 1
+            copies.append(pltpu.make_async_copy(head.at[xs, :, zs, half], head_buf.at[at, a], sems.at[at, 1 + a]))
+            others.append(pltpu.make_async_copy(in_proj.at[xs, :, zs, half], proj_buf.at[at, a], sems.at[at, 5 + a]))
         for copy in copies:
             copy.start()
         waits.append(copies)
@@ -306,11 +303,10 @@
     strided = spread(hidden.T, "zh", ZH)
     strided, picked, in_rows, out_rows = lax.optimization_barrier((strided, picked, in_rows, out_rows))
     size = NX * ZH * HALF
-    a_own = strided[:, :HALF, :].reshape(ZH * HALF, token_count).T
-    a_parts = [a_own] + [shift(a_own, ZAXIS, -s, NZ) for s in STEPS[1:]]
-    b_own = spread(strided[:, HALF:, :].reshape(ZH * HALF, token_count), "x", NX)
-    b_own = b_own.reshape(size, token_count).T
-    a_own = jnp.concatenate(a_parts, axis=1)
+    a_own = spread(strided[:, :HALF, :].reshape(ZH * HALF, token_count), "zl", ZL)
+    a_own = a_own.reshape(size, token_count).T
+    b_part = strided[:, HALF:, :].reshape(ZH * HALF, token_count).T
+    b_own = jnp.concatenate([b_part] + [shift(b_part, "x", -s, NX) for s in STEPS[1:]], axis=1)
     b_back, b_next = shift(b_own, ZAXIS, 1, NZ), shift(b_own, ZAXIS, -1, NZ)
     a_back, a_next = shift(a_own, "x", 1, NX), shift(a_own, "x", -1, NX)
     b_far, a_far = shift(b_back, ZAXIS, 1, NZ), shift(a_back, "x", 1, NX)

time: 188 us -> 185 us (0.984)
  blocking collectives: 48.1 us -> 45.5 us
  waiting for transfers between devices: 16.6 us -> 14.3 us
    all_to_all x2, starting transfers between devices: 19.8 us -> 23.8 us  [spread(): return lax.all_to_all(copies, axis, 0, 0, tiled=True)]
    all_to_all x3, blocking collectives: 48.1 us -> 45.5 us  [exchange(): return lax.all_to_all(value, axis, 0, 0, tiled=True)]
    ppermute x9, waiting for transfers between devices: 7.54 us -> 5.21 us  [shift(): lax.ppermute(value, axis, [(i, (i + step) % size) for i in range(size)])]
  transfers between devices with their start and end apart: 13 -> 13, of which waited for: 6 -> 5; matrix products, arithmetic and copies ran while one was open for 4% -> 4% of each run, Pallas kernels for 6% -> 6%
where the time goes in v5:
time: 185 us; the launch traced here: 183 us
  starting transfers between devices  66.3 us (36%)
  blocking collectives  45.5 us (25%)
  Pallas kernels  31.2 us (17%)
  waiting for transfers between devices  14.3 us (8%)
  between operations  13.6 us (7%)
  local copies, waits for them, and re-layouts  10.1 us (5%)
    all_to_all x3, blocking collectives, exchange(): return lax.all_to_all(value, axis, 0, 0, tiled=True)  45.5 us
    ppermute x9, starting transfers between devices, shift(): lax.ppermute(value, axis, [(i, (i + step) % size) for i in range(size)])  30.1 us
    all_to_all x2, starting transfers between devices, spread(): return lax.all_to_all(copies, axis, 0, 0, tiled=True)  23.8 us
    ppermute x1, starting transfers between devices, per_device(): theirs = lax.ppermute(mine, 'c', [(0, 1), (1, 0)])  12.4 us
    pallas_call x1, Pallas kernels, per_device(): pl.pallas_call(first_kernel, out_shape=(full((token_count, cols)), full((...  8.51 us
    pallas_call x1, Pallas kernels, per_device(): pl.pallas_call(logits_kernel, out_shape=(full((NX * ZL, ROWS + 8, TILE)),...  7.28 us
    pallas_call x1, Pallas kernels, per_device(): pl.pallas_call(whiten_kernel, out_shape=full((seqs, 64, 64), BF16), in_sp...  7.25 us
    all_to_all x2, waiting for transfers between devices, spread(): return lax.all_to_all(copies, axis, 0, 0, tiled=True)  6.93 us
  transfers between devices with their start and end apart: 13, of which 5 were waited for; matrix products, arithmetic and copies ran while one was open for 4% of the time, Pallas kernels for 6%

profile of v5, /device:TPU:1, one launch (start us, length us, event | category | flops | bytes accessed | tf_op | source)
XLA Modules:
  0.0 183.1 jit_solution(3104911483222450785)
XLA Ops:
  6.5 0.0 all-gather.2.cloned.1.call-start
  6.6 0.7 all-gather.2.cloned.1.call-update
  7.3 1.6 broadcast_in_dim.16
  8.9 15.6 %all-to-all-start = ((bf16[4,64,512]{2,1,0:T(8,128)(2,1)}), bf16[4,64,512]{2,1,0:T(8,128)(2,1)S(1)}, u32[]{:S(2)}, u32[]{:S(2)}) async-start(bf16[4,64,512]{2,1,0:T(8,128)(2,1)} %broadcast_in_dim.16), calls=%async_computation | async-start | bytes 524288 | tf_op jit(solution)/shard_map/all_to_all | solution.py:32
  24.5 1.4 copy.16.in_proj
  25.9 0.8 copy.17.out_proj
  26.7 0.9 copy.18.targets
  27.6 0.6 pad_add_fusion.place_ref
  28.2 3.1 %prepare.1 = (f32[512,64]{1,0:T(8,128)}, bf16[4096,64]{1,0:T(8,128)(2,1)}, bf16[1024,64]{1,0:T(8,128)(2,1)}) custom-call(s32[4]{0:T(128)} %pad_add_fusion.place_ref, bf16[4096,64]{1,0:T(8,128)(2,1)} %copy.16.in_proj, bf16[1024,64]{1,0:T(8,128)(2,1)} %copy.17.out_proj, s32[512,1]{1,0:T(8,128)} %copy.18.targets), custom_call_target="tpu_custom_call" | custom-call | tf_op jit(solution)/shard_map/prepare/pallas_call | solution.py:296
  31.4 6.9 %all-to-all-done = bf16[4,64,512]{2,1,0:T(8,128)(2,1)S(1)} async-done(((bf16[4,64,512]{2,1,0:T(8,128)(2,1)}), bf16[4,64,512]{2,1,0:T(8,128)(2,1)S(1)}, u32[]{:S(2)}, u32[]{:S(2)}) %all-to-all-start) | async-done | bytes 262176 | tf_op jit(solution)/shard_map/all_to_all | solution.py:32
  38.3 0.1 copy.19
  38.4 0.9 broadcast_in_dim.19
  39.3 8.2 %all-to-all-start.1 = ((bf16[4,128,512]{1,2,0:T(8,128)(2,1)}), bf16[4,128,512]{1,2,0:T(8,128)(2,1)}, u32[]{:S(2)}, u32[]{:S(2)}) async-start(bf16[4,128,512]{1,2,0:T(8,128)(2,1)} %broadcast_in_dim.19), calls=%async_computation.1 | async-start | bytes 1048576 | tf_op jit(solution)/shard_map/all_to_all | solution.py:32
  47.5 0.1 copy.21
  47.6 3.1 %collective-permute-start.2 = (bf16[512,128]{1,0:T(8,128)(2,1)S(1)}, bf16[512,128]{1,0:T(8,128)(2,1)S(1)}, u32[]{:S(2)}, u32[]{:S(2)}) collective-permute-start(bf16[512,128]{1,0:T(8,128)(2,1)S(1)} %bitcast.26), channel_id=1, source_target_pairs={{0,128},{128,256},{256,384},{384,0},{1,129},{129,257},{257,385},{3... | collective-permute-start | bytes 393224 | tf_op jit(solution)/shard_map/ppermute | solution.py:27
  50.8 3.4 %collective-permute-start.3 = (bf16[512,128]{1,0:T(8,128)(2,1)S(1)}, bf16[512,128]{1,0:T(8,128)(2,1)S(1)}, u32[]{:S(2)}, u32[]{:S(2)}) collective-permute-start(bf16[512,128]{1,0:T(8,128)(2,1)S(1)} %bitcast.27), channel_id=1, source_target_pairs={{0,384},{128,0},{256,128},{384,256},{1,385},{129,1},{257,129},{385... | collective-permute-start | bytes 393224 | tf_op jit(solution)/shard_map/ppermute | solution.py:27
  54.2 3.4 %collective-permute-start.4 = (bf16[512,128]{1,0:T(8,128)(2,1)S(1)}, bf16[512,128]{1,0:T(8,128)(2,1)S(1)}, u32[]{:S(2)}, u32[]{:S(2)}) collective-permute-start(bf16[512,128]{1,0:T(8,128)(2,1)S(1)} %bitcast.28), channel_id=1, source_target_pairs={{0,256},{128,384},{256,0},{384,128},{1,257},{129,385},{257,1},{385... | collective-permute-start | bytes 393224 | tf_op jit(solution)/shard_map/ppermute | solution.py:27
  57.6 0.0 collective-permute-done.2
  57.6 0.0 collective-permute-done.3
  57.6 3.8 %collective-permute-done.4 = bf16[512,128]{1,0:T(8,128)(2,1)S(1)} collective-permute-done((bf16[512,128]{1,0:T(8,128)(2,1)S(1)}, bf16[512,128]{1,0:T(8,128)(2,1)S(1)}, u32[]{:S(2)}, u32[]{:S(2)}) %collective-permute-start.4) | collective-permute-done | bytes 131104 | tf_op jit(solution)/shard_map/ppermute | solution.py:27
  61.4 0.1 pad_maximum_fusion.refs_1_
  61.5 4.4 %collective-permute-start.5 = (bf16[512,512]{1,0:T(8,128)(2,1)S(1)}, bf16[512,512]{1,0:T(8,128)(2,1)}, u32[]{:S(2)}, u32[]{:S(2)}) collective-permute-start(bf16[512,512]{1,0:T(8,128)(2,1)S(1)} %pad_maximum_fusion.refs_1_), channel_id=1, source_target_pairs={{0,8},{8,16},{16,24},{24,32},{32,40},{40,48},{48,56},{56,64},{64,7... | collective-permute-start | bytes 1572872 | tf_op jit(solution)/shard_map/ppermute | solution.py:27
  65.9 0.0 all-to-all-done.1
  65.9 1.1 bitcast_bitcast_fusion.refs_0_
  67.0 3.6 %collective-permute-start = (bf16[512,512]{1,0:T(8,128)(2,1)S(1)}, bf16[512,512]{1,0:T(8,128)(2,1)}, u32[]{:S(2)}, u32[]{:S(2)}) collective-permute-start(bf16[512,512]{1,0:T(8,128)(2,1)S(1)} %bitcast_bitcast_fusion.refs_0_), channel_id=1, source_target_pairs={{0,128},{128,256},{256,384},{384,0},{1,129},{129,257},{257,385},{3... | collective-permute-start | bytes 1572872 | tf_op jit(solution)/shard_map/ppermute | solution.py:27
  70.6 2.2 %collective-permute-start.8 = (bf16[512,512]{1,0:T(8,128)(2,1)S(1)}, bf16[512,512]{1,0:T(8,128)(2,1)S(1)}, u32[]{:S(2)}, u32[]{:S(2)}) collective-permute-start(bf16[512,512]{1,0:T(8,128)(2,1)S(1)} %pad_maximum_fusion.refs_1_), channel_id=1, source_target_pairs={{0,120},{8,0},{16,8},{24,16},{32,24},{40,32},{48,40},{56,48},{64,5... | collective-permute-start | bytes 1572872 | tf_op jit(solution)/shard_map/ppermute | solution.py:27
  72.8 3.0 %collective-permute-start.7 = (bf16[512,512]{1,0:T(8,128)(2,1)S(1)}, bf16[512,512]{1,0:T(8,128)(2,1)}, u32[]{:S(2)}, u32[]{:S(2)}) collective-permute-start(bf16[512,512]{1,0:T(8,128)(2,1)S(1)} %bitcast_bitcast_fusion.refs_0_), channel_id=1, source_target_pairs={{0,384},{128,0},{256,128},{384,256},{1,385},{129,1},{257,129},{385... | collective-permute-start | bytes 1572872 | tf_op jit(solution)/shard_map/ppermute | solution.py:27
  75.8 0.0 collective-permute-done.5.refs_4_
  75.8 3.0 %collective-permute-start.6 = (bf16[512,512]{1,0:T(8,128)(2,1)}, bf16[512,512]{1,0:T(8,128)(2,1)}, u32[]{:S(2)}, u32[]{:S(2)}) collective-permute-start(bf16[512,512]{1,0:T(8,128)(2,1)} %collective-permute-done.5.refs_4_), channel_id=1, source_target_pairs={{0,8},{8,16},{16,24},{24,32},{32,40},{40,48},{48,56},{56,64},{64,7... | collective-permute-start | bytes 1572872 | tf_op jit(solution)/shard_map/ppermute | solution.py:27
  78.8 0.7 collective-permute-done.refs_2_
  79.6 4.0 %collective-permute-start.1 = (bf16[512,512]{1,0:T(8,128)(2,1)}, bf16[512,512]{1,0:T(8,128)(2,1)}, u32[]{:S(2)}, u32[]{:S(2)}) collective-permute-start(bf16[512,512]{1,0:T(8,128)(2,1)} %collective-permute-done.refs_2_), channel_id=1, source_target_pairs={{0,128},{128,256},{256,384},{384,0},{1,129},{129,257},{257,385},{3... | collective-permute-start | bytes 1572872 | tf_op jit(solution)/shard_map/ppermute | solution.py:27
  83.5 0.0 collective-permute-done.8.refs_5_
  83.6 0.8 copy-done.6
  84.3 0.7 collective-permute-done.7.refs_3_
  85.0 8.5 %logits_first.1 = (f32[512,1024]{1,0:T(8,128)}, f32[128,64]{1,0:T(8,128)}) custom-call(s32[4]{0:T(128)} %pad_add_fusion.place_ref, bf16[512,512]{1,0:T(8,128)(2,1)} %copy-done.3, bf16[512,512]{1,0:T(8,128)(2,1)} %copy-done.2, bf16[512,512]{1,0:T(8,128)(2,1)} %collective-permute-done.refs_2_, bf16[512,512]{1,0:T(8,128)(2,1)} %collective-permute-done.7.refs_3_, ...), custom_call_target="tpu_custom_call" | custom-call | tf_op jit(solution)/shard_map/logits_first/pallas_call | solution.py:326
  93.5 0.0 collective-permute-done.6.refs_1_
  93.6 7.3 %logits_last.1 = (f32[16,40,128]{2,1,0:T(8,128)}, f32[128,64]{1,0:T(8,128)}) custom-call(s32[4]{0:T(128)} %pad_add_fusion.place_ref, bf16[512,512]{1,0:T(8,128)(2,1)} %collective-permute-done.1.refs_0_, bf16[512,512]{1,0:T(8,128)(2,1)} %collective-permute-done.6.refs_1_, bf16[4,4,4,2,32,1024]{5,4,3,2,1,0:T(8,128)(2,1)} %bitcast.21, ...), custom_call_target="tpu_custom_call" | custom-call | tf_op jit(solution)/shard_map/logits_last/pallas_call | solution.py:334
  100.8 13.4 %all_to_all.25.packed = f32[16,40,128]{2,1,0:T(8,128)} all-to-all(f32[16,40,128]{2,1,0:T(8,128)} %get-tuple-element.25), channel_id=1, replica_groups=mesh['x'=4,'zh'=4,'zl'=4,'y'=4,'c'=2] {'x','zl'}, dimensions={0} | all-to-all | bytes 655360 | tf_op jit(solution)/shard_map/all_to_all | solution.py:36
  114.2 2.3 %merge.1 = f32[16,40,128]{2,1,0:T(8,128)} custom-call(s32[4]{0:T(128)} %pad_add_fusion.place_ref, f32[16,40,128]{2,1,0:T(8,128)} %all_to_all.25.packed), custom_call_target="tpu_custom_call" | custom-call | tf_op jit(solution)/shard_map/merge/pallas_call | solution.py:342
  116.6 18.3 %all_to_all.26.packed = f32[16,40,128]{2,1,0:T(8,128)} all-to-all(f32[16,40,128]{2,1,0:T(8,128)} %merge.1), channel_id=1, replica_groups=mesh['x'=4,'zh'=4,'zl'=4,'y'=4,'c'=2] {'zh','zl'}, dimensions={0} | all-to-all | bytes 655360 | tf_op jit(solution)/shard_map/all_to_all | solution.py:36
  134.8 2.7 %gram.1 = f32[16,72,128]{2,1,0:T(8,128)} custom-call(s32[4]{0:T(128)} %pad_add_fusion.place_ref, s32[32]{0:T(128)} %lengths.3, f32[16,40,128]{2,1,0:T(8,128)} %all_to_all.26.packed, f32[128,64]{1,0:T(8,128)} %get-tuple-element.26.proj), custom_call_target="tpu_custom_call" | custom-call | tf_op jit(solution)/shard_map/gram/pallas_call | solution.py:351
  137.5 13.9 %all_to_all.27.mine = f32[16,72,128]{2,1,0:T(8,128)S(1)} all-to-all(f32[16,72,128]{2,1,0:T(8,128)} %gram.1), channel_id=1, replica_groups=mesh['x'=4,'zh'=4,'zl'=4,'y'=4,'c'=2] {'x','y'}, dimensions={0} | all-to-all | bytes 1179648 | tf_op jit(solution)/shard_map/all_to_all | solution.py:36
  151.4 12.4 %collective-permute-start.9 = (f32[16,72,128]{2,1,0:T(8,128)S(1)}, f32[16,72,128]{2,1,0:T(8,128)S(1)}, u32[]{:S(2)}, u32[]{:S(2)}) collective-permute-start(f32[16,72,128]{2,1,0:T(8,128)S(1)} %all_to_all.27.mine), channel_id=1, source_target_pairs={{0,1},{1,0},{2,3},{3,2},{4,5},{5,4},{6,7},{7,6},{8,9},{9,8},{10,11... | collective-permute-start | bytes 1769480 | tf_op jit(solution)/shard_map/ppermute | solution.py:359
  163.9 1.4 collective-permute-done.9.theirs
  165.3 0.8 copy-done.4
  166.1 7.3 %whiten.1 = bf16[32,64,64]{2,1,0:T(8,128)(2,1)} custom-call(s32[4]{0:T(128)} %pad_add_fusion.place_ref, s32[32]{0:T(128)} %lengths.3, f32[16,72,128]{2,1,0:T(8,128)} %copy-done.1, f32[16,72,128]{2,1,0:T(8,128)} %copy-done.4), custom_call_target="tpu_custom_call" | custom-call | tf_op jit(solution)/shard_map/whiten/pallas_call | solution.py:360
  173.4 1.5 reshape.21
  174.9 1.4 fusion.1
  (19 shorter events, 0.1 us)
Async XLA Ops:
  6.5 168.3 %copy-start = (bf16[256,4096]{1,0:T(8,128)(2,1)S(1)}, bf16[256,4096]{1,0:T(8,128)(2,1)}, u32[]{:S(2)}) copy-start(bf16[256,4096]{1,0:T(8,128)(2,1)} %param.13) | copy-start | bytes 6291460
  6.5 18.0 %copy-start.5 = (bf16[4096,64]{0,1:T(8,128)(2,1)S(1)}, bf16[4096,64]{0,1:T(8,128)(2,1)}, u32[]{:S(2)}) copy-start(bf16[4096,64]{0,1:T(8,128)(2,1)} %param.9) | copy-start | bytes 1572868
  6.5 19.4 %copy-start.7 = (bf16[1024,64]{0,1:T(8,128)(2,1)S(1)}, bf16[1024,64]{0,1:T(8,128)(2,1)}, u32[]{:S(2)}) copy-start(bf16[1024,64]{0,1:T(8,128)(2,1)} %param.10) | copy-start | bytes 393220
  6.5 20.2 %copy-start.8 = (s32[512]{0:T(512)S(1)}, s32[512]{0:T(512)}, u32[]{:S(2)}) copy-start(s32[512]{0:T(512)} %param.11) | copy-start | bytes 6148
  6.5 78.5 %all-gather.2.cloned.1.call-start = ((), (), s32[]{:S(2)}) async-start(), calls=%async_computation.5 | async-start | bytes 9437184 | tf_op jit(solution)/shard_map/all_gather | solution.py:295
  8.9 29.4 %all-to-all-start = ((bf16[4,64,512]{2,1,0:T(8,128)(2,1)}), bf16[4,64,512]{2,1,0:T(8,128)(2,1)S(1)}, u32[]{:S(2)}, u32[]{:S(2)}) async-start(bf16[4,64,512]{2,1,0:T(8,128)(2,1)} %broadcast_in_dim.16), calls=%async_computation | async-start | bytes 524288 | tf_op jit(solution)/shard_map/all_to_all | solution.py:32
  39.3 26.6 %all-to-all-start.1 = ((bf16[4,128,512]{1,2,0:T(8,128)(2,1)}), bf16[4,128,512]{1,2,0:T(8,128)(2,1)}, u32[]{:S(2)}, u32[]{:S(2)}) async-start(bf16[4,128,512]{1,2,0:T(8,128)(2,1)} %broadcast_in_dim.19), calls=%async_computation.1 | async-start | bytes 1048576 | tf_op jit(solution)/shard_map/all_to_all | solution.py:32
  47.6 10.0 %collective-permute-start.2 = (bf16[512,128]{1,0:T(8,128)(2,1)S(1)}, bf16[512,128]{1,0:T(8,128)(2,1)S(1)}, u32[]{:S(2)}, u32[]{:S(2)}) collective-permute-start(bf16[512,128]{1,0:T(8,128)(2,1)S(1)} %bitcast.26), channel_id=1, source_target_pairs={{0,128},{128,256},{256,384},{384,0},{1,129},{129,257},{257,385},{3... | collective-permute-start | bytes 393224 | tf_op jit(solution)/shard_map/ppermute | solution.py:27
  50.8 6.8 %collective-permute-start.3 = (bf16[512,128]{1,0:T(8,128)(2,1)S(1)}, bf16[512,128]{1,0:T(8,128)(2,1)S(1)}, u32[]{:S(2)}, u32[]{:S(2)}) collective-permute-start(bf16[512,128]{1,0:T(8,128)(2,1)S(1)} %bitcast.27), channel_id=1, source_target_pairs={{0,384},{128,0},{256,128},{384,256},{1,385},{129,1},{257,129},{385... | collective-permute-start | bytes 393224 | tf_op jit(solution)/shard_map/ppermute | solution.py:27
  54.2 7.3 %collective-permute-start.4 = (bf16[512,128]{1,0:T(8,128)(2,1)S(1)}, bf16[512,128]{1,0:T(8,128)(2,1)S(1)}, u32[]{:S(2)}, u32[]{:S(2)}) collective-permute-start(bf16[512,128]{1,0:T(8,128)(2,1)S(1)} %bitcast.28), channel_id=1, source_target_pairs={{0,256},{128,384},{256,0},{384,128},{1,257},{129,385},{257,1},{385... | collective-permute-start | bytes 393224 | tf_op jit(solution)/shard_map/ppermute | solution.py:27
  61.5 23.5 %copy-start.2 = (bf16[512,512]{1,0:T(8,128)(2,1)}, bf16[512,512]{1,0:T(8,128)(2,1)S(1)}, u32[]{:S(2)}) copy-start(bf16[512,512]{1,0:T(8,128)(2,1)S(1)} %pad_maximum_fusion.refs_1_) | copy-start | bytes 1572868
  61.5 14.3 %collective-permute-start.5 = (bf16[512,512]{1,0:T(8,128)(2,1)S(1)}, bf16[512,512]{1,0:T(8,128)(2,1)}, u32[]{:S(2)}, u32[]{:S(2)}) collective-permute-start(bf16[512,512]{1,0:T(8,128)(2,1)S(1)} %pad_maximum_fusion.refs_1_), channel_id=1, source_target_pairs={{0,8},{8,16},{16,24},{24,32},{32,40},{40,48},{48,56},{56,64},{64,7... | collective-permute-start | bytes 1572872 | tf_op jit(solution)/shard_map/ppermute | solution.py:27
  67.0 18.0 %copy-start.3 = (bf16[512,512]{1,0:T(8,128)(2,1)}, bf16[512,512]{1,0:T(8,128)(2,1)S(1)}, u32[]{:S(2)}) copy-start(bf16[512,512]{1,0:T(8,128)(2,1)S(1)} %bitcast_bitcast_fusion.refs_0_) | copy-start | bytes 1572868
  67.0 12.5 %collective-permute-start = (bf16[512,512]{1,0:T(8,128)(2,1)S(1)}, bf16[512,512]{1,0:T(8,128)(2,1)}, u32[]{:S(2)}, u32[]{:S(2)}) collective-permute-start(bf16[512,512]{1,0:T(8,128)(2,1)S(1)} %bitcast_bitcast_fusion.refs_0_), channel_id=1, source_target_pairs={{0,128},{128,256},{256,384},{384,0},{1,129},{129,257},{257,385},{3... | collective-permute-start | bytes 1572872 | tf_op jit(solution)/shard_map/ppermute | solution.py:27
  70.6 12.9 %collective-permute-start.8 = (bf16[512,512]{1,0:T(8,128)(2,1)S(1)}, bf16[512,512]{1,0:T(8,128)(2,1)S(1)}, u32[]{:S(2)}, u32[]{:S(2)}) collective-permute-start(bf16[512,512]{1,0:T(8,128)(2,1)S(1)} %pad_maximum_fusion.refs_1_), channel_id=1, source_target_pairs={{0,120},{8,0},{16,8},{24,16},{32,24},{40,32},{48,40},{56,48},{64,5... | collective-permute-start | bytes 1572872 | tf_op jit(solution)/shard_map/ppermute | solution.py:27
  72.8 12.2 %collective-permute-start.7 = (bf16[512,512]{1,0:T(8,128)(2,1)S(1)}, bf16[512,512]{1,0:T(8,128)(2,1)}, u32[]{:S(2)}, u32[]{:S(2)}) collective-permute-start(bf16[512,512]{1,0:T(8,128)(2,1)S(1)} %bitcast_bitcast_fusion.refs_0_), channel_id=1, source_target_pairs={{0,384},{128,0},{256,128},{384,256},{1,385},{129,1},{257,129},{385... | collective-permute-start | bytes 1572872 | tf_op jit(solution)/shard_map/ppermute | solution.py:27
  75.8 17.7 %collective-permute-start.6 = (bf16[512,512]{1,0:T(8,128)(2,1)}, bf16[512,512]{1,0:T(8,128)(2,1)}, u32[]{:S(2)}, u32[]{:S(2)}) collective-permute-start(bf16[512,512]{1,0:T(8,128)(2,1)} %collective-permute-done.5.refs_4_), channel_id=1, source_target_pairs={{0,8},{8,16},{16,24},{24,32},{32,40},{40,48},{48,56},{56,64},{64,7... | collective-permute-start | bytes 1572872 | tf_op jit(solution)/shard_map/ppermute | solution.py:27
  79.6 14.0 %collective-permute-start.1 = (bf16[512,512]{1,0:T(8,128)(2,1)}, bf16[512,512]{1,0:T(8,128)(2,1)}, u32[]{:S(2)}, u32[]{:S(2)}) collective-permute-start(bf16[512,512]{1,0:T(8,128)(2,1)} %collective-permute-done.refs_2_), channel_id=1, source_target_pairs={{0,128},{128,256},{256,384},{384,0},{1,129},{129,257},{257,385},{3... | collective-permute-start | bytes 1572872 | tf_op jit(solution)/shard_map/ppermute | solution.py:27
  83.5 0.8 copy-start.6
  151.4 13.9 %copy-start.1 = (f32[16,72,128]{2,1,0:T(8,128)}, f32[16,72,128]{2,1,0:T(8,128)S(1)}, u32[]{:S(2)}) copy-start(f32[16,72,128]{2,1,0:T(8,128)S(1)} %all_to_all.27.mine) | copy-start | bytes 1769476
  151.4 13.9 %collective-permute-start.9 = (f32[16,72,128]{2,1,0:T(8,128)S(1)}, f32[16,72,128]{2,1,0:T(8,128)S(1)}, u32[]{:S(2)}, u32[]{:S(2)}) collective-permute-start(f32[16,72,128]{2,1,0:T(8,128)S(1)} %all_to_all.27.mine), channel_id=1, source_target_pairs={{0,1},{1,0},{2,3},{3,2},{4,5},{5,4},{6,7},{7,6},{8,9},{9,8},{10,11... | collective-permute-start | bytes 1769480 | tf_op jit(solution)/shard_map/ppermute | solution.py:359
  165.3 0.8 copy-start.4
Sparse Core Ops, SparseCore 0:
  9.5 63.0 all-gather.1

commit v6 on v5

--- a/solution.py
+++ b/solution.py
@@ -146,9 +146,8 @@
         rest = weight - part1.astype(F32)
         part2 = rest.astype(BF16)
         part3 = (rest - part2.astype(F32)).astype(BF16)
-        mixed = jnp.dot(part1, table, preferred_element_type=F32)
-        mixed += jnp.dot(part2, table, preferred_element_type=F32)
-        mixed += jnp.dot(part3, table, preferred_element_type=F32)
+        parts = jnp.dot(jnp.concatenate([part1, part2, part3], axis=0), table, preferred_element_type=F32)
+        mixed = parts[0:TILE] + parts[TILE : 2 * TILE] + parts[2 * TILE :]
         data = jnp.concatenate([mixed, picked[rows, :]], axis=1)
         stat = stat_tile(peak, total, TILE)
         for b in range(ZL):
@@ -238,6 +237,7 @@
     trace_in = jnp.sum(jnp.where(left, 0.0, diag))
     damp = jnp.where(left, damping_ratio * trace_out / 64 + tiny_value, damping_ratio * trace_in / 64 + tiny_value)
     work = work + jnp.where(on_diag, damp, 0.0)
+
     def column(work, k):
         return jnp.where(left, work[:, k : k + 1], work[:, 64 + k : 65 + k])
 
@@ -285,7 +285,7 @@
 
 
 def per_device(hidden, head_weight, in_proj, out_proj, targets, lengths, grad_store):
-    token_count, width = hidden.shape
+    token_count, _ = hidden.shape
     x = lax.axis_index("x")
     z = lax.axis_index("zh") * ZL + lax.axis_index("zl")
     core = lax.axis_index("c")
@@ -306,7 +306,8 @@
     a_own = spread(strided[:, :HALF, :].reshape(ZH * HALF, token_count), "zl", ZL)
     a_own = a_own.reshape(size, token_count).T
     b_part = strided[:, HALF:, :].reshape(ZH * HALF, token_count).T
-    b_own = jnp.concatenate([b_part] + [shift(b_part, "x", -s, NX) for s in STEPS[1:]], axis=1)
+    b_parts = [b_part] + [shift(b_part, "x", -s, NX) for s in STEPS[1:]]
+    b_own = jnp.concatenate(b_parts, axis=1)
     b_back, b_next = shift(b_own, ZAXIS, 1, NZ), shift(b_own, ZAXIS, -1, NZ)
     a_back, a_next = shift(a_own, "x", 1, NX), shift(a_own, "x", -1, NX)
     b_far, a_far = shift(b_back, ZAXIS, 1, NZ), shift(a_back, "x", 1, NX)

time: 185 us -> 185 us (level)
  no operation moved by 1% of the time
where the time goes in v6:
time: 185 us; the launch traced here: 183 us
  starting transfers between devices  66.3 us (36%)
  blocking collectives  45.5 us (25%)
  Pallas kernels  31.1 us (17%)
  waiting for transfers between devices  14.3 us (8%)
  between operations  13.6 us (7%)
  local copies, waits for them, and re-layouts  10.1 us (5%)
    all_to_all x3, blocking collectives, exchange(): return lax.all_to_all(value, axis, 0, 0, tiled=True)  45.5 us
    ppermute x9, starting transfers between devices, shift(): lax.ppermute(value, axis, [(i, (i + step) % size) for i in range(size)])  30.1 us
    all_to_all x2, starting transfers between devices, spread(): return lax.all_to_all(copies, axis, 0, 0, tiled=True)  23.8 us
    ppermute x1, starting transfers between devices, per_device(): theirs = lax.ppermute(mine, 'c', [(0, 1), (1, 0)])  12.4 us
    pallas_call x1, Pallas kernels, per_device(): pl.pallas_call(first_kernel, out_shape=(full((token_count, cols)), full((...  8.51 us
    pallas_call x1, Pallas kernels, per_device(): pl.pallas_call(whiten_kernel, out_shape=full((seqs, 64, 64), BF16), in_sp...  7.25 us
    pallas_call x1, Pallas kernels, per_device(): pl.pallas_call(logits_kernel, out_shape=(full((NX * ZL, ROWS + 8, TILE)),...  7.18 us
    all_to_all x2, waiting for transfers between devices, spread(): return lax.all_to_all(copies, axis, 0, 0, tiled=True)  6.93 us
  transfers between devices with their start and end apart: 13, of which 5 were waited for; matrix products, arithmetic and copies ran while one was open for 4% of the time, Pallas kernels for 6%

profile of v6, /device:TPU:1, one launch (start us, length us, event | category | flops | bytes accessed | tf_op | source)
XLA Modules:
  0.0 183.0 jit_solution(16889602785427454582)
XLA Ops:
  6.5 0.0 all-gather.2.cloned.1.call-start
  6.6 0.7 all-gather.2.cloned.1.call-update
  7.3 1.6 broadcast_in_dim.16
  8.9 15.6 %all-to-all-start = ((bf16[4,64,512]{2,1,0:T(8,128)(2,1)}), bf16[4,64,512]{2,1,0:T(8,128)(2,1)S(1)}, u32[]{:S(2)}, u32[]{:S(2)}) async-start(bf16[4,64,512]{2,1,0:T(8,128)(2,1)} %broadcast_in_dim.16), calls=%async_computation | async-start | bytes 524288 | tf_op jit(solution)/shard_map/all_to_all | solution.py:32
  24.5 1.4 copy.16.in_proj
  25.9 0.8 copy.17.out_proj
  26.7 0.9 copy.18.targets
  27.6 0.6 pad_add_fusion.place_ref
  28.2 3.1 %prepare.1 = (f32[512,64]{1,0:T(8,128)}, bf16[4096,64]{1,0:T(8,128)(2,1)}, bf16[1024,64]{1,0:T(8,128)(2,1)}) custom-call(s32[4]{0:T(128)} %pad_add_fusion.place_ref, bf16[4096,64]{1,0:T(8,128)(2,1)} %copy.16.in_proj, bf16[1024,64]{1,0:T(8,128)(2,1)} %copy.17.out_proj, s32[512,1]{1,0:T(8,128)} %copy.18.targets), custom_call_target="tpu_custom_call" | custom-call | tf_op jit(solution)/shard_map/prepare/pallas_call | solution.py:296
  31.4 6.9 %all-to-all-done = bf16[4,64,512]{2,1,0:T(8,128)(2,1)S(1)} async-done(((bf16[4,64,512]{2,1,0:T(8,128)(2,1)}), bf16[4,64,512]{2,1,0:T(8,128)(2,1)S(1)}, u32[]{:S(2)}, u32[]{:S(2)}) %all-to-all-start) | async-done | bytes 262176 | tf_op jit(solution)/shard_map/all_to_all | solution.py:32
  38.3 0.1 copy.19
  38.4 0.9 broadcast_in_dim.19
  39.3 8.2 %all-to-all-start.1 = ((bf16[4,128,512]{1,2,0:T(8,128)(2,1)}), bf16[4,128,512]{1,2,0:T(8,128)(2,1)}, u32[]{:S(2)}, u32[]{:S(2)}) async-start(bf16[4,128,512]{1,2,0:T(8,128)(2,1)} %broadcast_in_dim.19), calls=%async_computation.1 | async-start | bytes 1048576 | tf_op jit(solution)/shard_map/all_to_all | solution.py:32
  47.5 0.1 copy.21
  47.6 3.1 %collective-permute-start.2 = (bf16[512,128]{1,0:T(8,128)(2,1)S(1)}, bf16[512,128]{1,0:T(8,128)(2,1)S(1)}, u32[]{:S(2)}, u32[]{:S(2)}) collective-permute-start(bf16[512,128]{1,0:T(8,128)(2,1)S(1)} %bitcast.26), channel_id=1, source_target_pairs={{0,128},{128,256},{256,384},{384,0},{1,129},{129,257},{257,385},{3... | collective-permute-start | bytes 393224 | tf_op jit(solution)/shard_map/ppermute | solution.py:27
  50.8 3.4 %collective-permute-start.3 = (bf16[512,128]{1,0:T(8,128)(2,1)S(1)}, bf16[512,128]{1,0:T(8,128)(2,1)S(1)}, u32[]{:S(2)}, u32[]{:S(2)}) collective-permute-start(bf16[512,128]{1,0:T(8,128)(2,1)S(1)} %bitcast.27), channel_id=1, source_target_pairs={{0,384},{128,0},{256,128},{384,256},{1,385},{129,1},{257,129},{385... | collective-permute-start | bytes 393224 | tf_op jit(solution)/shard_map/ppermute | solution.py:27
  54.2 3.4 %collective-permute-start.4 = (bf16[512,128]{1,0:T(8,128)(2,1)S(1)}, bf16[512,128]{1,0:T(8,128)(2,1)S(1)}, u32[]{:S(2)}, u32[]{:S(2)}) collective-permute-start(bf16[512,128]{1,0:T(8,128)(2,1)S(1)} %bitcast.28), channel_id=1, source_target_pairs={{0,256},{128,384},{256,0},{384,128},{1,257},{129,385},{257,1},{385... | collective-permute-start | bytes 393224 | tf_op jit(solution)/shard_map/ppermute | solution.py:27
  57.6 0.0 collective-permute-done.2
  57.6 0.0 collective-permute-done.3
  57.6 3.8 %collective-permute-done.4 = bf16[512,128]{1,0:T(8,128)(2,1)S(1)} collective-permute-done((bf16[512,128]{1,0:T(8,128)(2,1)S(1)}, bf16[512,128]{1,0:T(8,128)(2,1)S(1)}, u32[]{:S(2)}, u32[]{:S(2)}) %collective-permute-start.4) | collective-permute-done | bytes 131104 | tf_op jit(solution)/shard_map/ppermute | solution.py:27
  61.4 0.1 pad_maximum_fusion.refs_1_
  61.5 4.4 %collective-permute-start.5 = (bf16[512,512]{1,0:T(8,128)(2,1)S(1)}, bf16[512,512]{1,0:T(8,128)(2,1)}, u32[]{:S(2)}, u32[]{:S(2)}) collective-permute-start(bf16[512,512]{1,0:T(8,128)(2,1)S(1)} %pad_maximum_fusion.refs_1_), channel_id=1, source_target_pairs={{0,8},{8,16},{16,24},{24,32},{32,40},{40,48},{48,56},{56,64},{64,7... | collective-permute-start | bytes 1572872 | tf_op jit(solution)/shard_map/ppermute | solution.py:27
  65.9 0.0 all-to-all-done.1
  65.9 1.1 bitcast_bitcast_fusion.refs_0_
  67.0 3.6 %collective-permute-start = (bf16[512,512]{1,0:T(8,128)(2,1)S(1)}, bf16[512,512]{1,0:T(8,128)(2,1)}, u32[]{:S(2)}, u32[]{:S(2)}) collective-permute-start(bf16[512,512]{1,0:T(8,128)(2,1)S(1)} %bitcast_bitcast_fusion.refs_0_), channel_id=1, source_target_pairs={{0,128},{128,256},{256,384},{384,0},{1,129},{129,257},{257,385},{3... | collective-permute-start | bytes 1572872 | tf_op jit(solution)/shard_map/ppermute | solution.py:27
  70.6 2.2 %collective-permute-start.8 = (bf16[512,512]{1,0:T(8,128)(2,1)S(1)}, bf16[512,512]{1,0:T(8,128)(2,1)S(1)}, u32[]{:S(2)}, u32[]{:S(2)}) collective-permute-start(bf16[512,512]{1,0:T(8,128)(2,1)S(1)} %pad_maximum_fusion.refs_1_), channel_id=1, source_target_pairs={{0,120},{8,0},{16,8},{24,16},{32,24},{40,32},{48,40},{56,48},{64,5... | collective-permute-start | bytes 1572872 | tf_op jit(solution)/shard_map/ppermute | solution.py:27
  72.8 3.0 %collective-permute-start.7 = (bf16[512,512]{1,0:T(8,128)(2,1)S(1)}, bf16[512,512]{1,0:T(8,128)(2,1)}, u32[]{:S(2)}, u32[]{:S(2)}) collective-permute-start(bf16[512,512]{1,0:T(8,128)(2,1)S(1)} %bitcast_bitcast_fusion.refs_0_), channel_id=1, source_target_pairs={{0,384},{128,0},{256,128},{384,256},{1,385},{129,1},{257,129},{385... | collective-permute-start | bytes 1572872 | tf_op jit(solution)/shard_map/ppermute | solution.py:27
  75.8 0.0 collective-permute-done.5.refs_4_
  75.8 3.0 %collective-permute-start.6 = (bf16[512,512]{1,0:T(8,128)(2,1)}, bf16[512,512]{1,0:T(8,128)(2,1)}, u32[]{:S(2)}, u32[]{:S(2)}) collective-permute-start(bf16[512,512]{1,0:T(8,128)(2,1)} %collective-permute-done.5.refs_4_), channel_id=1, source_target_pairs={{0,8},{8,16},{16,24},{24,32},{32,40},{40,48},{48,56},{56,64},{64,7... | collective-permute-start | bytes 1572872 | tf_op jit(solution)/shard_map/ppermute | solution.py:27
  78.8 0.7 collective-permute-done.refs_2_
  79.6 4.0 %collective-permute-start.1 = (bf16[512,512]{1,0:T(8,128)(2,1)}, bf16[512,512]{1,0:T(8,128)(2,1)}, u32[]{:S(2)}, u32[]{:S(2)}) collective-permute-start(bf16[512,512]{1,0:T(8,128)(2,1)} %collective-permute-done.refs_2_), channel_id=1, source_target_pairs={{0,128},{128,256},{256,384},{384,0},{1,129},{129,257},{257,385},{3... | collective-permute-start | bytes 1572872 | tf_op jit(solution)/shard_map/ppermute | solution.py:27
  83.5 0.0 collective-permute-done.8.refs_5_
  83.6 0.8 copy-done.6
  84.3 0.7 collective-permute-done.7.refs_3_
  85.0 8.5 %logits_first.1 = (f32[512,1024]{1,0:T(8,128)}, f32[128,64]{1,0:T(8,128)}) custom-call(s32[4]{0:T(128)} %pad_add_fusion.place_ref, bf16[512,512]{1,0:T(8,128)(2,1)} %copy-done.3, bf16[512,512]{1,0:T(8,128)(2,1)} %copy-done.2, bf16[512,512]{1,0:T(8,128)(2,1)} %collective-permute-done.refs_2_, bf16[512,512]{1,0:T(8,128)(2,1)} %collective-permute-done.7.refs_3_, ...), custom_call_target="tpu_custom_call" | custom-call | tf_op jit(solution)/shard_map/logits_first/pallas_call | solution.py:327
  93.5 0.0 collective-permute-done.6.refs_1_
  93.6 7.2 %logits_last.1 = (f32[16,40,128]{2,1,0:T(8,128)}, f32[128,64]{1,0:T(8,128)}) custom-call(s32[4]{0:T(128)} %pad_add_fusion.place_ref, bf16[512,512]{1,0:T(8,128)(2,1)} %collective-permute-done.1.refs_0_, bf16[512,512]{1,0:T(8,128)(2,1)} %collective-permute-done.6.refs_1_, bf16[4,4,4,2,32,1024]{5,4,3,2,1,0:T(8,128)(2,1)} %bitcast.21, ...), custom_call_target="tpu_custom_call" | custom-call | tf_op jit(solution)/shard_map/logits_last/pallas_call | solution.py:335
  100.7 13.4 %all_to_all.25.packed = f32[16,40,128]{2,1,0:T(8,128)} all-to-all(f32[16,40,128]{2,1,0:T(8,128)} %get-tuple-element.25), channel_id=1, replica_groups=mesh['x'=4,'zh'=4,'zl'=4,'y'=4,'c'=2] {'x','zl'}, dimensions={0} | all-to-all | bytes 655360 | tf_op jit(solution)/shard_map/all_to_all | solution.py:36
  114.1 2.3 %merge.1 = f32[16,40,128]{2,1,0:T(8,128)} custom-call(s32[4]{0:T(128)} %pad_add_fusion.place_ref, f32[16,40,128]{2,1,0:T(8,128)} %all_to_all.25.packed), custom_call_target="tpu_custom_call" | custom-call | tf_op jit(solution)/shard_map/merge/pallas_call | solution.py:343
  116.5 18.3 %all_to_all.26.packed = f32[16,40,128]{2,1,0:T(8,128)} all-to-all(f32[16,40,128]{2,1,0:T(8,128)} %merge.1), channel_id=1, replica_groups=mesh['x'=4,'zh'=4,'zl'=4,'y'=4,'c'=2] {'zh','zl'}, dimensions={0} | all-to-all | bytes 655360 | tf_op jit(solution)/shard_map/all_to_all | solution.py:36
  134.7 2.7 %gram.1 = f32[16,72,128]{2,1,0:T(8,128)} custom-call(s32[4]{0:T(128)} %pad_add_fusion.place_ref, s32[32]{0:T(128)} %lengths.3, f32[16,40,128]{2,1,0:T(8,128)} %all_to_all.26.packed, f32[128,64]{1,0:T(8,128)} %get-tuple-element.26.proj), custom_call_target="tpu_custom_call" | custom-call | tf_op jit(solution)/shard_map/gram/pallas_call | solution.py:352
  137.4 13.9 %all_to_all.27.mine = f32[16,72,128]{2,1,0:T(8,128)S(1)} all-to-all(f32[16,72,128]{2,1,0:T(8,128)} %gram.1), channel_id=1, replica_groups=mesh['x'=4,'zh'=4,'zl'=4,'y'=4,'c'=2] {'x','y'}, dimensions={0} | all-to-all | bytes 1179648 | tf_op jit(solution)/shard_map/all_to_all | solution.py:36
  151.3 12.4 %collective-permute-start.9 = (f32[16,72,128]{2,1,0:T(8,128)S(1)}, f32[16,72,128]{2,1,0:T(8,128)S(1)}, u32[]{:S(2)}, u32[]{:S(2)}) collective-permute-start(f32[16,72,128]{2,1,0:T(8,128)S(1)} %all_to_all.27.mine), channel_id=1, source_target_pairs={{0,1},{1,0},{2,3},{3,2},{4,5},{5,4},{6,7},{7,6},{8,9},{9,8},{10,11... | collective-permute-start | bytes 1769480 | tf_op jit(solution)/shard_map/ppermute | solution.py:360
  163.8 1.4 collective-permute-done.9.theirs
  165.2 0.8 copy-done.4
  166.0 7.3 %whiten.1 = bf16[32,64,64]{2,1,0:T(8,128)(2,1)} custom-call(s32[4]{0:T(128)} %pad_add_fusion.place_ref, s32[32]{0:T(128)} %lengths.3, f32[16,72,128]{2,1,0:T(8,128)} %copy-done.1, f32[16,72,128]{2,1,0:T(8,128)} %copy-done.4), custom_call_target="tpu_custom_call" | custom-call | tf_op jit(solution)/shard_map/whiten/pallas_call | solution.py:361
  173.3 1.5 reshape.21
  174.8 1.4 fusion.1
  (19 shorter events, 0.1 us)
Async XLA Ops:
  6.5 168.2 %copy-start = (bf16[256,4096]{1,0:T(8,128)(2,1)S(1)}, bf16[256,4096]{1,0:T(8,128)(2,1)}, u32[]{:S(2)}) copy-start(bf16[256,4096]{1,0:T(8,128)(2,1)} %param.13) | copy-start | bytes 6291460
  6.5 18.0 %copy-start.5 = (bf16[4096,64]{0,1:T(8,128)(2,1)S(1)}, bf16[4096,64]{0,1:T(8,128)(2,1)}, u32[]{:S(2)}) copy-start(bf16[4096,64]{0,1:T(8,128)(2,1)} %param.9) | copy-start | bytes 1572868
  6.5 19.4 %copy-start.7 = (bf16[1024,64]{0,1:T(8,128)(2,1)S(1)}, bf16[1024,64]{0,1:T(8,128)(2,1)}, u32[]{:S(2)}) copy-start(bf16[1024,64]{0,1:T(8,128)(2,1)} %param.10) | copy-start | bytes 393220
  6.5 20.2 %copy-start.8 = (s32[512]{0:T(512)S(1)}, s32[512]{0:T(512)}, u32[]{:S(2)}) copy-start(s32[512]{0:T(512)} %param.11) | copy-start | bytes 6148
  6.5 78.5 %all-gather.2.cloned.1.call-start = ((), (), s32[]{:S(2)}) async-start(), calls=%async_computation.5 | async-start | bytes 9437184 | tf_op jit(solution)/shard_map/all_gather | solution.py:295
  8.9 29.4 %all-to-all-start = ((bf16[4,64,512]{2,1,0:T(8,128)(2,1)}), bf16[4,64,512]{2,1,0:T(8,128)(2,1)S(1)}, u32[]{:S(2)}, u32[]{:S(2)}) async-start(bf16[4,64,512]{2,1,0:T(8,128)(2,1)} %broadcast_in_dim.16), calls=%async_computation | async-start | bytes 524288 | tf_op jit(solution)/shard_map/all_to_all | solution.py:32
  39.3 26.6 %all-to-all-start.1 = ((bf16[4,128,512]{1,2,0:T(8,128)(2,1)}), bf16[4,128,512]{1,2,0:T(8,128)(2,1)}, u32[]{:S(2)}, u32[]{:S(2)}) async-start(bf16[4,128,512]{1,2,0:T(8,128)(2,1)} %broadcast_in_dim.19), calls=%async_computation.1 | async-start | bytes 1048576 | tf_op jit(solution)/shard_map/all_to_all | solution.py:32
  47.6 10.0 %collective-permute-start.2 = (bf16[512,128]{1,0:T(8,128)(2,1)S(1)}, bf16[512,128]{1,0:T(8,128)(2,1)S(1)}, u32[]{:S(2)}, u32[]{:S(2)}) collective-permute-start(bf16[512,128]{1,0:T(8,128)(2,1)S(1)} %bitcast.26), channel_id=1, source_target_pairs={{0,128},{128,256},{256,384},{384,0},{1,129},{129,257},{257,385},{3... | collective-permute-start | bytes 393224 | tf_op jit(solution)/shard_map/ppermute | solution.py:27
  50.8 6.8 %collective-permute-start.3 = (bf16[512,128]{1,0:T(8,128)(2,1)S(1)}, bf16[512,128]{1,0:T(8,128)(2,1)S(1)}, u32[]{:S(2)}, u32[]{:S(2)}) collective-permute-start(bf16[512,128]{1,0:T(8,128)(2,1)S(1)} %bitcast.27), channel_id=1, source_target_pairs={{0,384},{128,0},{256,128},{384,256},{1,385},{129,1},{257,129},{385... | collective-permute-start | bytes 393224 | tf_op jit(solution)/shard_map/ppermute | solution.py:27
  54.2 7.3 %collective-permute-start.4 = (bf16[512,128]{1,0:T(8,128)(2,1)S(1)}, bf16[512,128]{1,0:T(8,128)(2,1)S(1)}, u32[]{:S(2)}, u32[]{:S(2)}) collective-permute-start(bf16[512,128]{1,0:T(8,128)(2,1)S(1)} %bitcast.28), channel_id=1, source_target_pairs={{0,256},{128,384},{256,0},{384,128},{1,257},{129,385},{257,1},{385... | collective-permute-start | bytes 393224 | tf_op jit(solution)/shard_map/ppermute | solution.py:27
  61.5 23.5 %copy-start.2 = (bf16[512,512]{1,0:T(8,128)(2,1)}, bf16[512,512]{1,0:T(8,128)(2,1)S(1)}, u32[]{:S(2)}) copy-start(bf16[512,512]{1,0:T(8,128)(2,1)S(1)} %pad_maximum_fusion.refs_1_) | copy-start | bytes 1572868
  61.5 14.3 %collective-permute-start.5 = (bf16[512,512]{1,0:T(8,128)(2,1)S(1)}, bf16[512,512]{1,0:T(8,128)(2,1)}, u32[]{:S(2)}, u32[]{:S(2)}) collective-permute-start(bf16[512,512]{1,0:T(8,128)(2,1)S(1)} %pad_maximum_fusion.refs_1_), channel_id=1, source_target_pairs={{0,8},{8,16},{16,24},{24,32},{32,40},{40,48},{48,56},{56,64},{64,7... | collective-permute-start | bytes 1572872 | tf_op jit(solution)/shard_map/ppermute | solution.py:27
  67.0 18.0 %copy-start.3 = (bf16[512,512]{1,0:T(8,128)(2,1)}, bf16[512,512]{1,0:T(8,128)(2,1)S(1)}, u32[]{:S(2)}) copy-start(bf16[512,512]{1,0:T(8,128)(2,1)S(1)} %bitcast_bitcast_fusion.refs_0_) | copy-start | bytes 1572868
  67.0 12.5 %collective-permute-start = (bf16[512,512]{1,0:T(8,128)(2,1)S(1)}, bf16[512,512]{1,0:T(8,128)(2,1)}, u32[]{:S(2)}, u32[]{:S(2)}) collective-permute-start(bf16[512,512]{1,0:T(8,128)(2,1)S(1)} %bitcast_bitcast_fusion.refs_0_), channel_id=1, source_target_pairs={{0,128},{128,256},{256,384},{384,0},{1,129},{129,257},{257,385},{3... | collective-permute-start | bytes 1572872 | tf_op jit(solution)/shard_map/ppermute | solution.py:27
  70.6 12.9 %collective-permute-start.8 = (bf16[512,512]{1,0:T(8,128)(2,1)S(1)}, bf16[512,512]{1,0:T(8,128)(2,1)S(1)}, u32[]{:S(2)}, u32[]{:S(2)}) collective-permute-start(bf16[512,512]{1,0:T(8,128)(2,1)S(1)} %pad_maximum_fusion.refs_1_), channel_id=1, source_target_pairs={{0,120},{8,0},{16,8},{24,16},{32,24},{40,32},{48,40},{56,48},{64,5... | collective-permute-start | bytes 1572872 | tf_op jit(solution)/shard_map/ppermute | solution.py:27
  72.8 12.2 %collective-permute-start.7 = (bf16[512,512]{1,0:T(8,128)(2,1)S(1)}, bf16[512,512]{1,0:T(8,128)(2,1)}, u32[]{:S(2)}, u32[]{:S(2)}) collective-permute-start(bf16[512,512]{1,0:T(8,128)(2,1)S(1)} %bitcast_bitcast_fusion.refs_0_), channel_id=1, source_target_pairs={{0,384},{128,0},{256,128},{384,256},{1,385},{129,1},{257,129},{385... | collective-permute-start | bytes 1572872 | tf_op jit(solution)/shard_map/ppermute | solution.py:27
  75.8 17.7 %collective-permute-start.6 = (bf16[512,512]{1,0:T(8,128)(2,1)}, bf16[512,512]{1,0:T(8,128)(2,1)}, u32[]{:S(2)}, u32[]{:S(2)}) collective-permute-start(bf16[512,512]{1,0:T(8,128)(2,1)} %collective-permute-done.5.refs_4_), channel_id=1, source_target_pairs={{0,8},{8,16},{16,24},{24,32},{32,40},{40,48},{48,56},{56,64},{64,7... | collective-permute-start | bytes 1572872 | tf_op jit(solution)/shard_map/ppermute | solution.py:27
  79.6 14.0 %collective-permute-start.1 = (bf16[512,512]{1,0:T(8,128)(2,1)}, bf16[512,512]{1,0:T(8,128)(2,1)}, u32[]{:S(2)}, u32[]{:S(2)}) collective-permute-start(bf16[512,512]{1,0:T(8,128)(2,1)} %collective-permute-done.refs_2_), channel_id=1, source_target_pairs={{0,128},{128,256},{256,384},{384,0},{1,129},{129,257},{257,385},{3... | collective-permute-start | bytes 1572872 | tf_op jit(solution)/shard_map/ppermute | solution.py:27
  83.5 0.8 copy-start.6
  151.3 13.9 %copy-start.1 = (f32[16,72,128]{2,1,0:T(8,128)}, f32[16,72,128]{2,1,0:T(8,128)S(1)}, u32[]{:S(2)}) copy-start(f32[16,72,128]{2,1,0:T(8,128)S(1)} %all_to_all.27.mine) | copy-start | bytes 1769476
  151.3 13.9 %collective-permute-start.9 = (f32[16,72,128]{2,1,0:T(8,128)S(1)}, f32[16,72,128]{2,1,0:T(8,128)S(1)}, u32[]{:S(2)}, u32[]{:S(2)}) collective-permute-start(f32[16,72,128]{2,1,0:T(8,128)S(1)} %all_to_all.27.mine), channel_id=1, source_target_pairs={{0,1},{1,0},{2,3},{3,2},{4,5},{5,4},{6,7},{7,6},{8,9},{9,8},{10,11... | collective-permute-start | bytes 1769480 | tf_op jit(solution)/shard_map/ppermute | solution.py:360
  165.2 0.8 copy-start.4
Sparse Core Ops, SparseCore 0:
  9.5 63.0 all-gather.1
